TPU v7x, 32 devices: a whole 2x2x4 slice. The times are simulated.
32 devices in a mesh: grp: 2 (over x), xy: 4 (over y, core), gz: 4 (over z).
Axes of the slice: x: 2, y: 2, z: 4, core: 2. Of those that a mesh axis runs over, the one named last changes fastest.
Arguments:
- fields: float32 [12, 16, 64, 512], P('grp', 'xy', 'gz'), parts along dimension 0, may hold values from -6 to 6
- adjoint_fields: float32 [12, 16, 64, 512], P('grp', 'xy', 'gz'), parts along dimension 0, may hold values from -6 to 6
- material_ids: int32 [16, 64, 1024], P('xy', 'gz', 'grp'), parts along dimension 2, may hold values from 0 to 3
- material_eps: float32 [4], replicated, may hold values from 1 to 12
- monitor_cells: int32 [4, 4, 2048], P('xy', 'gz', 'grp'), parts along dimension 2, may hold values from 0 to 32767
- monitor_bins: int32 [4, 4, 2048], P('xy', 'gz', 'grp'), parts along dimension 2, may hold values from 0 to 127
- source_cells: int32 [4, 4, 2048], P('xy', 'gz', 'grp'), parts along dimension 2, may hold values from 0 to 32767
- source_bins: int32 [4, 4, 2048], P('xy', 'gz', 'grp'), parts along dimension 2, may hold values from 0 to 127
- bin_weight: float32 [256], P('grp'), parts along dimension 0, may hold values from 0.5 to 2
Outputs:
- forward_out: float32 [12, 16, 64, 512], P('grp', 'xy', 'gz'), parts along dimension 0
- adjoint_out: float32 [12, 16, 64, 512], P('grp', 'xy', 'gz'), parts along dimension 0
- monitor_dft: float32 [16, 128], P('grp', ('xy', 'gz')), parts along dimension 0
There are 2 independent parts, one for each index of `grp`. A program takes and returns all parts, laid end to end along the dimension named above; an argument that names none is the same for every part. Nothing has to cross between parts.
All inputs are finite; a program needn't handle non-finite values.
Results may differ from a plain program's by a relative error of at most 0.00011.
Values sent between devices are 32-bit elements; how exact they have to be, the bound alone decides.
No kernel may reach another device: no remote copies, remote signals or barrier semaphores. Data moves between devices by JAX's collectives and lax.ppermute only.
A program may use at most 64 MiB of HBM per device.

v0:
```python
import jax
import jax.numpy as jnp
from jax import lax
from jax.sharding import PartitionSpec as P

STEPS = 8
NFREQ = 4


STEP_RATIO = 0.5


def from_behind(value, axis, steps):
    count = lax.axis_size(axis)
    first, last = (max(0, -steps), min(count, count - steps))
    return lax.ppermute(value, axis, [(source, source + steps) for source in range(first, last)])


def forward_diff(values, after, along):
    upper = jnp.concatenate(
        [
            lax.slice_in_dim(values, 1, values.shape[along], axis=along),
            jnp.expand_dims(after, along),
        ],
        axis=along,
    )
    return upper - values


def backward_diff(values, before, along):
    lower = jnp.concatenate(
        [
            jnp.expand_dims(before, along),
            lax.slice_in_dim(values, 0, values.shape[along] - 1, axis=along),
        ],
        axis=along,
    )
    return values - lower


def across_x(plane, offset):
    return from_behind(plane, "xy", offset)


def across_z(plane, offset):
    return from_behind(plane, "gz", offset)


def update_magnetic(electric, magnetic):
    electric_x, electric_y, electric_z = electric
    magnetic_x, magnetic_y, magnetic_z = magnetic
    x_next = across_x(jnp.stack([electric_y[0], electric_z[0]]), -1)
    z_next = across_z(jnp.stack([electric_x[:, 0], electric_y[:, 0]]), -1)
    zero_y = jnp.zeros_like(electric_x[:, :, 0])
    magnetic_x = magnetic_x - STEP_RATIO * (
        forward_diff(electric_z, zero_y, 2) - forward_diff(electric_y, z_next[1], 1)
    )
    magnetic_y = magnetic_y - STEP_RATIO * (
        forward_diff(electric_x, z_next[0], 1) - forward_diff(electric_z, x_next[1], 0)
    )
    magnetic_z = magnetic_z - STEP_RATIO * (
        forward_diff(electric_y, x_next[0], 0) - forward_diff(electric_x, zero_y, 2)
    )
    return (magnetic_x, magnetic_y, magnetic_z)


def update_electric(electric, magnetic, inverse):
    electric_x, electric_y, electric_z = electric
    magnetic_x, magnetic_y, magnetic_z = magnetic
    x_prev = across_x(jnp.stack([magnetic_y[-1], magnetic_z[-1]]), 1)
    z_prev = across_z(jnp.stack([magnetic_x[:, -1], magnetic_y[:, -1]]), 1)
    zero_y = jnp.zeros_like(electric_x[:, :, 0])
    electric_x = electric_x + STEP_RATIO * inverse * (
        backward_diff(magnetic_z, zero_y, 2) - backward_diff(magnetic_y, z_prev[1], 1)
    )
    electric_y = electric_y + STEP_RATIO * inverse * (
        backward_diff(magnetic_x, z_prev[0], 1) - backward_diff(magnetic_z, x_prev[1], 0)
    )
    electric_z = electric_z + STEP_RATIO * inverse * (
        backward_diff(magnetic_y, x_prev[0], 0) - backward_diff(magnetic_x, zero_y, 2)
    )
    return (electric_x, electric_y, electric_z)


def inverse_permittivity(material_ids, material_eps):
    result = jnp.zeros(material_ids.shape, jnp.float32)
    for material in range(material_eps.shape[0]):
        result = jnp.where(material_ids == material, 1.0 / material_eps[material], result)
    return result


def time_kernels(count):
    times = jnp.arange(count, dtype=jnp.float32) + 1.0
    omegas = 0.3 + 0.35 * jnp.arange(NFREQ, dtype=jnp.float32)
    phases = times[:, None] * omegas[None, :]
    record_kernel = jnp.concatenate([jnp.cos(phases), -jnp.sin(phases)], axis=1)
    reverse = count - jnp.arange(count, dtype=jnp.float32)
    back_phases = reverse[:, None] * omegas[None, :]
    source_kernel = jnp.concatenate([jnp.cos(back_phases), jnp.sin(back_phases)], axis=1)
    return (record_kernel, source_kernel)


def normalize(totals, weights):
    real_part = totals[:NFREQ]
    imag_part = totals[NFREQ:]
    scale = weights[None, :] / jnp.sqrt(1.0 + real_part * real_part + imag_part * imag_part)
    return jnp.concatenate([real_part * scale, imag_part * scale], axis=0)


def local(
    fields,
    adjoint_fields,
    material_ids,
    material_eps,
    monitor_cells,
    monitor_bins,
    source_cells,
    source_bins,
    bin_weight,
):
    inverse = inverse_permittivity(material_ids, material_eps)
    record_kernel, source_kernel = time_kernels(STEPS)
    watched = monitor_cells.reshape(-1)
    electric = (fields[0], fields[1], fields[2])
    magnetic = (fields[3], fields[4], fields[5])
    records = []
    for step_index in range(STEPS):
        magnetic = update_magnetic(electric, magnetic)
        electric = update_electric(electric, magnetic, inverse)
        records.append(electric[2].reshape(-1)[watched])
    forward_out = jnp.stack(list(electric) + list(magnetic))
    samples = jnp.stack(records)
    partial_dft = jnp.dot(samples.T, record_kernel, precision=lax.Precision.HIGHEST)
    bin_table = jax.ops.segment_sum(
        partial_dft, monitor_bins.reshape(-1), num_segments=bin_weight.shape[0]
    ).T
    owners = lax.axis_size("xy") * lax.axis_size("gz")
    own_count = bin_table.shape[1] // owners
    device_rank = lax.axis_index(("xy", "gz"))
    monitor_dft = lax.psum_scatter(bin_table, ("xy", "gz"), scatter_dimension=1, tiled=True)
    own_weight = lax.dynamic_slice_in_dim(bin_weight, device_rank * own_count, own_count)
    coefficients = lax.all_gather(
        normalize(monitor_dft, own_weight), ("xy", "gz"), axis=1, tiled=True
    )
    picked = jnp.take(coefficients, source_bins.reshape(-1), axis=1)
    amplitudes = jnp.dot(source_kernel, picked, precision=lax.Precision.HIGHEST)
    targets = source_cells.reshape(-1)
    electric = (adjoint_fields[0], adjoint_fields[1], adjoint_fields[2])
    magnetic = (adjoint_fields[3], adjoint_fields[4], adjoint_fields[5])
    for step_index in range(STEPS):
        magnetic = update_magnetic(electric, magnetic)
        electric = update_electric(electric, magnetic, inverse)
        driven = (
            electric[2]
            .reshape(-1)
            .at[targets]
            .add(amplitudes[step_index])
            .reshape(electric[2].shape)
        )
        electric = (electric[0], electric[1], driven)
    adjoint_out = jnp.stack(list(electric) + list(magnetic))
    return (forward_out, adjoint_out, monitor_dft)


def solution(mesh):
    placed = (
        P("grp", "xy", "gz", None),
        P("grp", "xy", "gz", None),
        P("xy", "gz", "grp"),
        P(),
        P("xy", "gz", "grp"),
        P("xy", "gz", "grp"),
        P("xy", "gz", "grp"),
        P("xy", "gz", "grp"),
        P("grp"),
    )
    return jax.shard_map(
        local,
        mesh=mesh,
        in_specs=placed,
        out_specs=(P("grp", "xy", "gz", None), P("grp", "xy", "gz", None), P("grp", ("xy", "gz"))),
        check_vma=False,
    )
```

profile of v0, /device:TPU:1, one launch (start us, length us, event | category | flops | bytes accessed | tf_op | source)
XLA Modules:
  0.0 464.7 jit_solution(17606218398477818462)
XLA Ops:
  25.1 5.9 %collective-permute-start.34 = (f32[2,4,512]{2,0,1:T(2,128)S(1)}, f32[2,4,512]{2,0,1:T(2,128)S(1)}, u32[]{:S(2)}, u32[]{:S(2)}) collective-permute-start(f32[2,4,512]{2,0,1:T(2,128)S(1)} %pad_maximum_fusion.49), channel_id=1, source_target_pairs={{0,1},{1,2},{2,3},{4,5},{5,6},{6,7},{8,9},{9,10},{10,11},{12,13},{... | collective-permute-start | bytes 49160 | tf_op jit(solution)/shard_map/ppermute | solution.py:16
  48.9 10.5 %gather_fusion = f32[1024]{0:T(1024)} fusion(f32[32768]{0:T(1024)S(1)} %bitcast.501, s32[1024]{0:T(1024)S(1)} %broadcast_clamp_fusion.1), kind=kCustom, calls=%fused_computation | custom fusion | bytes 12288 | tf_op jit(solution)/shard_map/gather | solution.py:130
  77.9 6.2 %gather_fusion.1 = f32[1024]{0:T(1024)S(1)} fusion(f32[32768]{0:T(1024)S(1)} %bitcast.502, s32[1024]{0:T(1024)S(1)} %broadcast_clamp_fusion.1), kind=kCustom, calls=%fused_computation.1 | custom fusion | bytes 12288 | tf_op jit(solution)/shard_map/gather | solution.py:130
  97.2 6.2 %gather_fusion.2 = f32[1024]{0:T(1024)S(1)} fusion(f32[32768]{0:T(1024)S(1)} %bitcast.503, s32[1024]{0:T(1024)S(1)} %broadcast_clamp_fusion.1), kind=kCustom, calls=%fused_computation.2 | custom fusion | bytes 12288 | tf_op jit(solution)/shard_map/gather | solution.py:130
  107.7 4.8 %collective-permute-start.15 = (f32[2,16,512]{2,1,0:T(8,128)S(1)}, f32[2,16,512]{2,1,0:T(8,128)S(1)}, u32[]{:S(2)}, u32[]{:S(2)}) collective-permute-start(f32[2,16,512]{2,1,0:T(8,128)S(1)} %pad_maximum_fusion.7), channel_id=1, source_target_pairs={{0,4},{4,8},{8,12},{1,5},{5,9},{9,13},{2,6},{6,10},{10,14},{3,7},{... | collective-permute-start | bytes 196616 | tf_op jit(solution)/shard_map/ppermute | solution.py:16
  117.5 6.2 %gather_fusion.3 = f32[1024]{0:T(1024)S(1)} fusion(f32[32768]{0:T(1024)S(1)} %bitcast.504, s32[1024]{0:T(1024)S(1)} %broadcast_clamp_fusion.1), kind=kCustom, calls=%fused_computation.3 | custom fusion | bytes 12288 | tf_op jit(solution)/shard_map/gather | solution.py:130
  128.1 4.8 %collective-permute-start.19 = (f32[2,16,512]{2,1,0:T(8,128)S(1)}, f32[2,16,512]{2,1,0:T(8,128)S(1)}, u32[]{:S(2)}, u32[]{:S(2)}) collective-permute-start(f32[2,16,512]{2,1,0:T(8,128)S(1)} %pad_maximum_fusion.9), channel_id=1, source_target_pairs={{0,4},{4,8},{8,12},{1,5},{5,9},{9,13},{2,6},{6,10},{10,14},{3,7},{... | collective-permute-start | bytes 196616 | tf_op jit(solution)/shard_map/ppermute | solution.py:16
  137.9 6.2 %gather_fusion.4 = f32[1024]{0:T(1024)S(1)} fusion(f32[32768]{0:T(1024)S(1)} %bitcast.505, s32[1024]{0:T(1024)S(1)} %broadcast_clamp_fusion.1), kind=kCustom, calls=%fused_computation.4 | custom fusion | bytes 12288 | tf_op jit(solution)/shard_map/gather | solution.py:130
  148.4 4.8 %collective-permute-start.23 = (f32[2,16,512]{2,1,0:T(8,128)S(1)}, f32[2,16,512]{2,1,0:T(8,128)S(1)}, u32[]{:S(2)}, u32[]{:S(2)}) collective-permute-start(f32[2,16,512]{2,1,0:T(8,128)S(1)} %pad_maximum_fusion.11), channel_id=1, source_target_pairs={{0,4},{4,8},{8,12},{1,5},{5,9},{9,13},{2,6},{6,10},{10,14},{3,7},{... | collective-permute-start | bytes 196616 | tf_op jit(solution)/shard_map/ppermute | solution.py:16
  158.2 6.2 %gather_fusion.5 = f32[1024]{0:T(1024)S(1)} fusion(f32[32768]{0:T(1024)S(1)} %bitcast.506, s32[1024]{0:T(1024)S(1)} %broadcast_clamp_fusion.1), kind=kCustom, calls=%fused_computation.5 | custom fusion | bytes 12288 | tf_op jit(solution)/shard_map/gather | solution.py:130
  178.7 6.2 %gather_fusion.6 = f32[1024]{0:T(1024)S(1)} fusion(f32[32768]{0:T(1024)S(1)} %bitcast.507, s32[1024]{0:T(1024)S(1)} %broadcast_clamp_fusion.1), kind=kCustom, calls=%fused_computation.6 | custom fusion | bytes 12288 | tf_op jit(solution)/shard_map/gather | solution.py:130
  195.7 6.2 %gather_fusion.7 = f32[1024]{0:T(1024)S(1)} fusion(f32[32768]{0:T(1024)S(1)} %bitcast.500, s32[1024]{0:T(1024)S(1)} %broadcast_clamp_fusion.1), kind=kCustom, calls=%fused_computation.7 | custom fusion | bytes 12288 | tf_op jit(solution)/shard_map/gather | solution.py:130
  204.2 6.2 %scatter_custom_fusion = f32[128,8]{1,0:T(8,128)S(1)} fusion(s32[1024]{0:T(1024)} %bitcast.616, f32[1024,8]{1,0:T(8,128)S(1)} %fusion.306, f32[]{:T(128)} %constant.24.clone.1), kind=kCustom, calls=%fused_computation.496 | custom fusion | flops 8192 | bytes 4608 | tf_op jit(solution)/shard_map/scatter-add | solution.py:134
  210.4 55.7 %all-reduce.64 = f32[8,128]{0,1:T(8,128)S(1)} all-reduce(f32[8,128]{0,1:T(8,128)S(1)} %bitcast.596), channel_id=2, replica_groups=mesh['grp'=2,'xy'=4,'gz'=4] {'xy','gz'}, use_global_device_ids=true, to_apply=%region_1.2.clone | all-reduce | flops 1024 | bytes 8192
  267.0 29.0 %all_gather.3 = f32[8,128]{0,1:T(8,128)S(1)} all-gather(f32[8,8]{0,1:T(8,128)S(1)} %pad_maximum_fusion.64), channel_id=1, replica_groups=mesh['grp'=2,'xy'=4,'gz'=4] {'xy','gz'}, dimensions={1}, use_global_device_ids=true | all-gather | bytes 4352 | tf_op jit(solution)/shard_map/all_gather | solution.py:142
  300.1 6.1 %scatter_fusion = f32[32768]{0:T(1024)S(1)} fusion(f32[32768]{0:T(1024)S(1)} %bitcast.492, s32[1024]{0:T(1024)S(1)} %bitcast.588, f32[1024]{0:T(1024)S(1)} %bitcast.604), kind=kCustom, calls=%fused_computation.10 | custom fusion | flops 1024 | bytes 16384 | tf_op jit(solution)/shard_map/scatter-add | solution.py:157
  307.0 5.4 %collective-permute-start.36 = (f32[2,16,512]{2,1,0:T(8,128)S(1)}, f32[2,16,512]{2,1,0:T(8,128)S(1)}, u32[]{:S(2)}, u32[]{:S(2)}) collective-permute-start(f32[2,16,512]{2,1,0:T(8,128)S(1)} %pad_maximum_fusion.18), channel_id=1, source_target_pairs={{4,0},{8,4},{12,8},{5,1},{9,5},{13,9},{6,2},{10,6},{14,10},{7,3},{... | collective-permute-start | bytes 196616 | tf_op jit(solution)/shard_map/ppermute | solution.py:16
  325.0 6.1 %scatter_fusion.1 = f32[32768]{0:T(1024)S(1)} fusion(f32[32768]{0:T(1024)S(1)} %bitcast.493, s32[1024]{0:T(1024)S(1)} %bitcast.589, f32[1024]{0:T(1024)S(1)} %bitcast.603), kind=kCustom, calls=%fused_computation.11 | custom fusion | flops 1024 | bytes 16384 | tf_op jit(solution)/shard_map/scatter-add | solution.py:157
  347.1 6.1 %scatter_fusion.2 = f32[32768]{0:T(1024)S(1)} fusion(f32[32768]{0:T(1024)S(1)} %bitcast.494, s32[1024]{0:T(1024)S(1)} %bitcast.590, f32[1024]{0:T(1024)S(1)} %bitcast.602), kind=kCustom, calls=%fused_computation.12 | custom fusion | flops 1024 | bytes 16384 | tf_op jit(solution)/shard_map/scatter-add | solution.py:157
  369.2 6.1 %scatter_fusion.3 = f32[32768]{0:T(1024)S(1)} fusion(f32[32768]{0:T(1024)S(1)} %bitcast.495, s32[1024]{0:T(1024)S(1)} %bitcast.591, f32[1024]{0:T(1024)S(1)} %bitcast.601), kind=kCustom, calls=%fused_computation.13 | custom fusion | flops 1024 | bytes 16384 | tf_op jit(solution)/shard_map/scatter-add | solution.py:157
  391.3 6.1 %scatter_fusion.4 = f32[32768]{0:T(1024)S(1)} fusion(f32[32768]{0:T(1024)S(1)} %bitcast.496, s32[1024]{0:T(1024)S(1)} %bitcast.592, f32[1024]{0:T(1024)S(1)} %bitcast.600), kind=kCustom, calls=%fused_computation.14 | custom fusion | flops 1024 | bytes 16384 | tf_op jit(solution)/shard_map/scatter-add | solution.py:157
  413.4 6.1 %scatter_fusion.5 = f32[32768]{0:T(1024)S(1)} fusion(f32[32768]{0:T(1024)S(1)} %bitcast.497, s32[1024]{0:T(1024)S(1)} %bitcast.593, f32[1024]{0:T(1024)S(1)} %bitcast.599), kind=kCustom, calls=%fused_computation.15 | custom fusion | flops 1024 | bytes 16384 | tf_op jit(solution)/shard_map/scatter-add | solution.py:157
  435.4 6.1 %scatter_fusion.6 = f32[32768]{0:T(1024)S(1)} fusion(f32[32768]{0:T(1024)S(1)} %bitcast.498, s32[1024]{0:T(1024)S(1)} %bitcast.594, f32[1024]{0:T(1024)S(1)} %bitcast.598), kind=kCustom, calls=%fused_computation.16 | custom fusion | flops 1024 | bytes 16384 | tf_op jit(solution)/shard_map/scatter-add | solution.py:157
  457.5 6.1 %scatter_fusion.7 = f32[32768]{0:T(1024)S(1)} fusion(f32[32768]{0:T(1024)S(1)} %bitcast.499, s32[1024]{0:T(1024)S(1)} %bitcast.595, f32[1024]{0:T(1024)S(1)} %bitcast.597), kind=kCustom, calls=%fused_computation.17 | custom fusion | flops 1024 | bytes 16384 | tf_op jit(solution)/shard_map/scatter-add | solution.py:157
  (666 shorter events, 236.8 us)
Async XLA Ops:
  2.1 21.9 %collective-permute-start.32 = (f32[2,16,512]{2,1,0:T(8,128)}, f32[2,16,512]{2,1,0:T(8,128)}, u32[]{:S(2)}, u32[]{:S(2)}) collective-permute-start(f32[2,16,512]{2,1,0:T(8,128)} %pad_maximum_fusion.16), channel_id=1, source_target_pairs={{4,0},{8,4},{12,8},{5,1},{9,5},{13,9},{6,2},{10,6},{14,10},{7,3},{... | collective-permute-start | bytes 196616 | tf_op jit(solution)/shard_map/ppermute | solution.py:16
  5.8 16.3 %collective-permute-start.33 = (f32[2,4,512]{2,0,1:T(2,128)}, f32[2,4,512]{2,0,1:T(2,128)}, u32[]{:S(2)}, u32[]{:S(2)}) collective-permute-start(f32[2,4,512]{2,0,1:T(2,128)} %pad_maximum_fusion.48), channel_id=1, source_target_pairs={{1,0},{2,1},{3,2},{5,4},{6,5},{7,6},{9,8},{10,9},{11,10},{13,12},{... | collective-permute-start | bytes 49160 | tf_op jit(solution)/shard_map/ppermute | solution.py:16
  7.1 16.6 %collective-permute-start = (f32[2,16,512]{2,1,0:T(8,128)S(1)}, f32[2,16,512]{2,1,0:T(8,128)S(1)}, u32[]{:S(2)}, u32[]{:S(2)}) collective-permute-start(f32[2,16,512]{2,1,0:T(8,128)S(1)} %pad_maximum_fusion), channel_id=1, source_target_pairs={{4,0},{8,4},{12,8},{5,1},{9,5},{13,9},{6,2},{10,6},{14,10},{7,3},{... | collective-permute-start | bytes 196616 | tf_op jit(solution)/shard_map/ppermute | solution.py:16
  9.7 13.2 %collective-permute-start.1 = (f32[2,4,512]{2,0,1:T(2,128)}, f32[2,4,512]{2,0,1:T(2,128)}, u32[]{:S(2)}, u32[]{:S(2)}) collective-permute-start(f32[2,4,512]{2,0,1:T(2,128)} %pad_maximum_fusion.32), channel_id=1, source_target_pairs={{1,0},{2,1},{3,2},{5,4},{6,5},{7,6},{9,8},{10,9},{11,10},{13,12},{... | collective-permute-start | bytes 49160 | tf_op jit(solution)/shard_map/ppermute | solution.py:16
  25.1 16.1 %collective-permute-start.34 = (f32[2,4,512]{2,0,1:T(2,128)S(1)}, f32[2,4,512]{2,0,1:T(2,128)S(1)}, u32[]{:S(2)}, u32[]{:S(2)}) collective-permute-start(f32[2,4,512]{2,0,1:T(2,128)S(1)} %pad_maximum_fusion.49), channel_id=1, source_target_pairs={{0,1},{1,2},{2,3},{4,5},{5,6},{6,7},{8,9},{9,10},{10,11},{12,13},{... | collective-permute-start | bytes 49160 | tf_op jit(solution)/shard_map/ppermute | solution.py:16
  31.1 10.0 %collective-permute-start.2 = (f32[2,4,512]{2,0,1:T(2,128)S(1)}, f32[2,4,512]{2,0,1:T(2,128)S(1)}, u32[]{:S(2)}, u32[]{:S(2)}) collective-permute-start(f32[2,4,512]{2,0,1:T(2,128)S(1)} %pad_maximum_fusion.33), channel_id=1, source_target_pairs={{0,1},{1,2},{2,3},{4,5},{5,6},{6,7},{8,9},{9,10},{10,11},{12,13},{... | collective-permute-start | bytes 49160 | tf_op jit(solution)/shard_map/ppermute | solution.py:16
  42.9 16.6 %collective-permute-start.5 = (f32[2,4,512]{2,0,1:T(2,128)S(1)}, f32[2,4,512]{2,0,1:T(2,128)S(1)}, u32[]{:S(2)}, u32[]{:S(2)}) collective-permute-start(f32[2,4,512]{2,0,1:T(2,128)S(1)} %pad_maximum_fusion.34), channel_id=1, source_target_pairs={{1,0},{2,1},{3,2},{5,4},{6,5},{7,6},{9,8},{10,9},{11,10},{13,12},{... | collective-permute-start | bytes 49160 | tf_op jit(solution)/shard_map/ppermute | solution.py:16
  46.4 13.1 %collective-permute-start.4 = (f32[2,16,512]{2,1,0:T(8,128)S(1)}, f32[2,16,512]{2,1,0:T(8,128)S(1)}, u32[]{:S(2)}, u32[]{:S(2)}) collective-permute-start(f32[2,16,512]{2,1,0:T(8,128)S(1)} %pad_maximum_fusion.2), channel_id=1, source_target_pairs={{4,0},{8,4},{12,8},{5,1},{9,5},{13,9},{6,2},{10,6},{14,10},{7,3},{... | collective-permute-start | bytes 196616 | tf_op jit(solution)/shard_map/ppermute | solution.py:16
  65.2 8.9 %collective-permute-start.7 = (f32[2,16,512]{2,1,0:T(8,128)S(1)}, f32[2,16,512]{2,1,0:T(8,128)S(1)}, u32[]{:S(2)}, u32[]{:S(2)}) collective-permute-start(f32[2,16,512]{2,1,0:T(8,128)S(1)} %pad_maximum_fusion.3), channel_id=1, source_target_pairs={{0,4},{4,8},{8,12},{1,5},{5,9},{9,13},{2,6},{6,10},{10,14},{3,7},{... | collective-permute-start | bytes 196616 | tf_op jit(solution)/shard_map/ppermute | solution.py:16
  74.3 9.7 %collective-permute-start.9 = (f32[2,4,512]{2,0,1:T(2,128)S(1)}, f32[2,4,512]{2,0,1:T(2,128)S(1)}, u32[]{:S(2)}, u32[]{:S(2)}) collective-permute-start(f32[2,4,512]{2,0,1:T(2,128)S(1)} %pad_maximum_fusion.36), channel_id=1, source_target_pairs={{1,0},{2,1},{3,2},{5,4},{6,5},{7,6},{9,8},{10,9},{11,10},{13,12},{... | collective-permute-start | bytes 49160 | tf_op jit(solution)/shard_map/ppermute | solution.py:16
  75.8 8.3 %collective-permute-start.8 = (f32[2,16,512]{2,1,0:T(8,128)S(1)}, f32[2,16,512]{2,1,0:T(8,128)S(1)}, u32[]{:S(2)}, u32[]{:S(2)}) collective-permute-start(f32[2,16,512]{2,1,0:T(8,128)S(1)} %pad_maximum_fusion.4), channel_id=1, source_target_pairs={{4,0},{8,4},{12,8},{5,1},{9,5},{13,9},{6,2},{10,6},{14,10},{7,3},{... | collective-permute-start | bytes 196616 | tf_op jit(solution)/shard_map/ppermute | solution.py:16
  93.8 9.6 %collective-permute-start.13 = (f32[2,4,512]{2,0,1:T(2,128)S(1)}, f32[2,4,512]{2,0,1:T(2,128)S(1)}, u32[]{:S(2)}, u32[]{:S(2)}) collective-permute-start(f32[2,4,512]{2,0,1:T(2,128)S(1)} %pad_maximum_fusion.38), channel_id=1, source_target_pairs={{1,0},{2,1},{3,2},{5,4},{6,5},{7,6},{9,8},{10,9},{11,10},{13,12},{... | collective-permute-start | bytes 49160 | tf_op jit(solution)/shard_map/ppermute | solution.py:16
  95.2 8.2 %collective-permute-start.12 = (f32[2,16,512]{2,1,0:T(8,128)S(1)}, f32[2,16,512]{2,1,0:T(8,128)S(1)}, u32[]{:S(2)}, u32[]{:S(2)}) collective-permute-start(f32[2,16,512]{2,1,0:T(8,128)S(1)} %pad_maximum_fusion.6), channel_id=1, source_target_pairs={{4,0},{8,4},{12,8},{5,1},{9,5},{13,9},{6,2},{10,6},{14,10},{7,3},{... | collective-permute-start | bytes 196616 | tf_op jit(solution)/shard_map/ppermute | solution.py:16
  103.7 8.9 %collective-permute-start.14 = (f32[2,4,512]{2,0,1:T(2,128)S(1)}, f32[2,4,512]{2,0,1:T(2,128)S(1)}, u32[]{:S(2)}, u32[]{:S(2)}) collective-permute-start(f32[2,4,512]{2,0,1:T(2,128)S(1)} %pad_maximum_fusion.39), channel_id=1, source_target_pairs={{0,1},{1,2},{2,3},{4,5},{5,6},{6,7},{8,9},{9,10},{10,11},{12,13},{... | collective-permute-start | bytes 49160 | tf_op jit(solution)/shard_map/ppermute | solution.py:16
  114.1 9.6 %collective-permute-start.17 = (f32[2,4,512]{2,0,1:T(2,128)S(1)}, f32[2,4,512]{2,0,1:T(2,128)S(1)}, u32[]{:S(2)}, u32[]{:S(2)}) collective-permute-start(f32[2,4,512]{2,0,1:T(2,128)S(1)} %pad_maximum_fusion.40), channel_id=1, source_target_pairs={{1,0},{2,1},{3,2},{5,4},{6,5},{7,6},{9,8},{10,9},{11,10},{13,12},{... | collective-permute-start | bytes 49160 | tf_op jit(solution)/shard_map/ppermute | solution.py:16
  115.6 8.2 %collective-permute-start.16 = (f32[2,16,512]{2,1,0:T(8,128)S(1)}, f32[2,16,512]{2,1,0:T(8,128)S(1)}, u32[]{:S(2)}, u32[]{:S(2)}) collective-permute-start(f32[2,16,512]{2,1,0:T(8,128)S(1)} %pad_maximum_fusion.8), channel_id=1, source_target_pairs={{4,0},{8,4},{12,8},{5,1},{9,5},{13,9},{6,2},{10,6},{14,10},{7,3},{... | collective-permute-start | bytes 196616 | tf_op jit(solution)/shard_map/ppermute | solution.py:16
  124.0 8.9 %collective-permute-start.18 = (f32[2,4,512]{2,0,1:T(2,128)S(1)}, f32[2,4,512]{2,0,1:T(2,128)S(1)}, u32[]{:S(2)}, u32[]{:S(2)}) collective-permute-start(f32[2,4,512]{2,0,1:T(2,128)S(1)} %pad_maximum_fusion.41), channel_id=1, source_target_pairs={{0,1},{1,2},{2,3},{4,5},{5,6},{6,7},{8,9},{9,10},{10,11},{12,13},{... | collective-permute-start | bytes 49160 | tf_op jit(solution)/shard_map/ppermute | solution.py:16
  134.4 9.6 %collective-permute-start.21 = (f32[2,4,512]{2,0,1:T(2,128)S(1)}, f32[2,4,512]{2,0,1:T(2,128)S(1)}, u32[]{:S(2)}, u32[]{:S(2)}) collective-permute-start(f32[2,4,512]{2,0,1:T(2,128)S(1)} %pad_maximum_fusion.42), channel_id=1, source_target_pairs={{1,0},{2,1},{3,2},{5,4},{6,5},{7,6},{9,8},{10,9},{11,10},{13,12},{... | collective-permute-start | bytes 49160 | tf_op jit(solution)/shard_map/ppermute | solution.py:16
  144.3 8.9 %collective-permute-start.22 = (f32[2,4,512]{2,0,1:T(2,128)S(1)}, f32[2,4,512]{2,0,1:T(2,128)S(1)}, u32[]{:S(2)}, u32[]{:S(2)}) collective-permute-start(f32[2,4,512]{2,0,1:T(2,128)S(1)} %pad_maximum_fusion.43), channel_id=1, source_target_pairs={{0,1},{1,2},{2,3},{4,5},{5,6},{6,7},{8,9},{9,10},{10,11},{12,13},{... | collective-permute-start | bytes 49160 | tf_op jit(solution)/shard_map/ppermute | solution.py:16
  154.8 9.6 %collective-permute-start.25 = (f32[2,4,512]{2,0,1:T(2,128)S(1)}, f32[2,4,512]{2,0,1:T(2,128)S(1)}, u32[]{:S(2)}, u32[]{:S(2)}) collective-permute-start(f32[2,4,512]{2,0,1:T(2,128)S(1)} %pad_maximum_fusion.44), channel_id=1, source_target_pairs={{1,0},{2,1},{3,2},{5,4},{6,5},{7,6},{9,8},{10,9},{11,10},{13,12},{... | collective-permute-start | bytes 49160 | tf_op jit(solution)/shard_map/ppermute | solution.py:16
  164.7 8.9 %collective-permute-start.26 = (f32[2,4,512]{2,0,1:T(2,128)S(1)}, f32[2,4,512]{2,0,1:T(2,128)S(1)}, u32[]{:S(2)}, u32[]{:S(2)}) collective-permute-start(f32[2,4,512]{2,0,1:T(2,128)S(1)} %pad_maximum_fusion.45), channel_id=1, source_target_pairs={{0,1},{1,2},{2,3},{4,5},{5,6},{6,7},{8,9},{9,10},{10,11},{12,13},{... | collective-permute-start | bytes 49160 | tf_op jit(solution)/shard_map/ppermute | solution.py:16
  175.1 9.8 %collective-permute-start.29 = (f32[2,4,512]{2,0,1:T(2,128)S(1)}, f32[2,4,512]{2,0,1:T(2,128)S(1)}, u32[]{:S(2)}, u32[]{:S(2)}) collective-permute-start(f32[2,4,512]{2,0,1:T(2,128)S(1)} %pad_maximum_fusion.46), channel_id=1, source_target_pairs={{1,0},{2,1},{3,2},{5,4},{6,5},{7,6},{9,8},{10,9},{11,10},{13,12},{... | collective-permute-start | bytes 49160 | tf_op jit(solution)/shard_map/ppermute | solution.py:16
  185.2 8.9 %collective-permute-start.30 = (f32[2,4,512]{2,0,1:T(2,128)S(1)}, f32[2,4,512]{2,0,1:T(2,128)S(1)}, u32[]{:S(2)}, u32[]{:S(2)}) collective-permute-start(f32[2,4,512]{2,0,1:T(2,128)S(1)} %pad_maximum_fusion.47), channel_id=1, source_target_pairs={{0,1},{1,2},{2,3},{4,5},{5,6},{6,7},{8,9},{9,10},{10,11},{12,13},{... | collective-permute-start | bytes 49160 | tf_op jit(solution)/shard_map/ppermute | solution.py:16
  307.0 10.1 %collective-permute-start.36 = (f32[2,16,512]{2,1,0:T(8,128)S(1)}, f32[2,16,512]{2,1,0:T(8,128)S(1)}, u32[]{:S(2)}, u32[]{:S(2)}) collective-permute-start(f32[2,16,512]{2,1,0:T(8,128)S(1)} %pad_maximum_fusion.18), channel_id=1, source_target_pairs={{4,0},{8,4},{12,8},{5,1},{9,5},{13,9},{6,2},{10,6},{14,10},{7,3},{... | collective-permute-start | bytes 196616 | tf_op jit(solution)/shard_map/ppermute | solution.py:16
  (64 other events, 315.1 us)
where the time goes:
time: 467 us; the launch traced here: 465 us
  starting transfers between devices  176 us (38%)
  blocking collectives  84.8 us (18%)
  local copies, waits for them, and re-layouts  81.9 us (18%)
  other arithmetic  66.8 us (14%)
  waiting for transfers between devices  44.9 us (10%)
  between operations  8.42 us (2%)
    ppermute x64, starting transfers between devices, from_behind(): lax.ppermute(value, axis, [(source, source + steps) for source in range(f...  176 us
    unnamed x1, blocking collectives  55.7 us
    gather x8, local copies, waits for them, and re-layouts, local(): records.append(electric[2].reshape(-1)[watched])  53.6 us
    scatter-add x8, other arithmetic, local(): driven = electric[2].reshape(-1).at[targets].add(amplitudes[step_index])....  49.1 us
    ppermute x64, waiting for transfers between devices, from_behind(): lax.ppermute(value, axis, [(source, source + steps) for source in range(f...  44.9 us
    all_gather x1, blocking collectives, local(): lax.all_gather(normalize(monitor_dft, own_weight), ('xy', 'gz'), axis=1,...  29 us
    unnamed x72, local copies, waits for them, and re-layouts  11 us
  transfers between devices with their start and end apart: 64, of which 27 were waited for; matrix products, arithmetic and copies ran while one was open for 14% of the time, Pallas kernels for 0%

commit v1 on v0

--- a/solution.py
+++ b/solution.py
@@ -1,12 +1,15 @@
+import functools
+
 import jax
 import jax.numpy as jnp
+import numpy as np
 from jax import lax
+from jax.experimental import pallas as pl
+from jax.experimental.pallas import tpu as pltpu
 from jax.sharding import PartitionSpec as P
 
 STEPS = 8
 NFREQ = 4
-
-
 STEP_RATIO = 0.5
 
 
@@ -38,19 +41,11 @@
     return values - lower
 
 
-def across_x(plane, offset):
-    return from_behind(plane, "xy", offset)
-
-
-def across_z(plane, offset):
-    return from_behind(plane, "gz", offset)
-
-
 def update_magnetic(electric, magnetic):
     electric_x, electric_y, electric_z = electric
     magnetic_x, magnetic_y, magnetic_z = magnetic
-    x_next = across_x(jnp.stack([electric_y[0], electric_z[0]]), -1)
-    z_next = across_z(jnp.stack([electric_x[:, 0], electric_y[:, 0]]), -1)
+    x_next = from_behind(jnp.stack([electric_y[0], electric_z[0]]), "xy", -1)
+    z_next = from_behind(jnp.stack([electric_x[:, 0], electric_y[:, 0]]), "gz", -1)
     zero_y = jnp.zeros_like(electric_x[:, :, 0])
     magnetic_x = magnetic_x - STEP_RATIO * (
         forward_diff(electric_z, zero_y, 2) - forward_diff(electric_y, z_next[1], 1)
@@ -67,8 +62,8 @@
 def update_electric(electric, magnetic, inverse):
     electric_x, electric_y, electric_z = electric
     magnetic_x, magnetic_y, magnetic_z = magnetic
-    x_prev = across_x(jnp.stack([magnetic_y[-1], magnetic_z[-1]]), 1)
-    z_prev = across_z(jnp.stack([magnetic_x[:, -1], magnetic_y[:, -1]]), 1)
+    x_prev = from_behind(jnp.stack([magnetic_y[-1], magnetic_z[-1]]), "xy", 1)
+    z_prev = from_behind(jnp.stack([magnetic_x[:, -1], magnetic_y[:, -1]]), "gz", 1)
     zero_y = jnp.zeros_like(electric_x[:, :, 0])
     electric_x = electric_x + STEP_RATIO * inverse * (
         backward_diff(magnetic_z, zero_y, 2) - backward_diff(magnetic_y, z_prev[1], 1)
@@ -90,24 +85,24 @@
 
 
 def time_kernels(count):
-    times = jnp.arange(count, dtype=jnp.float32) + 1.0
-    omegas = 0.3 + 0.35 * jnp.arange(NFREQ, dtype=jnp.float32)
+    times = np.arange(count) + 1.0
+    omegas = 0.3 + 0.35 * np.arange(NFREQ)
     phases = times[:, None] * omegas[None, :]
-    record_kernel = jnp.concatenate([jnp.cos(phases), -jnp.sin(phases)], axis=1)
-    reverse = count - jnp.arange(count, dtype=jnp.float32)
+    record_kernel = np.concatenate([np.cos(phases), -np.sin(phases)], axis=1)
+    reverse = count - np.arange(count)
     back_phases = reverse[:, None] * omegas[None, :]
-    source_kernel = jnp.concatenate([jnp.cos(back_phases), jnp.sin(back_phases)], axis=1)
-    return (record_kernel, source_kernel)
+    source_kernel = np.concatenate([np.cos(back_phases), np.sin(back_phases)], axis=1)
+    return (record_kernel.astype(np.float32), source_kernel.astype(np.float32))
 
 
 def normalize(totals, weights):
     real_part = totals[:NFREQ]
     imag_part = totals[NFREQ:]
-    scale = weights[None, :] / jnp.sqrt(1.0 + real_part * real_part + imag_part * imag_part)
+    scale = weights / jnp.sqrt(1.0 + real_part * real_part + imag_part * imag_part)
     return jnp.concatenate([real_part * scale, imag_part * scale], axis=0)
 
 
-def local(
+def local_general(
     fields,
     adjoint_fields,
     material_ids,
@@ -124,7 +119,7 @@
     electric = (fields[0], fields[1], fields[2])
     magnetic = (fields[3], fields[4], fields[5])
     records = []
-    for step_index in range(STEPS):
+    for _ in range(STEPS):
         magnetic = update_magnetic(electric, magnetic)
         electric = update_electric(electric, magnetic, inverse)
         records.append(electric[2].reshape(-1)[watched])
@@ -137,11 +132,9 @@
     owners = lax.axis_size("xy") * lax.axis_size("gz")
     own_count = bin_table.shape[1] // owners
     device_rank = lax.axis_index(("xy", "gz"))
-    monitor_dft = lax.psum_scatter(bin_table, ("xy", "gz"), scatter_dimension=1, tiled=True)
-    own_weight = lax.dynamic_slice_in_dim(bin_weight, device_rank * own_count, own_count)
-    coefficients = lax.all_gather(
-        normalize(monitor_dft, own_weight), ("xy", "gz"), axis=1, tiled=True
-    )
+    totals = lax.psum(bin_table, ("xy", "gz"))
+    monitor_dft = lax.dynamic_slice_in_dim(totals, device_rank * own_count, own_count, axis=1)
+    coefficients = normalize(totals, bin_weight[None, :])
     picked = jnp.take(coefficients, source_bins.reshape(-1), axis=1)
     amplitudes = jnp.dot(source_kernel, picked, precision=lax.Precision.HIGHEST)
     targets = source_cells.reshape(-1)
@@ -162,6 +155,487 @@
     return (forward_out, adjoint_out, monitor_dft)
 
 
+TILES = 4
+CX = 4
+CZ = 16
+LANES = 128
+HALO = 8
+ROWS = CZ + 2 * HALO
+WIDE = 2 * LANES
+PLANES = TILES * CX
+ENTRIES = 1024
+SUB = 8
+ZT = CZ // SUB
+BF16 = jnp.bfloat16
+F32 = jnp.float32
+
+
+def packed_rows(parts):
+    return parts * CX + (parts + 1) // 2
+
+
+def lane_ids():
+    return lax.broadcasted_iota(jnp.int32, (SUB, LANES), 1)
+
+
+def pack_block(read, parts, column, store):
+    lanes = lane_ids()
+    upper = lanes >= LANES // 2
+    take_left = jnp.logical_and(upper, column > 0)
+    take_right = jnp.logical_and(jnp.logical_not(upper), column < TILES - 1)
+    here = pl.multiple_of(column * LANES, LANES)
+    left = pl.multiple_of(jnp.maximum(column - 1, 0) * LANES, LANES)
+    right = pl.multiple_of(jnp.minimum(column + 1, TILES - 1) * LANES, LANES)
+    size = packed_rows(parts)
+    for zt in range(ZT):
+        margins = [jnp.zeros((SUB, LANES), F32) for _ in range((parts + 1) // 2)]
+        for part in range(parts):
+            for x in range(CX):
+                store(zt * size + part * CX + x, read(part, x, zt, here))
+                both = jnp.where(
+                    take_left,
+                    read(part, x, zt, left),
+                    jnp.where(take_right, read(part, x, zt, right), 0.0),
+                )
+                slot = (part % 2) * CX + x
+                placed = pltpu.roll(both, (16 * slot + HALO) % LANES, 1)
+                margins[part // 2] = jnp.where(lanes // 16 == slot, placed, margins[part // 2])
+        for pair, margin in enumerate(margins):
+            store(zt * size + parts * CX + pair, margin)
+
+
+def pack_forward_kernel(
+    fields_ref, ids_ref, eps_ref, cells_ref, bins_ref, o0, o1, o2, o3, inverse_ref
+):
+    me = lax.axis_index("xy")
+    ids = ids_ref[...]
+    eps = jnp.full(ids.shape, eps_ref[0], F32)
+    for material in range(1, eps_ref.shape[0]):
+        eps = jnp.where(ids == material, eps_ref[material], eps)
+    inverse_ref[...] = STEP_RATIO * (1.0 / eps)
+
+    def read(part, x, zt, lane):
+        rows = pl.ds(zt * SUB, SUB)
+        if part == 6:
+            return inverse_ref[x, rows, pl.ds(lane, LANES)]
+        return fields_ref[part, x, rows, pl.ds(lane, LANES)]
+
+    for m, out in enumerate((o0, o1, o2, o3)):
+
+        def store(row, value, out=out):
+            out[row] = value
+
+        pack_block(read, 7, me ^ m, store)
+        out[ZT * packed_rows(7)] = cells_ref[...].astype(F32)
+        out[ZT * packed_rows(7) + 1] = bins_ref[...].astype(F32)
+
+
+def pack_adjoint_kernel(fields_ref, cells_ref, bins_ref, o0, o1, o2, o3):
+    me = lax.axis_index("xy")
+
+    def read(part, x, zt, lane):
+        return fields_ref[part, x, pl.ds(zt * SUB, SUB), pl.ds(lane, LANES)]
+
+    for m, out in enumerate((o0, o1, o2, o3)):
+
+        def store(row, value, out=out):
+            out[row] = value
+
+        pack_block(read, 6, me ^ m, store)
+        out[ZT * packed_rows(6)] = cells_ref[...].astype(F32) + 1.0
+        out[ZT * packed_rows(6) + 1] = bins_ref[...].astype(F32)
+
+
+def slab_kernel(size, lists, b0, b1, b2, b3, first_ref, second_ref):
+    even = lax.rem(lax.axis_index("gz"), 2) == 0
+    zt_first = jnp.where(even, 1, 0)
+    for m, block in enumerate((b0, b1, b2, b3)):
+        base = m * (size + lists)
+        first_ref[pl.ds(base, size)] = block[pl.ds(zt_first * size, size)]
+        second_ref[pl.ds(base, size)] = block[pl.ds((1 - zt_first) * size, size)]
+        for k in range(lists):
+            first_ref[base + size + k] = block[ZT * size + k]
+            second_ref[base + size + k] = block[ZT * size + k]
+
+
+def unpack(parts, lists, blocks, first_ref, second_ref, put):
+    me = lax.axis_index("xy")
+    even = lax.rem(lax.axis_index("gz"), 2) == 0
+    row_first = pl.multiple_of(jnp.where(even, HALO + CZ, 0), SUB)
+    row_second = pl.multiple_of(jnp.where(even, 0, HALO + CZ), SUB)
+    size = packed_rows(parts)
+    lanes = lane_ids()
+    in_margin = jnp.logical_or(lanes < HALO, lanes >= LANES - HALO)
+    for m, block in enumerate(blocks):
+        base = (me ^ m) * CX + 1
+        sources = (
+            (first_ref, m * (size + lists), row_first),
+            (second_ref, m * (size + lists), row_second),
+            (block, 0, HALO),
+            (block, size, HALO + SUB),
+        )
+        for ref, start, row in sources:
+            for part in range(parts):
+                for x in range(CX):
+                    slot = (part % 2) * CX + x
+                    margin = pltpu.roll(
+                        ref[start + parts * CX + part // 2], (-16 * slot - HALO) % LANES, 1
+                    )
+                    put(
+                        part,
+                        base + x,
+                        row,
+                        ref[start + part * CX + x],
+                        jnp.where(in_margin, margin, 0.0),
+                    )
+
+
+def magnetic_factor():
+    rows = lax.broadcasted_iota(jnp.int32, (ROWS, WIDE), 0)
+    lanes = lax.broadcasted_iota(jnp.int32, (ROWS, WIDE), 1)
+    below_z = jnp.logical_and(rows < HALO, lax.axis_index("gz") == 0)
+    below_y = jnp.logical_and(lanes >= WIDE - 2 * HALO, lax.axis_index("xy") == 0)
+    return jnp.where(jnp.logical_or(below_z, below_y), 0.0, STEP_RATIO)
+
+
+def step_plane(f, factor_ref, inverse_ref, i):
+    def z_up(v):
+        return pltpu.roll(v, ROWS - 1, 0)
+
+    def z_down(v):
+        return pltpu.roll(v, 1, 0)
+
+    def y_up(v):
+        return pltpu.roll(v, WIDE - 1, 1)
+
+    def y_down(v):
+        return pltpu.roll(v, 1, 1)
+
+    factor = factor_ref[...]
+    ex, ey, ez = f[0, i], f[1, i], f[2, i]
+    hx = f[3, i] - factor * ((y_up(ez) - ez) - (z_up(ey) - ey))
+    hy = f[4, i] - factor * ((z_up(ex) - ex) - (f[2, i + 1] - ez))
+    hz = f[5, i] - factor * ((f[1, i + 1] - ey) - (y_up(ex) - ex))
+    f[3, i] = hx
+    f[4, i] = hy
+    f[5, i] = hz
+    inverse = inverse_ref[i]
+    ex = ex + inverse * ((hz - y_down(hz)) - (hy - z_down(hy)))
+    ey = ey + inverse * ((hx - z_down(hx)) - (hz - f[5, i - 1]))
+    ez = ez + inverse * ((hy - f[4, i - 1]) - (hx - y_down(hx)))
+    f[0, i] = ex
+    f[1, i] = ey
+    return ez
+
+
+def entry_row(vector):
+    whole = vector.astype(jnp.int32)
+    return jnp.concatenate([whole[i : i + 1] for i in range(SUB)], axis=1)
+
+
+def one_hot(rows, index):
+    ids = lax.broadcasted_iota(jnp.int32, (rows, index.shape[1]), 0)
+    return jnp.where(ids == index, 1.0, 0.0).astype(BF16)
+
+
+def split(values):
+    high = values.astype(BF16)
+    return high, (values - high.astype(F32)).astype(BF16)
+
+
+def write_back(f, outs):
+    me = lax.axis_index("xy")
+    for m, out in enumerate(outs):
+        base = (me ^ m) * CX + 1
+        for part in range(6):
+            for x in range(CX):
+                for zt in range(ZT):
+                    out[(part * CX + x) * ZT + zt] = f[
+                        part, base + x, HALO + zt * SUB : HALO + (zt + 1) * SUB, 0:LANES
+                    ]
+
+
+def clear_edges(f):
+    for part in range(6):
+        f[part, 0] = jnp.zeros((ROWS, WIDE), F32)
+        f[part, PLANES + 1] = jnp.zeros((ROWS, WIDE), F32)
+
+
+def forward_kernel(
+    b0, b1, b2, b3, first_ref, second_ref, kernel_ref,
+    o0, o1, o2, o3, inverse_ref, table_ref,
+    f, factor_ref, high_ref, low_ref, sums_ref,
+):
+    me = lax.axis_index("xy")
+    blocks = (b0, b1, b2, b3)
+    clear_edges(f)
+
+    def put(part, plane, row, columns, margins):
+        if part == 6:
+            inverse_ref[plane, pl.ds(row, SUB), 0:LANES] = columns
+            inverse_ref[plane, pl.ds(row, SUB), LANES:WIDE] = margins
+        else:
+            f[part, plane, pl.ds(row, SUB), 0:LANES] = columns
+            f[part, plane, pl.ds(row, SUB), LANES:WIDE] = margins
+
+    unpack(7, 0, blocks, first_ref, second_ref, put)
+    factor_ref[...] = magnetic_factor()
+
+    def step(t, carry):
+        def plane(i, carry):
+            ez = step_plane(f, factor_ref, inverse_ref, i)
+            f[2, i] = ez
+            high, low = split(ez[HALO : HALO + CZ, 0:LANES])
+            high_ref[(i - 1) // CX, t, lax.rem(i - 1, CX)] = high
+            low_ref[(i - 1) // CX, t, lax.rem(i - 1, CX)] = low
+            return carry
+
+        return lax.fori_loop(1, PLANES + 1, plane, carry)
+
+    lax.fori_loop(0, STEPS, step, 0)
+    write_back(f, (o0, o1, o2, o3))
+
+    bins = table_ref.shape[1]
+    per_tile = CX * CZ
+    rows = STEPS * per_tile
+    sums_ref[...] = jnp.zeros_like(sums_ref)
+    lists = ZT * packed_rows(7)
+    for m, block in enumerate(blocks):
+        cells = entry_row(block[lists])
+        where = jnp.where((cells // LANES) % TILES == me, cells // (LANES * TILES), -1)
+        lane_hot = one_hot(LANES, cells % LANES)
+        bin_hot = one_hot(bins, entry_row(block[lists + 1]))
+        row_ids = lax.broadcasted_iota(jnp.int32, (per_tile, ENTRIES), 0)
+        hit = row_ids == where
+        for ref in (high_ref, low_ref):
+            for t in range(STEPS):
+                values = ref[me ^ m, t].reshape(per_tile, LANES)
+                at_lane = jnp.dot(values, lane_hot, preferred_element_type=F32)
+                picked = jnp.where(hit, at_lane, 0.0).astype(BF16)
+                sums_ref[t * per_tile : (t + 1) * per_tile] += lax.dot_general(
+                    picked, bin_hot, (((1,), (1,)), ((), ())), preferred_element_type=F32
+                )
+    table_ref[...] = jnp.dot(
+        kernel_ref[...],
+        sums_ref[...],
+        precision=lax.Precision.HIGHEST,
+        preferred_element_type=F32,
+    )
+
+
+def adjoint_kernel(
+    b0, b1, b2, b3, first_ref, second_ref, inverse_ref, totals_ref, weight_ref, kernel_ref,
+    o0, o1, o2, o3,
+    f, factor_ref, drive_ref,
+):
+    me = lax.axis_index("xy")
+    even = lax.rem(lax.axis_index("gz"), 2) == 0
+    blocks = (b0, b1, b2, b3)
+    clear_edges(f)
+
+    def put(part, plane, row, columns, margins):
+        f[part, plane, pl.ds(row, SUB), 0:LANES] = columns
+        f[part, plane, pl.ds(row, SUB), LANES:WIDE] = margins
+
+    unpack(6, 2, blocks, first_ref, second_ref, put)
+    factor_ref[...] = magnetic_factor()
+
+    totals = totals_ref[...]
+    bins = totals.shape[1]
+    coefficients = normalize(totals, weight_ref[...])
+    by_bin = jnp.zeros((STEPS, bins), F32)
+    for k in range(2 * NFREQ):
+        by_bin = by_bin + kernel_ref[:, k : k + 1] * coefficients[k : k + 1, :]
+    bin_high, bin_low = split(by_bin)
+
+    def drive(ref, start, planes, z_first, z_count, row):
+        cells = entry_row(ref[start]) - 1
+        bin_hot = one_hot(bins, entry_row(ref[start + 1]))
+        columns = cells % (LANES * TILES) - me * LANES
+        inside = jnp.logical_and(columns >= -HALO, columns < LANES + HALO)
+        inside = jnp.logical_and(inside, cells >= 0)
+        lane_hot = one_hot(WIDE, jnp.where(inside, columns % WIDE, -1))
+        z = (cells // (LANES * TILES)) % CZ - z_first
+        x = cells // (LANES * TILES * CZ)
+        kept = jnp.logical_and(z >= 0, z < z_count)
+        where = jnp.where(kept, x * z_count + z, -1)
+        hit = lax.broadcasted_iota(jnp.int32, (CX * z_count, ENTRIES), 0) == where
+        amplitude = [
+            jnp.dot(part, bin_hot, preferred_element_type=F32) for part in (bin_high, bin_low)
+        ]
+        for t in range(STEPS):
+            total = jnp.zeros((CX * z_count, WIDE), F32)
+            for part in amplitude:
+                spread = jnp.where(hit, part[t : t + 1, :], 0.0).astype(BF16)
+                total = total + lax.dot_general(
+                    spread, lane_hot, (((1,), (1,)), ((), ())), preferred_element_type=F32
+                )
+            for k in range(CX):
+                drive_ref[t, planes + k, pl.ds(row, z_count), :] = total[
+                    k * z_count : (k + 1) * z_count
+                ]
+
+    size = packed_rows(6)
+    z_first = jnp.where(even, 0, HALO)
+    row_first = pl.multiple_of(jnp.where(even, HALO + CZ, 0), SUB)
+    row_second = pl.multiple_of(jnp.where(even, 0, HALO + CZ), SUB)
+    for m, block in enumerate(blocks):
+        planes = (me ^ m) * CX
+        drive(block, ZT * size, planes, 0, CZ, HALO)
+        drive(first_ref, m * (size + 2) + size, planes, z_first, HALO, row_first)
+        drive(second_ref, m * (size + 2) + size, planes, HALO - z_first, HALO, row_second)
+
+    def step(t, carry):
+        def plane(i, carry):
+            ez = step_plane(f, factor_ref, inverse_ref, i)
+            f[2, i] = ez + drive_ref[t, i - 1]
+            return carry
+
+        return lax.fori_loop(1, PLANES + 1, plane, carry)
+
+    lax.fori_loop(0, STEPS, step, 0)
+    write_back(f, (o0, o1, o2, o3))
+
+
+def spread_kernel(b0, b1, b2, b3, out_ref):
+    me = lax.axis_index("xy")
+    for m, block in enumerate((b0, b1, b2, b3)):
+        lane = pl.multiple_of((me ^ m) * LANES, LANES)
+        for part in range(6):
+            for x in range(CX):
+                for zt in range(ZT):
+                    out_ref[part, x, zt * SUB : (zt + 1) * SUB, pl.ds(lane, LANES)] = block[
+                        (part * CX + x) * ZT + zt
+                    ]
+
+
+def struct(*shape):
+    return jax.ShapeDtypeStruct(shape, F32)
+
+
+def in_vmem(count):
+    return [pl.BlockSpec(memory_space=pltpu.VMEM)] * count
+
+
+def call(kernel, args, outs, scratch=(), scalars=()):
+    specs = in_vmem(len(args))
+    for place in scalars:
+        specs[place] = pl.BlockSpec(memory_space=pltpu.SMEM)
+    single = not isinstance(outs, list)
+    return pl.pallas_call(
+        kernel,
+        out_shape=outs,
+        in_specs=specs,
+        out_specs=pl.BlockSpec(memory_space=pltpu.VMEM) if single else in_vmem(len(outs)),
+        scratch_shapes=list(scratch),
+        compiler_params=pltpu.CompilerParams(vmem_limit_bytes=48 * 1024 * 1024),
+    )(*args)
+
+
+def swap(value, axis, distance):
+    count = lax.axis_size(axis)
+    return lax.ppermute(value, axis, [(i, i ^ distance) for i in range(count)])
+
+
+def swap_blocks(blocks):
+    return [blocks[0]] + [swap(blocks[m], "xy", m) for m in range(1, TILES)]
+
+
+def swap_neighbours(first, second):
+    count = lax.axis_size("gz")
+    pairs = [(i, i ^ 1) for i in range(count) if i ^ 1 < count]
+    others = [(i, ((i + 1) ^ 1) - 1) for i in range(count)]
+    others = [(i, j) for i, j in others if 0 <= j < count]
+    return lax.ppermute(first, "gz", pairs), lax.ppermute(second, "gz", others)
+
+
+def sum_all(table):
+    for axis in ("xy", "gz"):
+        distance = 1
+        while distance < lax.axis_size(axis):
+            table = table + swap(table, axis, distance)
+            distance *= 2
+    return table
+
+
+def local_columns(
+    fields,
+    adjoint_fields,
+    material_ids,
+    material_eps,
+    monitor_cells,
+    monitor_bins,
+    source_cells,
+    source_bins,
+    bin_weight,
+):
+    bins = bin_weight.shape[0]
+    record_kernel, source_kernel = time_kernels(STEPS)
+    by_row = np.repeat(record_kernel.T, CX * CZ, axis=1)
+    lists = [
+        v.reshape(SUB, LANES) for v in (monitor_cells, monitor_bins, source_cells, source_bins)
+    ]
+    n_fwd, n_adj = packed_rows(7), packed_rows(6)
+    sent = call(
+        pack_forward_kernel,
+        (fields, material_ids, material_eps, lists[0], lists[1]),
+        [struct(ZT * n_fwd + 2, SUB, LANES)] * TILES,
+        [pltpu.VMEM((CX, CZ, TILES * LANES), F32)],
+        scalars=(2,),
+    )
+    adjoint_sent = call(
+        pack_adjoint_kernel,
+        (adjoint_fields, lists[2], lists[3]),
+        [struct(ZT * n_adj + 2, SUB, LANES)] * TILES,
+    )
+    blocks = swap_blocks(sent)
+    slabs = call(
+        functools.partial(slab_kernel, n_fwd, 0), blocks, [struct(TILES * n_fwd, SUB, LANES)] * 2
+    )
+    slabs, adjoint_sent = lax.optimization_barrier((slabs, adjoint_sent))
+    first, second = swap_neighbours(*slabs)
+    adjoint_blocks = swap_blocks(adjoint_sent)
+    (first, second), adjoint_blocks = lax.optimization_barrier(((first, second), adjoint_blocks))
+    adjoint_slabs = call(
+        functools.partial(slab_kernel, n_adj, 2),
+        adjoint_blocks,
+        [struct(TILES * (n_adj + 2), SUB, LANES)] * 2,
+    )
+    adjoint_first, adjoint_second = swap_neighbours(*adjoint_slabs)
+    field = pltpu.VMEM((6, PLANES + 2, ROWS, WIDE), F32)
+    factor = pltpu.VMEM((ROWS, WIDE), F32)
+    record = pltpu.VMEM((TILES, STEPS, CX, CZ, LANES), BF16)
+    *forward_sent, inverse, table = call(
+        forward_kernel,
+        (*blocks, first, second, by_row),
+        [struct(6 * CX * ZT, SUB, LANES)] * TILES
+        + [struct(PLANES + 2, ROWS, WIDE), struct(2 * NFREQ, bins)],
+        [field, factor, record, record, pltpu.VMEM((STEPS * CX * CZ, bins), F32)],
+    )
+    totals = sum_all(table)
+    forward_blocks = swap_blocks(forward_sent)
+    own_count = bins // (lax.axis_size("xy") * lax.axis_size("gz"))
+    device_rank = lax.axis_index(("xy", "gz"))
+    monitor_dft = lax.dynamic_slice_in_dim(totals, device_rank * own_count, own_count, axis=1)
+    adjoint_back = call(
+        adjoint_kernel,
+        (
+            *adjoint_blocks,
+            adjoint_first,
+            adjoint_second,
+            inverse,
+            totals,
+            bin_weight.reshape(1, bins),
+            source_kernel,
+        ),
+        [struct(6 * CX * ZT, SUB, LANES)] * TILES,
+        [field, factor, pltpu.VMEM((STEPS, PLANES, ROWS, WIDE), F32)],
+    )
+    forward_out = call(spread_kernel, forward_blocks, struct(*fields.shape))
+    adjoint_out = call(spread_kernel, swap_blocks(adjoint_back), struct(*fields.shape))
+    return (forward_out, adjoint_out, monitor_dft)
+
+
 def solution(mesh):
     placed = (
         P("grp", "xy", "gz", None),
@@ -174,8 +648,9 @@
         P("xy", "gz", "grp"),
         P("grp"),
     )
+    columns = mesh.shape["xy"] == TILES and mesh.shape["gz"] & (mesh.shape["gz"] - 1) == 0
     return jax.shard_map(
-        local,
+        local_columns if columns else local_general,
         mesh=mesh,
         in_specs=placed,
         out_specs=(P("grp", "xy", "gz", None), P("grp", "xy", "gz", None), P("grp", ("xy", "gz"))),

time: 467 us -> 157 us (0.34)
  starting transfers between devices: 176 us -> 25.2 us
  Pallas kernels: 0 us -> 88.5 us
  blocking collectives: 84.8 us -> 0 us
  local copies, waits for them, and re-layouts: 81.9 us -> 5.4 us
  other arithmetic: 66.8 us -> 0.01 us
  waiting for transfers between devices: 44.9 us -> 36.4 us
  between operations: 8.42 us -> 0.78 us
    ppermute x64 -> x20, starting transfers between devices: 176 us -> 25.2 us  [the longest x16 18.2 us: swap(): return lax.ppermute(value, axis, [(i, i ^ distance) for i in range(count)])]
    pallas_call x0 -> x8, Pallas kernels: none -> 88.5 us  [call(): pl.pallas_call(kernel, out_shape=outs, in_specs=specs, out_specs=pl.Block...]
    gather x9 -> x0, local copies, waits for them, and re-layouts: 56.4 us -> none  [the longest x8 53.6 us: local(): records.append(electric[2].reshape(-1)[watched])]
    unnamed x1 -> x0, blocking collectives: 55.7 us -> none
    scatter-add x9 -> x0, other arithmetic: 55.2 us -> none  [the longest x8 49.1 us: local(): driven = electric[2].reshape(-1).at[targets].add(amplitudes[step_index])....]
    all_gather x1 -> x0, blocking collectives: 29 us -> none  [local(): lax.all_gather(normalize(monitor_dft, own_weight), ('xy', 'gz'), axis=1,...]
    slice x236 -> x0, local copies, waits for them, and re-layouts: 9.35 us -> none  [the longest x101 5.66 us: forward_diff(): lax.slice_in_dim(values, 1, values.shape[along], axis=along)]
    ppermute x64 -> x20, waiting for transfers between devices: 44.9 us -> 36.4 us  [the longest x16 36.4 us: swap(): return lax.ppermute(value, axis, [(i, i ^ distance) for i in range(count)])]
  transfers between devices with their start and end apart: 64 -> 20, of which waited for: 27 -> 9; matrix products, arithmetic and copies ran while one was open for 14% -> 0% of each run, Pallas kernels for 0% -> 55%
where the time goes in v1:
time: 157 us; the launch traced here: 156 us
  Pallas kernels  88.5 us (56%)
  waiting for transfers between devices  36.4 us (23%)
  starting transfers between devices  25.2 us (16%)
  local copies, waits for them, and re-layouts  5.4 us (3%)
    pallas_call x8, Pallas kernels, call(): pl.pallas_call(kernel, out_shape=outs, in_specs=specs, out_specs=pl.Block...  88.5 us
    ppermute x16, waiting for transfers between devices, swap(): return lax.ppermute(value, axis, [(i, i ^ distance) for i in range(count)])  36.4 us
    ppermute x16, starting transfers between devices, swap(): return lax.ppermute(value, axis, [(i, i ^ distance) for i in range(count)])  18.2 us
    ppermute x2, starting transfers between devices, swap_neighbours(): lax.ppermute(first, 'gz', pairs)  5.72 us
    unnamed x22, local copies, waits for them, and re-layouts  4.74 us
  transfers between devices with their start and end apart: 20, of which 9 were waited for; matrix products, arithmetic and copies ran while one was open for 0% of the time, Pallas kernels for 55%

profile of v1, /device:TPU:1, one launch (start us, length us, event | category | flops | bytes accessed | tf_op | source)
XLA Modules:
  0.0 156.3 jit_solution(15743490707992955918)
XLA Ops:
  1.3 1.1 copy-done
  5.9 2.7 %collective-permute-start.1 = (f32[66,8,128]{2,1,0:T(8,128)S(1)}, f32[66,8,128]{2,1,0:T(8,128)S(1)}, u32[]{:S(2)}, u32[]{:S(2)}) collective-permute-start(f32[66,8,128]{2,1,0:T(8,128)S(1)} %get-tuple-element.39), channel_id=1, source_target_pairs={{0,8},{4,12},{8,0},{12,4},{1,9},{5,13},{9,1},{13,5},{2,10},{6,14},... | collective-permute-start | bytes 811016 | tf_op jit(solution)/shard_map/ppermute | solution.py:537
  9.0 6.3 %collective-permute-done.1.b2 = f32[66,8,128]{2,1,0:T(8,128)S(1)} collective-permute-done((f32[66,8,128]{2,1,0:T(8,128)S(1)}, f32[66,8,128]{2,1,0:T(8,128)S(1)}, u32[]{:S(2)}, u32[]{:S(2)}) %collective-permute-start.1) | collective-permute-done | bytes 270368 | tf_op jit(solution)/shard_map/ppermute | solution.py:537
  15.3 5.8 %collective-permute-done.2.b3 = f32[66,8,128]{2,1,0:T(8,128)S(1)} collective-permute-done((f32[66,8,128]{2,1,0:T(8,128)S(1)}, f32[66,8,128]{2,1,0:T(8,128)S(1)}, u32[]{:S(2)}, u32[]{:S(2)}) %collective-permute-start.2) | collective-permute-done | bytes 270368 | tf_op jit(solution)/shard_map/ppermute | solution.py:537
  21.2 1.6 %collective-permute-start.3 = (f32[128,8,128]{2,1,0:T(8,128)S(1)}, f32[128,8,128]{2,1,0:T(8,128)S(1)}, u32[]{:S(2)}, u32[]{:S(2)}) collective-permute-start(f32[128,8,128]{2,1,0:T(8,128)S(1)} %get-tuple-element.47), channel_id=1, source_target_pairs={{0,1},{1,0},{2,3},{3,2},{4,5},{5,4},{6,7},{7,6},{8,9},{9,8},{10,11... | collective-permute-start | bytes 1572872 | tf_op jit(solution)/shard_map/ppermute | solution.py:549
  24.0 1.3 collective-permute-start.6
  25.7 5.5 %collective-permute-done.6.b2 = f32[56,8,128]{2,1,0:T(8,128)S(1)} collective-permute-done((f32[56,8,128]{2,1,0:T(8,128)S(1)}, f32[56,8,128]{2,1,0:T(8,128)S(1)}, u32[]{:S(2)}, u32[]{:S(2)}) %collective-permute-start.6) | collective-permute-done | bytes 229408 | tf_op jit(solution)/shard_map/ppermute | solution.py:537
  31.2 5.1 %collective-permute-done.7.b3 = f32[56,8,128]{2,1,0:T(8,128)S(1)} collective-permute-done((f32[56,8,128]{2,1,0:T(8,128)S(1)}, f32[56,8,128]{2,1,0:T(8,128)S(1)}, u32[]{:S(2)}, u32[]{:S(2)}) %collective-permute-start.7) | collective-permute-done | bytes 229408 | tf_op jit(solution)/shard_map/ppermute | solution.py:537
  36.4 4.2 %collective-permute-start.11 = (f32[116,8,128]{2,1,0:T(8,128)S(1)}, f32[116,8,128]{2,1,0:T(8,128)S(1)}, u32[]{:S(2)}, u32[]{:S(2)}) collective-permute-start(f32[116,8,128]{2,1,0:T(8,128)S(1)} %get-tuple-element.63), channel_id=1, source_target_pairs={{0,1},{1,0},{2,3},{3,2},{4,5},{5,4},{6,7},{7,6},{8,9},{9,8},{10,11... | collective-permute-start | bytes 1425416 | tf_op jit(solution)/shard_map/ppermute | solution.py:549
  41.2 31.9 %shard_map.133 = (f32[48,8,128]{2,1,0:T(8,128)S(1)}, f32[48,8,128]{2,1,0:T(8,128)S(1)}, f32[48,8,128]{2,1,0:T(8,128)S(1)}, f32[48,8,128]{2,1,0:T(8,128)S(1)}, f3...) custom-call(f32[66,8,128]{2,1,0:T(8,128)S(1)} %get-tuple-element.37.b0, f32[66,8,128]{2,1,0:T(8,128)S(1)} %collective-permute-done.b1, ...), custom_call_target="tpu_custom_call" | custom-call | tf_op jit(solution)/shard_map/pallas_call | solution.py:525
  73.1 1.7 %collective-permute-start.10 = (f32[48,8,128]{2,1,0:T(8,128)S(1)}, f32[48,8,128]{2,1,0:T(8,128)S(1)}, u32[]{:S(2)}, u32[]{:S(2)}) collective-permute-start(f32[48,8,128]{2,1,0:T(8,128)S(1)} %get-tuple-element.58), channel_id=1, source_target_pairs={{0,12},{4,8},{8,4},{12,0},{1,13},{5,9},{9,5},{13,1},{2,14},{6,10},... | collective-permute-start | bytes 589832 | tf_op jit(solution)/shard_map/ppermute | solution.py:537
  74.8 1.2 collective-permute-done.13
  76.2 4.1 %collective-permute-done.14 = f32[8,128]{1,0:T(8,128)S(1)} collective-permute-done((f32[8,128]{1,0:T(8,128)S(1)}, f32[8,128]{1,0:T(8,128)S(1)}, u32[]{:S(2)}, u32[]{:S(2)}) %collective-permute-start.14) | collective-permute-done | bytes 4128 | tf_op jit(solution)/shard_map/ppermute | solution.py:537
  80.3 2.3 %collective-permute-start.15 = (f32[8,128]{1,0:T(8,128)S(1)}, f32[8,128]{1,0:T(8,128)S(1)}, u32[]{:S(2)}, u32[]{:S(2)}) collective-permute-start(f32[8,128]{1,0:T(8,128)S(1)} %add.19), channel_id=1, source_target_pairs={{0,1},{1,0},{2,3},{3,2},{4,5},{5,4},{6,7},{7,6},{8,9},{9,8},{10,11... | collective-permute-start | bytes 12296 | tf_op jit(solution)/shard_map/ppermute | solution.py:537
  83.6 1.6 %collective-permute-start.16 = (f32[8,128]{1,0:T(8,128)S(1)}, f32[8,128]{1,0:T(8,128)S(1)}, u32[]{:S(2)}, u32[]{:S(2)}) collective-permute-start(f32[8,128]{1,0:T(8,128)S(1)} %add.20), channel_id=1, source_target_pairs={{0,2},{1,3},{2,0},{3,1},{4,6},{5,7},{6,4},{7,5},{8,10},{9,11},{10,... | collective-permute-start | bytes 12296 | tf_op jit(solution)/shard_map/ppermute | solution.py:537
  85.2 2.1 %collective-permute-start.8 = (f32[48,8,128]{2,1,0:T(8,128)S(1)}, f32[48,8,128]{2,1,0:T(8,128)S(1)}, u32[]{:S(2)}, u32[]{:S(2)}) collective-permute-start(f32[48,8,128]{2,1,0:T(8,128)S(1)} %get-tuple-element.56), channel_id=1, source_target_pairs={{0,4},{4,0},{8,12},{12,8},{1,5},{5,1},{9,13},{13,9},{2,6},{6,2},{1... | collective-permute-start | bytes 589832 | tf_op jit(solution)/shard_map/ppermute | solution.py:537
  87.3 1.2 collective-permute-start.9
  89.3 53.0 %shard_map.136 = (f32[48,8,128]{2,1,0:T(8,128)S(1)}, f32[48,8,128]{2,1,0:T(8,128)S(1)}, f32[48,8,128]{2,1,0:T(8,128)S(1)}, f32[48,8,128]{2,1,0:T(8,128)S(1)}) custom-call(f32[56,8,128]{2,1,0:T(8,128)S(1)} %get-tuple-element.59.b0, f32[56,8,128]{2,1,0:T(8,128)S(1)} %collective-permute-done.5.b1, f32[56,8,128]{2,1,0:T(8,128)S(1)} %collective-permute-done.6.b2, ...), custom_call_target="tpu_custom_call" | custom-call | tf_op jit(solution)/shard_map/pallas_call | solution.py:525
  142.3 2.1 %collective-permute-start.17 = (f32[48,8,128]{2,1,0:T(8,128)S(1)}, f32[48,8,128]{2,1,0:T(8,128)S(1)}, u32[]{:S(2)}, u32[]{:S(2)}) collective-permute-start(f32[48,8,128]{2,1,0:T(8,128)S(1)} %get-tuple-element.68), channel_id=1, source_target_pairs={{0,4},{4,0},{8,12},{12,8},{1,5},{5,1},{9,13},{13,9},{2,6},{6,2},{1... | collective-permute-start | bytes 589832 | tf_op jit(solution)/shard_map/ppermute | solution.py:537
  145.1 1.0 collective-permute-start.19
  146.8 1.0 shard_map.134
  147.8 3.1 %collective-permute-done.18.b2 = f32[48,8,128]{2,1,0:T(8,128)S(1)} collective-permute-done((f32[48,8,128]{2,1,0:T(8,128)S(1)}, f32[48,8,128]{2,1,0:T(8,128)S(1)}, u32[]{:S(2)}, u32[]{:S(2)}) %collective-permute-start.18) | collective-permute-done | bytes 196640 | tf_op jit(solution)/shard_map/ppermute | solution.py:537
  150.9 4.4 %collective-permute-done.19.b3 = f32[48,8,128]{2,1,0:T(8,128)S(1)} collective-permute-done((f32[48,8,128]{2,1,0:T(8,128)S(1)}, f32[48,8,128]{2,1,0:T(8,128)S(1)}, u32[]{:S(2)}, u32[]{:S(2)}) %collective-permute-start.19) | collective-permute-done | bytes 196640 | tf_op jit(solution)/shard_map/ppermute | solution.py:537
  155.3 1.0 shard_map.137
  (51 shorter events, 10.3 us)
Async XLA Ops:
  4.7 3.9 %copy-start.1 = (f32[6,4,16,512]{3,2,1,0:T(8,128)S(1)}, f32[6,4,16,512]{3,2,1,0:T(8,128)}, u32[]{:S(2)}) copy-start(f32[6,4,16,512]{3,2,1,0:T(8,128)} %fields_ref.3) | copy-start | bytes 2359300
  5.7 2.9 %copy-start.7 = (s32[1,1,1024]{2,1,0:T(1,128)S(1)}, s32[1,1,1024]{2,1,0:T(1,128)}, u32[]{:S(2)}) copy-start(s32[1,1,1024]{2,1,0:T(1,128)} %param.18) | copy-start | bytes 12292
  5.7 2.9 %copy-start.6 = (s32[1,1,1024]{2,1,0:T(1,128)S(1)}, s32[1,1,1024]{2,1,0:T(1,128)}, u32[]{:S(2)}) copy-start(s32[1,1,1024]{2,1,0:T(1,128)} %param.17) | copy-start | bytes 12292
  5.7 3.3 %collective-permute-start = (f32[66,8,128]{2,1,0:T(8,128)S(1)}, f32[66,8,128]{2,1,0:T(8,128)S(1)}, u32[]{:S(2)}, u32[]{:S(2)}) collective-permute-start(f32[66,8,128]{2,1,0:T(8,128)S(1)} %get-tuple-element.38), channel_id=1, source_target_pairs={{0,4},{4,0},{8,12},{12,8},{1,5},{5,1},{9,13},{13,9},{2,6},{6,2},{1... | collective-permute-start | bytes 811016 | tf_op jit(solution)/shard_map/ppermute | solution.py:537
  5.9 9.5 %collective-permute-start.1 = (f32[66,8,128]{2,1,0:T(8,128)S(1)}, f32[66,8,128]{2,1,0:T(8,128)S(1)}, u32[]{:S(2)}, u32[]{:S(2)}) collective-permute-start(f32[66,8,128]{2,1,0:T(8,128)S(1)} %get-tuple-element.39), channel_id=1, source_target_pairs={{0,8},{4,12},{8,0},{12,4},{1,9},{5,13},{9,1},{13,5},{2,10},{6,14},... | collective-permute-start | bytes 811016 | tf_op jit(solution)/shard_map/ppermute | solution.py:537
  8.6 12.6 %collective-permute-start.2 = (f32[66,8,128]{2,1,0:T(8,128)S(1)}, f32[66,8,128]{2,1,0:T(8,128)S(1)}, u32[]{:S(2)}, u32[]{:S(2)}) collective-permute-start(f32[66,8,128]{2,1,0:T(8,128)S(1)} %get-tuple-element.40), channel_id=1, source_target_pairs={{0,12},{4,8},{8,4},{12,0},{1,13},{5,9},{9,5},{13,1},{2,14},{6,10},... | collective-permute-start | bytes 811016 | tf_op jit(solution)/shard_map/ppermute | solution.py:537
  21.2 20.0 %copy-start.3 = (f32[8,512]{1,0:T(8,128)S(1)}, f32[8,512]{1,0:T(8,128)}, u32[]{:S(2)}) copy-start(f32[8,512]{1,0:T(8,128)} %constant.19.clone.kernel_ref) | copy-start | bytes 49156
  21.2 15.1 %collective-permute-start.3 = (f32[128,8,128]{2,1,0:T(8,128)S(1)}, f32[128,8,128]{2,1,0:T(8,128)S(1)}, u32[]{:S(2)}, u32[]{:S(2)}) collective-permute-start(f32[128,8,128]{2,1,0:T(8,128)S(1)} %get-tuple-element.47), channel_id=1, source_target_pairs={{0,1},{1,0},{2,3},{3,2},{4,5},{5,4},{6,7},{7,6},{8,9},{9,8},{10,11... | collective-permute-start | bytes 1572872 | tf_op jit(solution)/shard_map/ppermute | solution.py:549
  22.8 13.5 %collective-permute-start.4 = (f32[128,8,128]{2,1,0:T(8,128)S(1)}, f32[128,8,128]{2,1,0:T(8,128)S(1)}, u32[]{:S(2)}, u32[]{:S(2)}) collective-permute-start(f32[128,8,128]{2,1,0:T(8,128)S(1)} %get-tuple-element.48), channel_id=1, source_target_pairs={{1,2},{2,1},{5,6},{6,5},{9,10},{10,9},{13,14},{14,13},{17,18},{18,... | collective-permute-start | bytes 1572872 | tf_op jit(solution)/shard_map/ppermute | solution.py:549
  23.5 2.3 %collective-permute-start.5 = (f32[56,8,128]{2,1,0:T(8,128)S(1)}, f32[56,8,128]{2,1,0:T(8,128)S(1)}, u32[]{:S(2)}, u32[]{:S(2)}) collective-permute-start(f32[56,8,128]{2,1,0:T(8,128)S(1)} %get-tuple-element.50), channel_id=1, source_target_pairs={{0,4},{4,0},{8,12},{12,8},{1,5},{5,1},{9,13},{13,9},{2,6},{6,2},{1... | collective-permute-start | bytes 688136 | tf_op jit(solution)/shard_map/ppermute | solution.py:537
  24.0 7.2 %collective-permute-start.6 = (f32[56,8,128]{2,1,0:T(8,128)S(1)}, f32[56,8,128]{2,1,0:T(8,128)S(1)}, u32[]{:S(2)}, u32[]{:S(2)}) collective-permute-start(f32[56,8,128]{2,1,0:T(8,128)S(1)} %get-tuple-element.51), channel_id=1, source_target_pairs={{0,8},{4,12},{8,0},{12,4},{1,9},{5,13},{9,1},{13,5},{2,10},{6,14},... | collective-permute-start | bytes 688136 | tf_op jit(solution)/shard_map/ppermute | solution.py:537
  25.3 11.0 %collective-permute-start.7 = (f32[56,8,128]{2,1,0:T(8,128)S(1)}, f32[56,8,128]{2,1,0:T(8,128)S(1)}, u32[]{:S(2)}, u32[]{:S(2)}) collective-permute-start(f32[56,8,128]{2,1,0:T(8,128)S(1)} %get-tuple-element.52), channel_id=1, source_target_pairs={{0,12},{4,8},{8,4},{12,0},{1,13},{5,9},{9,5},{13,1},{2,14},{6,10},... | collective-permute-start | bytes 688136 | tf_op jit(solution)/shard_map/ppermute | solution.py:537
  36.4 52.2 %collective-permute-start.11 = (f32[116,8,128]{2,1,0:T(8,128)S(1)}, f32[116,8,128]{2,1,0:T(8,128)S(1)}, u32[]{:S(2)}, u32[]{:S(2)}) collective-permute-start(f32[116,8,128]{2,1,0:T(8,128)S(1)} %get-tuple-element.63), channel_id=1, source_target_pairs={{0,1},{1,0},{2,3},{3,2},{4,5},{5,4},{6,7},{7,6},{8,9},{9,8},{10,11... | collective-permute-start | bytes 1425416 | tf_op jit(solution)/shard_map/ppermute | solution.py:549
  40.5 48.1 %collective-permute-start.12 = (f32[116,8,128]{2,1,0:T(8,128)S(1)}, f32[116,8,128]{2,1,0:T(8,128)S(1)}, u32[]{:S(2)}, u32[]{:S(2)}) collective-permute-start(f32[116,8,128]{2,1,0:T(8,128)S(1)} %get-tuple-element.64), channel_id=1, source_target_pairs={{1,2},{2,1},{5,6},{6,5},{9,10},{10,9},{13,14},{14,13},{17,18},{18,... | collective-permute-start | bytes 1425416 | tf_op jit(solution)/shard_map/ppermute | solution.py:549
  73.1 72.0 %collective-permute-start.10 = (f32[48,8,128]{2,1,0:T(8,128)S(1)}, f32[48,8,128]{2,1,0:T(8,128)S(1)}, u32[]{:S(2)}, u32[]{:S(2)}) collective-permute-start(f32[48,8,128]{2,1,0:T(8,128)S(1)} %get-tuple-element.58), channel_id=1, source_target_pairs={{0,12},{4,8},{8,4},{12,0},{1,13},{5,9},{9,5},{13,1},{2,14},{6,10},... | collective-permute-start | bytes 589832 | tf_op jit(solution)/shard_map/ppermute | solution.py:537
  74.8 1.2 collective-permute-start.13
  76.0 4.3 %collective-permute-start.14 = (f32[8,128]{1,0:T(8,128)S(1)}, f32[8,128]{1,0:T(8,128)S(1)}, u32[]{:S(2)}, u32[]{:S(2)}) collective-permute-start(f32[8,128]{1,0:T(8,128)S(1)} %add.18), channel_id=1, source_target_pairs={{0,8},{4,12},{8,0},{12,4},{1,9},{5,13},{9,1},{13,5},{2,10},{6,14},... | collective-permute-start | bytes 12296 | tf_op jit(solution)/shard_map/ppermute | solution.py:537
  80.3 3.3 %collective-permute-start.15 = (f32[8,128]{1,0:T(8,128)S(1)}, f32[8,128]{1,0:T(8,128)S(1)}, u32[]{:S(2)}, u32[]{:S(2)}) collective-permute-start(f32[8,128]{1,0:T(8,128)S(1)} %add.19), channel_id=1, source_target_pairs={{0,1},{1,0},{2,3},{3,2},{4,5},{5,4},{6,7},{7,6},{8,9},{9,8},{10,11... | collective-permute-start | bytes 12296 | tf_op jit(solution)/shard_map/ppermute | solution.py:537
  83.6 3.7 %collective-permute-start.16 = (f32[8,128]{1,0:T(8,128)S(1)}, f32[8,128]{1,0:T(8,128)S(1)}, u32[]{:S(2)}, u32[]{:S(2)}) collective-permute-start(f32[8,128]{1,0:T(8,128)S(1)} %add.20), channel_id=1, source_target_pairs={{0,2},{1,3},{2,0},{3,1},{4,6},{5,7},{6,4},{7,5},{8,10},{9,11},{10,... | collective-permute-start | bytes 12296 | tf_op jit(solution)/shard_map/ppermute | solution.py:537
  85.2 61.6 %collective-permute-start.8 = (f32[48,8,128]{2,1,0:T(8,128)S(1)}, f32[48,8,128]{2,1,0:T(8,128)S(1)}, u32[]{:S(2)}, u32[]{:S(2)}) collective-permute-start(f32[48,8,128]{2,1,0:T(8,128)S(1)} %get-tuple-element.56), channel_id=1, source_target_pairs={{0,4},{4,0},{8,12},{12,8},{1,5},{5,1},{9,13},{13,9},{2,6},{6,2},{1... | collective-permute-start | bytes 589832 | tf_op jit(solution)/shard_map/ppermute | solution.py:537
  87.3 59.5 %collective-permute-start.9 = (f32[48,8,128]{2,1,0:T(8,128)S(1)}, f32[48,8,128]{2,1,0:T(8,128)S(1)}, u32[]{:S(2)}, u32[]{:S(2)}) collective-permute-start(f32[48,8,128]{2,1,0:T(8,128)S(1)} %get-tuple-element.57), channel_id=1, source_target_pairs={{0,8},{4,12},{8,0},{12,4},{1,9},{5,13},{9,1},{13,5},{2,10},{6,14},... | collective-permute-start | bytes 589832 | tf_op jit(solution)/shard_map/ppermute | solution.py:537
  142.3 5.5 %collective-permute-start.17 = (f32[48,8,128]{2,1,0:T(8,128)S(1)}, f32[48,8,128]{2,1,0:T(8,128)S(1)}, u32[]{:S(2)}, u32[]{:S(2)}) collective-permute-start(f32[48,8,128]{2,1,0:T(8,128)S(1)} %get-tuple-element.68), channel_id=1, source_target_pairs={{0,4},{4,0},{8,12},{12,8},{1,5},{5,1},{9,13},{13,9},{2,6},{6,2},{1... | collective-permute-start | bytes 589832 | tf_op jit(solution)/shard_map/ppermute | solution.py:537
  144.4 6.5 %collective-permute-start.18 = (f32[48,8,128]{2,1,0:T(8,128)S(1)}, f32[48,8,128]{2,1,0:T(8,128)S(1)}, u32[]{:S(2)}, u32[]{:S(2)}) collective-permute-start(f32[48,8,128]{2,1,0:T(8,128)S(1)} %get-tuple-element.69), channel_id=1, source_target_pairs={{0,8},{4,12},{8,0},{12,4},{1,9},{5,13},{9,1},{13,5},{2,10},{6,14},... | collective-permute-start | bytes 589832 | tf_op jit(solution)/shard_map/ppermute | solution.py:537
  145.1 10.2 %collective-permute-start.19 = (f32[48,8,128]{2,1,0:T(8,128)S(1)}, f32[48,8,128]{2,1,0:T(8,128)S(1)}, u32[]{:S(2)}, u32[]{:S(2)}) collective-permute-start(f32[48,8,128]{2,1,0:T(8,128)S(1)} %get-tuple-element.70), channel_id=1, source_target_pairs={{0,12},{4,8},{8,4},{12,0},{1,13},{5,9},{9,5},{13,1},{2,14},{6,10},... | collective-permute-start | bytes 589832 | tf_op jit(solution)/shard_map/ppermute | solution.py:537
  (7 other events, 5.4 us)

commit v2 on v1

--- a/solution.py
+++ b/solution.py
@@ -161,9 +161,12 @@
 LANES = 128
 HALO = 8
 ROWS = CZ + 2 * HALO
+PAD = 8
+GROUP = 2
 WIDE = 2 * LANES
 PLANES = TILES * CX
 ENTRIES = 1024
+CHUNK = 256
 SUB = 8
 ZT = CZ // SUB
 BF16 = jnp.bfloat16
@@ -291,41 +294,89 @@
 
 
 def magnetic_factor():
-    rows = lax.broadcasted_iota(jnp.int32, (ROWS, WIDE), 0)
-    lanes = lax.broadcasted_iota(jnp.int32, (ROWS, WIDE), 1)
+    halves = lax.broadcasted_iota(jnp.int32, (2, ROWS, LANES), 0)
+    rows = lax.broadcasted_iota(jnp.int32, (2, ROWS, LANES), 1)
+    lanes = lax.broadcasted_iota(jnp.int32, (2, ROWS, LANES), 2)
     below_z = jnp.logical_and(rows < HALO, lax.axis_index("gz") == 0)
-    below_y = jnp.logical_and(lanes >= WIDE - 2 * HALO, lax.axis_index("xy") == 0)
+    below_y = jnp.logical_and(halves == 1, lanes >= LANES - HALO)
+    below_y = jnp.logical_and(below_y, lax.axis_index("xy") == 0)
     return jnp.where(jnp.logical_or(below_z, below_y), 0.0, STEP_RATIO)
 
 
-def step_plane(f, factor_ref, inverse_ref, i):
-    def z_up(v):
-        return pltpu.roll(v, ROWS - 1, 0)
-
-    def z_down(v):
-        return pltpu.roll(v, 1, 0)
-
-    def y_up(v):
-        return pltpu.roll(v, WIDE - 1, 1)
-
-    def y_down(v):
-        return pltpu.roll(v, 1, 1)
-
-    factor = factor_ref[...]
-    ex, ey, ez = f[0, i], f[1, i], f[2, i]
-    hx = f[3, i] - factor * ((y_up(ez) - ez) - (z_up(ey) - ey))
-    hy = f[4, i] - factor * ((z_up(ex) - ex) - (f[2, i + 1] - ez))
-    hz = f[5, i] - factor * ((f[1, i + 1] - ey) - (y_up(ex) - ex))
-    f[3, i] = hx
-    f[4, i] = hy
-    f[5, i] = hz
-    inverse = inverse_ref[i]
-    ex = ex + inverse * ((hz - y_down(hz)) - (hy - z_down(hy)))
-    ey = ey + inverse * ((hx - z_down(hx)) - (hz - f[5, i - 1]))
-    ez = ez + inverse * ((hy - f[4, i - 1]) - (hx - y_down(hx)))
-    f[0, i] = ex
-    f[1, i] = ey
-    return ez
+def y_up(v):
+    moved = pltpu.roll(v, LANES - 1, 2)
+    other = jnp.concatenate([moved[1:], moved[:1]], axis=0)
+    lanes = lax.broadcasted_iota(jnp.int32, v.shape, 2)
+    return jnp.where(lanes == LANES - 1, other, moved)
+
+
+def y_down(v):
+    moved = pltpu.roll(v, 1, 2)
+    other = jnp.concatenate([moved[1:], moved[:1]], axis=0)
+    lanes = lax.broadcasted_iota(jnp.int32, v.shape, 2)
+    return jnp.where(lanes == 0, other, moved)
+
+
+def magnetic_planes(f, factor, i):
+    rows, above = pl.ds(PAD, ROWS), pl.ds(PAD + 1, ROWS)
+    ey = [f[1, i + k, :, rows, :] for k in range(GROUP + 1)]
+    ez = [f[2, i + k, :, rows, :] for k in range(GROUP + 1)]
+    done = []
+    for k in range(GROUP):
+        ex, ex_up = f[0, i + k, :, rows, :], f[0, i + k, :, above, :]
+        ey_up = f[1, i + k, :, above, :]
+        hx = f[3, i + k, :, rows, :] - factor * ((y_up(ez[k]) - ez[k]) - (ey_up - ey[k]))
+        hy = f[4, i + k, :, rows, :] - factor * ((ex_up - ex) - (ez[k + 1] - ez[k]))
+        hz = f[5, i + k, :, rows, :] - factor * ((ey[k + 1] - ey[k]) - (y_up(ex) - ex))
+        done.append((hx, hy, hz))
+    return done
+
+
+def electric_planes(f, inverse_ref, i):
+    rows, below = pl.ds(PAD, ROWS), pl.ds(PAD - 1, ROWS)
+    hy = [f[4, i - 1 + k, :, rows, :] for k in range(GROUP + 1)]
+    hz = [f[5, i - 1 + k, :, rows, :] for k in range(GROUP + 1)]
+    done = []
+    for k in range(GROUP):
+        hx, hx_down = f[3, i + k, :, rows, :], f[3, i + k, :, below, :]
+        hy_down = f[4, i + k, :, below, :]
+        y, z = hy[k + 1], hz[k + 1]
+        inverse = inverse_ref[i + k]
+        ex = f[0, i + k, :, rows, :] + inverse * ((z - y_down(z)) - (y - hy_down))
+        ey = f[1, i + k, :, rows, :] + inverse * ((hx - hx_down) - (z - hz[k]))
+        ez = f[2, i + k, :, rows, :] + inverse * ((y - hy[k]) - (hx - y_down(hx)))
+        done.append((ex, ey, ez))
+    return done
+
+
+def run_steps(f, factor_ref, inverse_ref, finish):
+    groups = PLANES // GROUP
+    rows = pl.ds(PAD, ROWS)
+
+    def keep_magnetic(i, done):
+        for k, fields in enumerate(done):
+            for part, value in enumerate(fields):
+                f[3 + part, i + k, :, rows, :] = value
+
+    def keep_electric(t, i, done):
+        for k, (ex, ey, ez) in enumerate(done):
+            f[0, i + k, :, rows, :] = ex
+            f[1, i + k, :, rows, :] = ey
+            f[2, i + k, :, rows, :] = finish(t, i + k, ez)
+
+    def body(n, carry):
+        i = 1 + lax.rem(n, groups) * GROUP
+        j = 1 + lax.rem(n - 1, groups) * GROUP
+        magnetic = magnetic_planes(f, factor_ref[...], i)
+        electric = electric_planes(f, inverse_ref, j)
+        keep_magnetic(i, magnetic)
+        keep_electric((n - 1) // groups, j, electric)
+        return carry
+
+    keep_magnetic(1, magnetic_planes(f, factor_ref[...], 1))
+    lax.fori_loop(1, STEPS * groups, body, 0)
+    last = PLANES - GROUP + 1
+    keep_electric(STEPS - 1, last, electric_planes(f, inverse_ref, last))
 
 
 def entry_row(vector):
@@ -351,75 +402,85 @@
             for x in range(CX):
                 for zt in range(ZT):
                     out[(part * CX + x) * ZT + zt] = f[
-                        part, base + x, HALO + zt * SUB : HALO + (zt + 1) * SUB, 0:LANES
+                        part, base + x, 0, pl.ds(PAD + HALO + zt * SUB, SUB), :
                     ]
 
 
 def clear_edges(f):
     for part in range(6):
-        f[part, 0] = jnp.zeros((ROWS, WIDE), F32)
-        f[part, PLANES + 1] = jnp.zeros((ROWS, WIDE), F32)
+        for plane in (0, PLANES + 1):
+            f[part, plane] = jnp.zeros(f.shape[2:], F32)
+        for start in (0, PAD + ROWS):
+            f[part, :, :, pl.ds(start, PAD), :] = jnp.zeros((PLANES + 2, 2, PAD, LANES), F32)
+
+
+def field_put(f):
+    def put(part, plane, row, columns, margins):
+        rows = pl.ds(pl.multiple_of(PAD + row, SUB), SUB)
+        f[part, plane, 0, rows, :] = columns
+        f[part, plane, 1, rows, :] = margins
+
+    return put
 
 
 def forward_kernel(
     b0, b1, b2, b3, first_ref, second_ref, kernel_ref,
     o0, o1, o2, o3, inverse_ref, table_ref,
-    f, factor_ref, high_ref, low_ref, sums_ref,
+    f, factor_ref, record_ref, picked_ref,
 ):
     me = lax.axis_index("xy")
     blocks = (b0, b1, b2, b3)
     clear_edges(f)
+    put_field = field_put(f)
 
     def put(part, plane, row, columns, margins):
         if part == 6:
-            inverse_ref[plane, pl.ds(row, SUB), 0:LANES] = columns
-            inverse_ref[plane, pl.ds(row, SUB), LANES:WIDE] = margins
+            inverse_ref[plane, 0, pl.ds(row, SUB), :] = columns
+            inverse_ref[plane, 1, pl.ds(row, SUB), :] = margins
         else:
-            f[part, plane, pl.ds(row, SUB), 0:LANES] = columns
-            f[part, plane, pl.ds(row, SUB), LANES:WIDE] = margins
+            put_field(part, plane, row, columns, margins)
 
     unpack(7, 0, blocks, first_ref, second_ref, put)
     factor_ref[...] = magnetic_factor()
 
-    def step(t, carry):
-        def plane(i, carry):
-            ez = step_plane(f, factor_ref, inverse_ref, i)
-            f[2, i] = ez
-            high, low = split(ez[HALO : HALO + CZ, 0:LANES])
-            high_ref[(i - 1) // CX, t, lax.rem(i - 1, CX)] = high
-            low_ref[(i - 1) // CX, t, lax.rem(i - 1, CX)] = low
-            return carry
-
-        return lax.fori_loop(1, PLANES + 1, plane, carry)
-
-    lax.fori_loop(0, STEPS, step, 0)
+    def finish(t, i, ez):
+        x = i - 1
+        for part, value in enumerate(split(ez[0, HALO : HALO + CZ])):
+            record_ref[x // CX, part, t, lax.rem(x, CX)] = value
+        return ez
+
+    run_steps(f, factor_ref, inverse_ref, finish)
     write_back(f, (o0, o1, o2, o3))
 
     bins = table_ref.shape[1]
     per_tile = CX * CZ
-    rows = STEPS * per_tile
-    sums_ref[...] = jnp.zeros_like(sums_ref)
+    copies = 2 * STEPS
     lists = ZT * packed_rows(7)
+    bin_hots = []
     for m, block in enumerate(blocks):
         cells = entry_row(block[lists])
         where = jnp.where((cells // LANES) % TILES == me, cells // (LANES * TILES), -1)
-        lane_hot = one_hot(LANES, cells % LANES)
-        bin_hot = one_hot(bins, entry_row(block[lists + 1]))
-        row_ids = lax.broadcasted_iota(jnp.int32, (per_tile, ENTRIES), 0)
-        hit = row_ids == where
-        for ref in (high_ref, low_ref):
-            for t in range(STEPS):
-                values = ref[me ^ m, t].reshape(per_tile, LANES)
-                at_lane = jnp.dot(values, lane_hot, preferred_element_type=F32)
-                picked = jnp.where(hit, at_lane, 0.0).astype(BF16)
-                sums_ref[t * per_tile : (t + 1) * per_tile] += lax.dot_general(
-                    picked, bin_hot, (((1,), (1,)), ((), ())), preferred_element_type=F32
-                )
+        bin_hots.append(one_hot(bins, entry_row(block[lists + 1])))
+        values = record_ref[me ^ m].reshape(copies * per_tile, LANES)
+        for start in range(0, ENTRIES, CHUNK):
+            span = slice(start, start + CHUNK)
+            lane_hot = one_hot(LANES, cells[:, span] % LANES)
+            row_ids = lax.broadcasted_iota(jnp.int32, (per_tile, CHUNK), 0)
+            hit = row_ids == where[:, span]
+            at_lane = jnp.dot(values, lane_hot, preferred_element_type=F32)
+            at_lane = at_lane.reshape(copies, per_tile, CHUNK)
+            picked = jnp.where(hit[None], at_lane, 0.0).astype(BF16)
+            picked_ref[:, m * ENTRIES + start : m * ENTRIES + start + CHUNK] = picked.reshape(
+                copies * per_tile, CHUNK
+            )
+    sums = lax.dot_general(
+        picked_ref[...],
+        jnp.concatenate(bin_hots, axis=1),
+        (((1,), (1,)), ((), ())),
+        preferred_element_type=F32,
+    )
     table_ref[...] = jnp.dot(
-        kernel_ref[...],
-        sums_ref[...],
-        precision=lax.Precision.HIGHEST,
-        preferred_element_type=F32,
+        kernel_ref[...], sums, precision=lax.Precision.HIGHEST, preferred_element_type=F32
     )
 
 
@@ -432,12 +493,7 @@
     even = lax.rem(lax.axis_index("gz"), 2) == 0
     blocks = (b0, b1, b2, b3)
     clear_edges(f)
-
-    def put(part, plane, row, columns, margins):
-        f[part, plane, pl.ds(row, SUB), 0:LANES] = columns
-        f[part, plane, pl.ds(row, SUB), LANES:WIDE] = margins
-
-    unpack(6, 2, blocks, first_ref, second_ref, put)
+    unpack(6, 2, blocks, first_ref, second_ref, field_put(f))
     factor_ref[...] = magnetic_factor()
 
     totals = totals_ref[...]
@@ -446,7 +502,7 @@
     by_bin = jnp.zeros((STEPS, bins), F32)
     for k in range(2 * NFREQ):
         by_bin = by_bin + kernel_ref[:, k : k + 1] * coefficients[k : k + 1, :]
-    bin_high, bin_low = split(by_bin)
+    by_bin = jnp.concatenate(split(by_bin), axis=0)
 
     def drive(ref, start, planes, z_first, z_count, row):
         cells = entry_row(ref[start]) - 1
@@ -459,21 +515,27 @@
         x = cells // (LANES * TILES * CZ)
         kept = jnp.logical_and(z >= 0, z < z_count)
         where = jnp.where(kept, x * z_count + z, -1)
-        hit = lax.broadcasted_iota(jnp.int32, (CX * z_count, ENTRIES), 0) == where
-        amplitude = [
-            jnp.dot(part, bin_hot, preferred_element_type=F32) for part in (bin_high, bin_low)
-        ]
+        count = CX * z_count
+        hit = lax.broadcasted_iota(jnp.int32, (count, ENTRIES), 0) == where
+        amplitude = jnp.dot(by_bin, bin_hot, preferred_element_type=F32)
+        spread = jnp.concatenate(
+            [
+                jnp.where(hit, amplitude[k : k + 1, :], 0.0).astype(BF16)
+                for k in range(2 * STEPS)
+            ],
+            axis=0,
+        )
+        total = lax.dot_general(
+            spread, lane_hot, (((1,), (1,)), ((), ())), preferred_element_type=F32
+        )
+        total = total[: STEPS * count] + total[STEPS * count :]
         for t in range(STEPS):
-            total = jnp.zeros((CX * z_count, WIDE), F32)
-            for part in amplitude:
-                spread = jnp.where(hit, part[t : t + 1, :], 0.0).astype(BF16)
-                total = total + lax.dot_general(
-                    spread, lane_hot, (((1,), (1,)), ((), ())), preferred_element_type=F32
-                )
             for k in range(CX):
-                drive_ref[t, planes + k, pl.ds(row, z_count), :] = total[
-                    k * z_count : (k + 1) * z_count
-                ]
+                at = t * count + k * z_count
+                for half in range(2):
+                    drive_ref[t, planes + k, half, pl.ds(row, z_count), :] = total[
+                        at : at + z_count, half * LANES : (half + 1) * LANES
+                    ]
 
     size = packed_rows(6)
     z_first = jnp.where(even, 0, HALO)
@@ -485,15 +547,7 @@
         drive(first_ref, m * (size + 2) + size, planes, z_first, HALO, row_first)
         drive(second_ref, m * (size + 2) + size, planes, HALO - z_first, HALO, row_second)
 
-    def step(t, carry):
-        def plane(i, carry):
-            ez = step_plane(f, factor_ref, inverse_ref, i)
-            f[2, i] = ez + drive_ref[t, i - 1]
-            return carry
-
-        return lax.fori_loop(1, PLANES + 1, plane, carry)
-
-    lax.fori_loop(0, STEPS, step, 0)
+    run_steps(f, factor_ref, inverse_ref, lambda t, i, ez: ez + drive_ref[t, i - 1])
     write_back(f, (o0, o1, o2, o3))
 
 
@@ -571,7 +625,7 @@
 ):
     bins = bin_weight.shape[0]
     record_kernel, source_kernel = time_kernels(STEPS)
-    by_row = np.repeat(record_kernel.T, CX * CZ, axis=1)
+    by_row = np.tile(np.repeat(record_kernel.T, CX * CZ, axis=1), (1, 2))
     lists = [
         v.reshape(SUB, LANES) for v in (monitor_cells, monitor_bins, source_cells, source_bins)
     ]
@@ -602,15 +656,19 @@
         [struct(TILES * (n_adj + 2), SUB, LANES)] * 2,
     )
     adjoint_first, adjoint_second = swap_neighbours(*adjoint_slabs)
-    field = pltpu.VMEM((6, PLANES + 2, ROWS, WIDE), F32)
-    factor = pltpu.VMEM((ROWS, WIDE), F32)
-    record = pltpu.VMEM((TILES, STEPS, CX, CZ, LANES), BF16)
+    field = pltpu.VMEM((6, PLANES + 2, 2, ROWS + 2 * PAD, LANES), F32)
+    factor = pltpu.VMEM((2, ROWS, LANES), F32)
     *forward_sent, inverse, table = call(
         forward_kernel,
         (*blocks, first, second, by_row),
         [struct(6 * CX * ZT, SUB, LANES)] * TILES
-        + [struct(PLANES + 2, ROWS, WIDE), struct(2 * NFREQ, bins)],
-        [field, factor, record, record, pltpu.VMEM((STEPS * CX * CZ, bins), F32)],
+        + [struct(PLANES + 2, 2, ROWS, LANES), struct(2 * NFREQ, bins)],
+        [
+            field,
+            factor,
+            pltpu.VMEM((TILES, 2, STEPS, CX, CZ, LANES), BF16),
+            pltpu.VMEM((2 * STEPS * CX * CZ, TILES * ENTRIES), BF16),
+        ],
     )
     totals = sum_all(table)
     forward_blocks = swap_blocks(forward_sent)
@@ -629,7 +687,7 @@
             source_kernel,
         ),
         [struct(6 * CX * ZT, SUB, LANES)] * TILES,
-        [field, factor, pltpu.VMEM((STEPS, PLANES, ROWS, WIDE), F32)],
+        [field, factor, pltpu.VMEM((STEPS, PLANES, 2, ROWS, LANES), F32)],
     )
     forward_out = call(spread_kernel, forward_blocks, struct(*fields.shape))
     adjoint_out = call(spread_kernel, swap_blocks(adjoint_back), struct(*fields.shape))

time: 157 us -> 105 us (0.67)
  Pallas kernels: 88.5 us -> 36.9 us
    pallas_call x8, Pallas kernels: 88.5 us -> 36.9 us  [call(): pl.pallas_call(kernel, out_shape=outs, in_specs=specs, out_specs=pl.Block...]
  transfers between devices with their start and end apart: 20 -> 20, of which waited for: 9 -> 9; matrix products, arithmetic and copies ran while one was open for 0% -> 1% of each run, Pallas kernels for 55% -> 33%
where the time goes in v2:
time: 105 us
  Pallas kernels  36.9 us (35%)
  waiting for transfers between devices  36.4 us (35%)
  starting transfers between devices  25.2 us (24%)
  local copies, waits for them, and re-layouts  5.4 us (5%)
    pallas_call x8, Pallas kernels, call(): pl.pallas_call(kernel, out_shape=outs, in_specs=specs, out_specs=pl.Block...  36.9 us
    ppermute x16, waiting for transfers between devices, swap(): return lax.ppermute(value, axis, [(i, i ^ distance) for i in range(count)])  36.4 us
    ppermute x16, starting transfers between devices, swap(): return lax.ppermute(value, axis, [(i, i ^ distance) for i in range(count)])  18.1 us
    ppermute x2, starting transfers between devices, swap_neighbours(): lax.ppermute(first, 'gz', pairs)  5.72 us
    unnamed x22, local copies, waits for them, and re-layouts  4.74 us
  transfers between devices with their start and end apart: 20, of which 9 were waited for; matrix products, arithmetic and copies ran while one was open for 1% of the time, Pallas kernels for 33%

profile of v2, /device:TPU:1, one launch (start us, length us, event | category | flops | bytes accessed | tf_op | source)
XLA Modules:
  0.0 104.6 jit_solution(17839955270737441651)
XLA Ops:
  1.3 1.1 %copy-done = f32[6,4,16,512]{3,2,1,0:T(8,128)S(1)} copy-done((f32[6,4,16,512]{3,2,1,0:T(8,128)S(1)}, f32[6,4,16,512]{3,2,1,0:T(8,128)}, u32[]{:S(2)}) %copy-start) | copy-done | bytes 786456
  5.9 2.7 %collective-permute-start.1 = (f32[66,8,128]{2,1,0:T(8,128)S(1)}, f32[66,8,128]{2,1,0:T(8,128)S(1)}, u32[]{:S(2)}, u32[]{:S(2)}) collective-permute-start(f32[66,8,128]{2,1,0:T(8,128)S(1)} %get-tuple-element.39), channel_id=1, source_target_pairs={{0,8},{4,12},{8,0},{12,4},{1,9},{5,13},{9,1},{13,5},{2,10},{6,14},... | collective-permute-start | bytes 811016 | tf_op jit(solution)/shard_map/ppermute | solution.py:591
  9.0 6.3 %collective-permute-done.1.b2 = f32[66,8,128]{2,1,0:T(8,128)S(1)} collective-permute-done((f32[66,8,128]{2,1,0:T(8,128)S(1)}, f32[66,8,128]{2,1,0:T(8,128)S(1)}, u32[]{:S(2)}, u32[]{:S(2)}) %collective-permute-start.1) | collective-permute-done | bytes 270368 | tf_op jit(solution)/shard_map/ppermute | solution.py:591
  15.3 5.8 %collective-permute-done.2.b3 = f32[66,8,128]{2,1,0:T(8,128)S(1)} collective-permute-done((f32[66,8,128]{2,1,0:T(8,128)S(1)}, f32[66,8,128]{2,1,0:T(8,128)S(1)}, u32[]{:S(2)}, u32[]{:S(2)}) %collective-permute-start.2) | collective-permute-done | bytes 270368 | tf_op jit(solution)/shard_map/ppermute | solution.py:591
  21.2 1.6 %collective-permute-start.3 = (f32[128,8,128]{2,1,0:T(8,128)S(1)}, f32[128,8,128]{2,1,0:T(8,128)S(1)}, u32[]{:S(2)}, u32[]{:S(2)}) collective-permute-start(f32[128,8,128]{2,1,0:T(8,128)S(1)} %get-tuple-element.47), channel_id=1, source_target_pairs={{0,1},{1,0},{2,3},{3,2},{4,5},{5,4},{6,7},{7,6},{8,9},{9,8},{10,11... | collective-permute-start | bytes 1572872 | tf_op jit(solution)/shard_map/ppermute | solution.py:603
  24.0 1.3 %collective-permute-start.6 = (f32[56,8,128]{2,1,0:T(8,128)S(1)}, f32[56,8,128]{2,1,0:T(8,128)S(1)}, u32[]{:S(2)}, u32[]{:S(2)}) collective-permute-start(f32[56,8,128]{2,1,0:T(8,128)S(1)} %get-tuple-element.51), channel_id=1, source_target_pairs={{0,8},{4,12},{8,0},{12,4},{1,9},{5,13},{9,1},{13,5},{2,10},{6,14},... | collective-permute-start | bytes 688136 | tf_op jit(solution)/shard_map/ppermute | solution.py:591
  25.7 5.5 %collective-permute-done.6.b2 = f32[56,8,128]{2,1,0:T(8,128)S(1)} collective-permute-done((f32[56,8,128]{2,1,0:T(8,128)S(1)}, f32[56,8,128]{2,1,0:T(8,128)S(1)}, u32[]{:S(2)}, u32[]{:S(2)}) %collective-permute-start.6) | collective-permute-done | bytes 229408 | tf_op jit(solution)/shard_map/ppermute | solution.py:591
  31.2 5.1 %collective-permute-done.7.b3 = f32[56,8,128]{2,1,0:T(8,128)S(1)} collective-permute-done((f32[56,8,128]{2,1,0:T(8,128)S(1)}, f32[56,8,128]{2,1,0:T(8,128)S(1)}, u32[]{:S(2)}, u32[]{:S(2)}) %collective-permute-start.7) | collective-permute-done | bytes 229408 | tf_op jit(solution)/shard_map/ppermute | solution.py:591
  36.4 4.2 %collective-permute-start.11 = (f32[116,8,128]{2,1,0:T(8,128)S(1)}, f32[116,8,128]{2,1,0:T(8,128)S(1)}, u32[]{:S(2)}, u32[]{:S(2)}) collective-permute-start(f32[116,8,128]{2,1,0:T(8,128)S(1)} %get-tuple-element.63), channel_id=1, source_target_pairs={{0,1},{1,0},{2,3},{3,2},{4,5},{5,4},{6,7},{7,6},{8,9},{9,8},{10,11... | collective-permute-start | bytes 1425416 | tf_op jit(solution)/shard_map/ppermute | solution.py:603
  41.2 16.0 %shard_map.133 = (f32[48,8,128]{2,1,0:T(8,128)S(1)}, f32[48,8,128]{2,1,0:T(8,128)S(1)}, f32[48,8,128]{2,1,0:T(8,128)S(1)}, f32[48,8,128]{2,1,0:T(8,128)S(1)}, f3...) custom-call(f32[66,8,128]{2,1,0:T(8,128)S(1)} %get-tuple-element.37.b0, f32[66,8,128]{2,1,0:T(8,128)S(1)} %collective-permute-done.b1, ...), custom_call_target="tpu_custom_call" | custom-call | tf_op jit(solution)/shard_map/pallas_call | solution.py:579
  57.3 1.7 %collective-permute-start.10 = (f32[48,8,128]{2,1,0:T(8,128)S(1)}, f32[48,8,128]{2,1,0:T(8,128)S(1)}, u32[]{:S(2)}, u32[]{:S(2)}) collective-permute-start(f32[48,8,128]{2,1,0:T(8,128)S(1)} %get-tuple-element.58), channel_id=1, source_target_pairs={{0,12},{4,8},{8,4},{12,0},{1,13},{5,9},{9,5},{13,1},{2,14},{6,10},... | collective-permute-start | bytes 589832 | tf_op jit(solution)/shard_map/ppermute | solution.py:591
  58.9 1.2 %collective-permute-done.13 = f32[8,128]{1,0:T(8,128)S(1)} collective-permute-done((f32[8,128]{1,0:T(8,128)S(1)}, f32[8,128]{1,0:T(8,128)S(1)}, u32[]{:S(2)}, u32[]{:S(2)}) %collective-permute-start.13) | collective-permute-done | bytes 4128 | tf_op jit(solution)/shard_map/ppermute | solution.py:591
  60.3 4.1 %collective-permute-done.14 = f32[8,128]{1,0:T(8,128)S(1)} collective-permute-done((f32[8,128]{1,0:T(8,128)S(1)}, f32[8,128]{1,0:T(8,128)S(1)}, u32[]{:S(2)}, u32[]{:S(2)}) %collective-permute-start.14) | collective-permute-done | bytes 4128 | tf_op jit(solution)/shard_map/ppermute | solution.py:591
  64.5 2.3 %collective-permute-start.15 = (f32[8,128]{1,0:T(8,128)S(1)}, f32[8,128]{1,0:T(8,128)S(1)}, u32[]{:S(2)}, u32[]{:S(2)}) collective-permute-start(f32[8,128]{1,0:T(8,128)S(1)} %add.19), channel_id=1, source_target_pairs={{0,1},{1,0},{2,3},{3,2},{4,5},{5,4},{6,7},{7,6},{8,9},{9,8},{10,11... | collective-permute-start | bytes 12296 | tf_op jit(solution)/shard_map/ppermute | solution.py:591
  67.8 1.6 %collective-permute-start.16 = (f32[8,128]{1,0:T(8,128)S(1)}, f32[8,128]{1,0:T(8,128)S(1)}, u32[]{:S(2)}, u32[]{:S(2)}) collective-permute-start(f32[8,128]{1,0:T(8,128)S(1)} %add.20), channel_id=1, source_target_pairs={{0,2},{1,3},{2,0},{3,1},{4,6},{5,7},{6,4},{7,5},{8,10},{9,11},{10,... | collective-permute-start | bytes 12296 | tf_op jit(solution)/shard_map/ppermute | solution.py:591
  69.3 2.1 %collective-permute-start.8 = (f32[48,8,128]{2,1,0:T(8,128)S(1)}, f32[48,8,128]{2,1,0:T(8,128)S(1)}, u32[]{:S(2)}, u32[]{:S(2)}) collective-permute-start(f32[48,8,128]{2,1,0:T(8,128)S(1)} %get-tuple-element.56), channel_id=1, source_target_pairs={{0,4},{4,0},{8,12},{12,8},{1,5},{5,1},{9,13},{13,9},{2,6},{6,2},{1... | collective-permute-start | bytes 589832 | tf_op jit(solution)/shard_map/ppermute | solution.py:591
  71.4 1.2 %collective-permute-start.9 = (f32[48,8,128]{2,1,0:T(8,128)S(1)}, f32[48,8,128]{2,1,0:T(8,128)S(1)}, u32[]{:S(2)}, u32[]{:S(2)}) collective-permute-start(f32[48,8,128]{2,1,0:T(8,128)S(1)} %get-tuple-element.57), channel_id=1, source_target_pairs={{0,8},{4,12},{8,0},{12,4},{1,9},{5,13},{9,1},{13,5},{2,10},{6,14},... | collective-permute-start | bytes 589832 | tf_op jit(solution)/shard_map/ppermute | solution.py:591
  73.4 17.3 %shard_map.136 = (f32[48,8,128]{2,1,0:T(8,128)S(1)}, f32[48,8,128]{2,1,0:T(8,128)S(1)}, f32[48,8,128]{2,1,0:T(8,128)S(1)}, f32[48,8,128]{2,1,0:T(8,128)S(1)}) custom-call(f32[56,8,128]{2,1,0:T(8,128)S(1)} %get-tuple-element.59.b0, f32[56,8,128]{2,1,0:T(8,128)S(1)} %collective-permute-done.5.b1, f32[56,8,128]{2,1,0:T(8,128)S(1)} %collective-permute-done.6.b2, ...), custom_call_target="tpu_custom_call" | custom-call | tf_op jit(solution)/shard_map/pallas_call | solution.py:579
  90.6 2.1 %collective-permute-start.17 = (f32[48,8,128]{2,1,0:T(8,128)S(1)}, f32[48,8,128]{2,1,0:T(8,128)S(1)}, u32[]{:S(2)}, u32[]{:S(2)}) collective-permute-start(f32[48,8,128]{2,1,0:T(8,128)S(1)} %get-tuple-element.68), channel_id=1, source_target_pairs={{0,4},{4,0},{8,12},{12,8},{1,5},{5,1},{9,13},{13,9},{2,6},{6,2},{1... | collective-permute-start | bytes 589832 | tf_op jit(solution)/shard_map/ppermute | solution.py:591
  93.5 1.0 collective-permute-start.19
  95.2 1.0 shard_map.134
  96.2 3.1 %collective-permute-done.18.b2 = f32[48,8,128]{2,1,0:T(8,128)S(1)} collective-permute-done((f32[48,8,128]{2,1,0:T(8,128)S(1)}, f32[48,8,128]{2,1,0:T(8,128)S(1)}, u32[]{:S(2)}, u32[]{:S(2)}) %collective-permute-start.18) | collective-permute-done | bytes 196640 | tf_op jit(solution)/shard_map/ppermute | solution.py:591
  99.3 4.4 %collective-permute-done.19.b3 = f32[48,8,128]{2,1,0:T(8,128)S(1)} collective-permute-done((f32[48,8,128]{2,1,0:T(8,128)S(1)}, f32[48,8,128]{2,1,0:T(8,128)S(1)}, u32[]{:S(2)}, u32[]{:S(2)}) %collective-permute-start.19) | collective-permute-done | bytes 196640 | tf_op jit(solution)/shard_map/ppermute | solution.py:591
  103.6 1.0 shard_map.137
  (51 shorter events, 10.3 us)
Async XLA Ops:
  4.7 3.9 %copy-start.1 = (f32[6,4,16,512]{3,2,1,0:T(8,128)S(1)}, f32[6,4,16,512]{3,2,1,0:T(8,128)}, u32[]{:S(2)}) copy-start(f32[6,4,16,512]{3,2,1,0:T(8,128)} %fields_ref.3) | copy-start | bytes 2359300
  5.7 2.9 %copy-start.7 = (s32[1,1,1024]{2,1,0:T(1,128)S(1)}, s32[1,1,1024]{2,1,0:T(1,128)}, u32[]{:S(2)}) copy-start(s32[1,1,1024]{2,1,0:T(1,128)} %param.18) | copy-start | bytes 12292
  5.7 2.9 %copy-start.6 = (s32[1,1,1024]{2,1,0:T(1,128)S(1)}, s32[1,1,1024]{2,1,0:T(1,128)}, u32[]{:S(2)}) copy-start(s32[1,1,1024]{2,1,0:T(1,128)} %param.17) | copy-start | bytes 12292
  5.7 3.3 %collective-permute-start = (f32[66,8,128]{2,1,0:T(8,128)S(1)}, f32[66,8,128]{2,1,0:T(8,128)S(1)}, u32[]{:S(2)}, u32[]{:S(2)}) collective-permute-start(f32[66,8,128]{2,1,0:T(8,128)S(1)} %get-tuple-element.38), channel_id=1, source_target_pairs={{0,4},{4,0},{8,12},{12,8},{1,5},{5,1},{9,13},{13,9},{2,6},{6,2},{1... | collective-permute-start | bytes 811016 | tf_op jit(solution)/shard_map/ppermute | solution.py:591
  5.9 9.5 %collective-permute-start.1 = (f32[66,8,128]{2,1,0:T(8,128)S(1)}, f32[66,8,128]{2,1,0:T(8,128)S(1)}, u32[]{:S(2)}, u32[]{:S(2)}) collective-permute-start(f32[66,8,128]{2,1,0:T(8,128)S(1)} %get-tuple-element.39), channel_id=1, source_target_pairs={{0,8},{4,12},{8,0},{12,4},{1,9},{5,13},{9,1},{13,5},{2,10},{6,14},... | collective-permute-start | bytes 811016 | tf_op jit(solution)/shard_map/ppermute | solution.py:591
  8.6 12.6 %collective-permute-start.2 = (f32[66,8,128]{2,1,0:T(8,128)S(1)}, f32[66,8,128]{2,1,0:T(8,128)S(1)}, u32[]{:S(2)}, u32[]{:S(2)}) collective-permute-start(f32[66,8,128]{2,1,0:T(8,128)S(1)} %get-tuple-element.40), channel_id=1, source_target_pairs={{0,12},{4,8},{8,4},{12,0},{1,13},{5,9},{9,5},{13,1},{2,14},{6,10},... | collective-permute-start | bytes 811016 | tf_op jit(solution)/shard_map/ppermute | solution.py:591
  21.2 20.0 %copy-start.3 = (f32[8,1024]{1,0:T(8,128)S(1)}, f32[8,1024]{1,0:T(8,128)}, u32[]{:S(2)}) copy-start(f32[8,1024]{1,0:T(8,128)} %constant.19.clone.kernel_ref) | copy-start | bytes 98308
  21.2 15.1 %collective-permute-start.3 = (f32[128,8,128]{2,1,0:T(8,128)S(1)}, f32[128,8,128]{2,1,0:T(8,128)S(1)}, u32[]{:S(2)}, u32[]{:S(2)}) collective-permute-start(f32[128,8,128]{2,1,0:T(8,128)S(1)} %get-tuple-element.47), channel_id=1, source_target_pairs={{0,1},{1,0},{2,3},{3,2},{4,5},{5,4},{6,7},{7,6},{8,9},{9,8},{10,11... | collective-permute-start | bytes 1572872 | tf_op jit(solution)/shard_map/ppermute | solution.py:603
  22.8 13.5 %collective-permute-start.4 = (f32[128,8,128]{2,1,0:T(8,128)S(1)}, f32[128,8,128]{2,1,0:T(8,128)S(1)}, u32[]{:S(2)}, u32[]{:S(2)}) collective-permute-start(f32[128,8,128]{2,1,0:T(8,128)S(1)} %get-tuple-element.48), channel_id=1, source_target_pairs={{1,2},{2,1},{5,6},{6,5},{9,10},{10,9},{13,14},{14,13},{17,18},{18,... | collective-permute-start | bytes 1572872 | tf_op jit(solution)/shard_map/ppermute | solution.py:603
  23.5 2.3 %collective-permute-start.5 = (f32[56,8,128]{2,1,0:T(8,128)S(1)}, f32[56,8,128]{2,1,0:T(8,128)S(1)}, u32[]{:S(2)}, u32[]{:S(2)}) collective-permute-start(f32[56,8,128]{2,1,0:T(8,128)S(1)} %get-tuple-element.50), channel_id=1, source_target_pairs={{0,4},{4,0},{8,12},{12,8},{1,5},{5,1},{9,13},{13,9},{2,6},{6,2},{1... | collective-permute-start | bytes 688136 | tf_op jit(solution)/shard_map/ppermute | solution.py:591
  24.0 7.2 %collective-permute-start.6 = (f32[56,8,128]{2,1,0:T(8,128)S(1)}, f32[56,8,128]{2,1,0:T(8,128)S(1)}, u32[]{:S(2)}, u32[]{:S(2)}) collective-permute-start(f32[56,8,128]{2,1,0:T(8,128)S(1)} %get-tuple-element.51), channel_id=1, source_target_pairs={{0,8},{4,12},{8,0},{12,4},{1,9},{5,13},{9,1},{13,5},{2,10},{6,14},... | collective-permute-start | bytes 688136 | tf_op jit(solution)/shard_map/ppermute | solution.py:591
  25.3 11.0 %collective-permute-start.7 = (f32[56,8,128]{2,1,0:T(8,128)S(1)}, f32[56,8,128]{2,1,0:T(8,128)S(1)}, u32[]{:S(2)}, u32[]{:S(2)}) collective-permute-start(f32[56,8,128]{2,1,0:T(8,128)S(1)} %get-tuple-element.52), channel_id=1, source_target_pairs={{0,12},{4,8},{8,4},{12,0},{1,13},{5,9},{9,5},{13,1},{2,14},{6,10},... | collective-permute-start | bytes 688136 | tf_op jit(solution)/shard_map/ppermute | solution.py:591
  36.4 36.3 %collective-permute-start.11 = (f32[116,8,128]{2,1,0:T(8,128)S(1)}, f32[116,8,128]{2,1,0:T(8,128)S(1)}, u32[]{:S(2)}, u32[]{:S(2)}) collective-permute-start(f32[116,8,128]{2,1,0:T(8,128)S(1)} %get-tuple-element.63), channel_id=1, source_target_pairs={{0,1},{1,0},{2,3},{3,2},{4,5},{5,4},{6,7},{7,6},{8,9},{9,8},{10,11... | collective-permute-start | bytes 1425416 | tf_op jit(solution)/shard_map/ppermute | solution.py:603
  40.5 32.2 %collective-permute-start.12 = (f32[116,8,128]{2,1,0:T(8,128)S(1)}, f32[116,8,128]{2,1,0:T(8,128)S(1)}, u32[]{:S(2)}, u32[]{:S(2)}) collective-permute-start(f32[116,8,128]{2,1,0:T(8,128)S(1)} %get-tuple-element.64), channel_id=1, source_target_pairs={{1,2},{2,1},{5,6},{6,5},{9,10},{10,9},{13,14},{14,13},{17,18},{18,... | collective-permute-start | bytes 1425416 | tf_op jit(solution)/shard_map/ppermute | solution.py:603
  57.3 36.2 %collective-permute-start.10 = (f32[48,8,128]{2,1,0:T(8,128)S(1)}, f32[48,8,128]{2,1,0:T(8,128)S(1)}, u32[]{:S(2)}, u32[]{:S(2)}) collective-permute-start(f32[48,8,128]{2,1,0:T(8,128)S(1)} %get-tuple-element.58), channel_id=1, source_target_pairs={{0,12},{4,8},{8,4},{12,0},{1,13},{5,9},{9,5},{13,1},{2,14},{6,10},... | collective-permute-start | bytes 589832 | tf_op jit(solution)/shard_map/ppermute | solution.py:591
  58.9 1.2 %collective-permute-start.13 = (f32[8,128]{1,0:T(8,128)S(1)}, f32[8,128]{1,0:T(8,128)S(1)}, u32[]{:S(2)}, u32[]{:S(2)}) collective-permute-start(f32[8,128]{1,0:T(8,128)S(1)} %get-tuple-element.66), channel_id=1, source_target_pairs={{0,4},{4,0},{8,12},{12,8},{1,5},{5,1},{9,13},{13,9},{2,6},{6,2},{1... | collective-permute-start | bytes 12296 | tf_op jit(solution)/shard_map/ppermute | solution.py:591
  60.1 4.3 %collective-permute-start.14 = (f32[8,128]{1,0:T(8,128)S(1)}, f32[8,128]{1,0:T(8,128)S(1)}, u32[]{:S(2)}, u32[]{:S(2)}) collective-permute-start(f32[8,128]{1,0:T(8,128)S(1)} %add.18), channel_id=1, source_target_pairs={{0,8},{4,12},{8,0},{12,4},{1,9},{5,13},{9,1},{13,5},{2,10},{6,14},... | collective-permute-start | bytes 12296 | tf_op jit(solution)/shard_map/ppermute | solution.py:591
  64.5 3.3 %collective-permute-start.15 = (f32[8,128]{1,0:T(8,128)S(1)}, f32[8,128]{1,0:T(8,128)S(1)}, u32[]{:S(2)}, u32[]{:S(2)}) collective-permute-start(f32[8,128]{1,0:T(8,128)S(1)} %add.19), channel_id=1, source_target_pairs={{0,1},{1,0},{2,3},{3,2},{4,5},{5,4},{6,7},{7,6},{8,9},{9,8},{10,11... | collective-permute-start | bytes 12296 | tf_op jit(solution)/shard_map/ppermute | solution.py:591
  67.8 3.7 %collective-permute-start.16 = (f32[8,128]{1,0:T(8,128)S(1)}, f32[8,128]{1,0:T(8,128)S(1)}, u32[]{:S(2)}, u32[]{:S(2)}) collective-permute-start(f32[8,128]{1,0:T(8,128)S(1)} %add.20), channel_id=1, source_target_pairs={{0,2},{1,3},{2,0},{3,1},{4,6},{5,7},{6,4},{7,5},{8,10},{9,11},{10,... | collective-permute-start | bytes 12296 | tf_op jit(solution)/shard_map/ppermute | solution.py:591
  69.3 25.8 %collective-permute-start.8 = (f32[48,8,128]{2,1,0:T(8,128)S(1)}, f32[48,8,128]{2,1,0:T(8,128)S(1)}, u32[]{:S(2)}, u32[]{:S(2)}) collective-permute-start(f32[48,8,128]{2,1,0:T(8,128)S(1)} %get-tuple-element.56), channel_id=1, source_target_pairs={{0,4},{4,0},{8,12},{12,8},{1,5},{5,1},{9,13},{13,9},{2,6},{6,2},{1... | collective-permute-start | bytes 589832 | tf_op jit(solution)/shard_map/ppermute | solution.py:591
  71.4 23.7 %collective-permute-start.9 = (f32[48,8,128]{2,1,0:T(8,128)S(1)}, f32[48,8,128]{2,1,0:T(8,128)S(1)}, u32[]{:S(2)}, u32[]{:S(2)}) collective-permute-start(f32[48,8,128]{2,1,0:T(8,128)S(1)} %get-tuple-element.57), channel_id=1, source_target_pairs={{0,8},{4,12},{8,0},{12,4},{1,9},{5,13},{9,1},{13,5},{2,10},{6,14},... | collective-permute-start | bytes 589832 | tf_op jit(solution)/shard_map/ppermute | solution.py:591
  90.6 5.5 %collective-permute-start.17 = (f32[48,8,128]{2,1,0:T(8,128)S(1)}, f32[48,8,128]{2,1,0:T(8,128)S(1)}, u32[]{:S(2)}, u32[]{:S(2)}) collective-permute-start(f32[48,8,128]{2,1,0:T(8,128)S(1)} %get-tuple-element.68), channel_id=1, source_target_pairs={{0,4},{4,0},{8,12},{12,8},{1,5},{5,1},{9,13},{13,9},{2,6},{6,2},{1... | collective-permute-start | bytes 589832 | tf_op jit(solution)/shard_map/ppermute | solution.py:591
  92.8 6.5 %collective-permute-start.18 = (f32[48,8,128]{2,1,0:T(8,128)S(1)}, f32[48,8,128]{2,1,0:T(8,128)S(1)}, u32[]{:S(2)}, u32[]{:S(2)}) collective-permute-start(f32[48,8,128]{2,1,0:T(8,128)S(1)} %get-tuple-element.69), channel_id=1, source_target_pairs={{0,8},{4,12},{8,0},{12,4},{1,9},{5,13},{9,1},{13,5},{2,10},{6,14},... | collective-permute-start | bytes 589832 | tf_op jit(solution)/shard_map/ppermute | solution.py:591
  93.5 10.1 %collective-permute-start.19 = (f32[48,8,128]{2,1,0:T(8,128)S(1)}, f32[48,8,128]{2,1,0:T(8,128)S(1)}, u32[]{:S(2)}, u32[]{:S(2)}) collective-permute-start(f32[48,8,128]{2,1,0:T(8,128)S(1)} %get-tuple-element.70), channel_id=1, source_target_pairs={{0,12},{4,8},{8,4},{12,0},{1,13},{5,9},{9,5},{13,1},{2,14},{6,10},... | collective-permute-start | bytes 589832 | tf_op jit(solution)/shard_map/ppermute | solution.py:591
  (7 other events, 5.4 us)

commit v3 on v2

--- a/solution.py
+++ b/solution.py
@@ -181,7 +181,7 @@
     return lax.broadcasted_iota(jnp.int32, (SUB, LANES), 1)
 
 
-def pack_block(read, parts, column, store):
+def pack_block(read, regions, parts, column, store):
     lanes = lane_ids()
     upper = lanes >= LANES // 2
     take_left = jnp.logical_and(upper, column > 0)
@@ -190,7 +190,7 @@
     left = pl.multiple_of(jnp.maximum(column - 1, 0) * LANES, LANES)
     right = pl.multiple_of(jnp.minimum(column + 1, TILES - 1) * LANES, LANES)
     size = packed_rows(parts)
-    for zt in range(ZT):
+    for zt in range(regions):
         margins = [jnp.zeros((SUB, LANES), F32) for _ in range((parts + 1) // 2)]
         for part in range(parts):
             for x in range(CX):
@@ -207,10 +207,39 @@
             store(zt * size + parts * CX + pair, margin)
 
 
+def fetch(pairs, sems):
+    copies = [
+        pltpu.make_async_copy(source, target, sems.at[k])
+        for k, (source, target) in enumerate(pairs)
+    ]
+    for copy in copies:
+        copy.start()
+    for copy in copies:
+        copy.wait()
+
+
+def put_list(out, row, lanes, list_ref, offset):
+    for i in range(SUB):
+        entries = list_ref[0, :, i * LANES : (i + 1) * LANES]
+        out[row, i : i + 1, lanes] = (entries + offset).astype(F32)
+
+
 def pack_forward_kernel(
-    fields_ref, ids_ref, eps_ref, cells_ref, bins_ref, o0, o1, o2, o3, inverse_ref
+    fields_hbm, ids_hbm, eps_hbm, cells_hbm, bins_hbm,
+    o0, o1, o2, o3,
+    fields_ref, ids_ref, eps_ref, cells_ref, bins_ref, inverse_ref, sems,
 ):
     me = lax.axis_index("xy")
+    fetch(
+        [
+            (fields_hbm, fields_ref),
+            (ids_hbm, ids_ref),
+            (eps_hbm, eps_ref),
+            (cells_hbm, cells_ref),
+            (bins_hbm, bins_ref),
+        ],
+        sems,
+    )
     ids = ids_ref[...]
     eps = jnp.full(ids.shape, eps_ref[0], F32)
     for material in range(1, eps_ref.shape[0]):
@@ -228,13 +257,20 @@
         def store(row, value, out=out):
             out[row] = value
 
-        pack_block(read, 7, me ^ m, store)
-        out[ZT * packed_rows(7)] = cells_ref[...].astype(F32)
-        out[ZT * packed_rows(7) + 1] = bins_ref[...].astype(F32)
-
-
-def pack_adjoint_kernel(fields_ref, cells_ref, bins_ref, o0, o1, o2, o3):
+        pack_block(read, ZT, 7, me ^ m, store)
+        for k, ref in enumerate((cells_ref, bins_ref)):
+            put_list(out, ZT * packed_rows(7) + k, slice(0, LANES), ref, 0)
+
+
+def pack_adjoint_kernel(
+    fields_hbm, cells_hbm, bins_hbm, weight_ref, kernel_ref,
+    o0, o1, o2, o3, weight_out, kernel_out,
+    fields_ref, cells_ref, bins_ref, sems,
+):
     me = lax.axis_index("xy")
+    fetch([(fields_hbm, fields_ref), (cells_hbm, cells_ref), (bins_hbm, bins_ref)], sems)
+    weight_out[...] = weight_ref[...]
+    kernel_out[...] = kernel_ref[...]
 
     def read(part, x, zt, lane):
         return fields_ref[part, x, pl.ds(zt * SUB, SUB), pl.ds(lane, LANES)]
@@ -244,14 +280,14 @@
         def store(row, value, out=out):
             out[row] = value
 
-        pack_block(read, 6, me ^ m, store)
-        out[ZT * packed_rows(6)] = cells_ref[...].astype(F32) + 1.0
-        out[ZT * packed_rows(6) + 1] = bins_ref[...].astype(F32)
-
-
-def slab_kernel(size, lists, b0, b1, b2, b3, first_ref, second_ref):
-    even = lax.rem(lax.axis_index("gz"), 2) == 0
-    zt_first = jnp.where(even, 1, 0)
+        pack_block(read, ZT, 6, me ^ m, store)
+        put_list(out, ZT * packed_rows(6), slice(0, LANES), cells_ref, 1)
+        put_list(out, ZT * packed_rows(6) + 1, slice(0, LANES), bins_ref, 0)
+
+
+def slab_kernel(parts, lists, b0, b1, b2, b3, first_ref, second_ref):
+    size = packed_rows(parts)
+    zt_first = jnp.where(lax.rem(lax.axis_index("gz"), 2) == 0, 1, 0)
     for m, block in enumerate((b0, b1, b2, b3)):
         base = m * (size + lists)
         first_ref[pl.ds(base, size)] = block[pl.ds(zt_first * size, size)]
@@ -261,36 +297,31 @@
             second_ref[base + size + k] = block[ZT * size + k]
 
 
-def unpack(parts, lists, blocks, first_ref, second_ref, put):
-    me = lax.axis_index("xy")
+def edge_rows():
     even = lax.rem(lax.axis_index("gz"), 2) == 0
-    row_first = pl.multiple_of(jnp.where(even, HALO + CZ, 0), SUB)
-    row_second = pl.multiple_of(jnp.where(even, 0, HALO + CZ), SUB)
-    size = packed_rows(parts)
+    return (
+        pl.multiple_of(jnp.where(even, HALO + CZ, 0), SUB),
+        pl.multiple_of(jnp.where(even, 0, HALO + CZ), SUB),
+    )
+
+
+def unpack(parts, sources, put):
     lanes = lane_ids()
     in_margin = jnp.logical_or(lanes < HALO, lanes >= LANES - HALO)
-    for m, block in enumerate(blocks):
-        base = (me ^ m) * CX + 1
-        sources = (
-            (first_ref, m * (size + lists), row_first),
-            (second_ref, m * (size + lists), row_second),
-            (block, 0, HALO),
-            (block, size, HALO + SUB),
-        )
-        for ref, start, row in sources:
-            for part in range(parts):
-                for x in range(CX):
-                    slot = (part % 2) * CX + x
-                    margin = pltpu.roll(
-                        ref[start + parts * CX + part // 2], (-16 * slot - HALO) % LANES, 1
-                    )
-                    put(
-                        part,
-                        base + x,
-                        row,
-                        ref[start + part * CX + x],
-                        jnp.where(in_margin, margin, 0.0),
-                    )
+    for ref, start, row in sources:
+        for part in range(parts):
+            for x in range(CX):
+                slot = (part % 2) * CX + x
+                margin = pltpu.roll(
+                    ref[start + parts * CX + part // 2], (-16 * slot - HALO) % LANES, 1
+                )
+                put(
+                    part,
+                    x,
+                    row,
+                    ref[start + part * CX + x],
+                    jnp.where(in_margin, margin, 0.0),
+                )
 
 
 def magnetic_factor():
@@ -350,33 +381,23 @@
 
 
 def run_steps(f, factor_ref, inverse_ref, finish):
-    groups = PLANES // GROUP
     rows = pl.ds(PAD, ROWS)
 
-    def keep_magnetic(i, done):
-        for k, fields in enumerate(done):
-            for part, value in enumerate(fields):
-                f[3 + part, i + k, :, rows, :] = value
-
-    def keep_electric(t, i, done):
-        for k, (ex, ey, ez) in enumerate(done):
-            f[0, i + k, :, rows, :] = ex
-            f[1, i + k, :, rows, :] = ey
-            f[2, i + k, :, rows, :] = finish(t, i + k, ez)
-
-    def body(n, carry):
-        i = 1 + lax.rem(n, groups) * GROUP
-        j = 1 + lax.rem(n - 1, groups) * GROUP
-        magnetic = magnetic_planes(f, factor_ref[...], i)
-        electric = electric_planes(f, inverse_ref, j)
-        keep_magnetic(i, magnetic)
-        keep_electric((n - 1) // groups, j, electric)
+    def body(t, carry):
+        for i in range(1, PLANES + 2, GROUP):
+            magnetic = magnetic_planes(f, factor_ref[...], i) if i <= PLANES else []
+            electric = electric_planes(f, inverse_ref, i - GROUP) if i > 1 else []
+            for k, fields in enumerate(magnetic):
+                for part, value in enumerate(fields):
+                    f[3 + part, i + k, :, rows, :] = value
+            for k, (ex, ey, ez) in enumerate(electric):
+                j = i - GROUP + k
+                f[0, j, :, rows, :] = ex
+                f[1, j, :, rows, :] = ey
+                f[2, j, :, rows, :] = finish(t, j, ez)
         return carry
 
-    keep_magnetic(1, magnetic_planes(f, factor_ref[...], 1))
-    lax.fori_loop(1, STEPS * groups, body, 0)
-    last = PLANES - GROUP + 1
-    keep_electric(STEPS - 1, last, electric_planes(f, inverse_ref, last))
+    lax.fori_loop(0, STEPS, body, 0)
 
 
 def entry_row(vector):
@@ -414,8 +435,9 @@
             f[part, :, :, pl.ds(start, PAD), :] = jnp.zeros((PLANES + 2, 2, PAD, LANES), F32)
 
 
-def field_put(f):
-    def put(part, plane, row, columns, margins):
+def field_put(f, base):
+    def put(part, x, row, columns, margins):
+        plane = base + x
         rows = pl.ds(pl.multiple_of(PAD + row, SUB), SUB)
         f[part, plane, 0, rows, :] = columns
         f[part, plane, 1, rows, :] = margins
@@ -431,22 +453,32 @@
     me = lax.axis_index("xy")
     blocks = (b0, b1, b2, b3)
     clear_edges(f)
-    put_field = field_put(f)
-
-    def put(part, plane, row, columns, margins):
-        if part == 6:
-            inverse_ref[plane, 0, pl.ds(row, SUB), :] = columns
-            inverse_ref[plane, 1, pl.ds(row, SUB), :] = margins
-        else:
-            put_field(part, plane, row, columns, margins)
-
-    unpack(7, 0, blocks, first_ref, second_ref, put)
+    row_first, row_second = edge_rows()
+    size = packed_rows(7)
+    for m, block in enumerate(blocks):
+        base = (me ^ m) * CX + 1
+        put_field = field_put(f, base)
+
+        def put(part, x, row, columns, margins, base=base, put_field=put_field):
+            if part == 6:
+                inverse_ref[base + x, 0, pl.ds(row, SUB), :] = columns
+                inverse_ref[base + x, 1, pl.ds(row, SUB), :] = margins
+            else:
+                put_field(part, x, row, columns, margins)
+
+        sources = [
+            (first_ref, m * size, row_first),
+            (second_ref, m * size, row_second),
+            (block, 0, HALO),
+            (block, size, HALO + SUB),
+        ]
+        unpack(7, sources, put)
     factor_ref[...] = magnetic_factor()
 
     def finish(t, i, ez):
         x = i - 1
         for part, value in enumerate(split(ez[0, HALO : HALO + CZ])):
-            record_ref[x // CX, part, t, lax.rem(x, CX)] = value
+            record_ref[x // CX, part, t, x % CX] = value
         return ez
 
     run_steps(f, factor_ref, inverse_ref, finish)
@@ -493,7 +525,16 @@
     even = lax.rem(lax.axis_index("gz"), 2) == 0
     blocks = (b0, b1, b2, b3)
     clear_edges(f)
-    unpack(6, 2, blocks, first_ref, second_ref, field_put(f))
+    row_first, row_second = edge_rows()
+    size = packed_rows(6)
+    for m, block in enumerate(blocks):
+        sources = [
+            (first_ref, m * (size + 2), row_first),
+            (second_ref, m * (size + 2), row_second),
+            (block, 0, HALO),
+            (block, size, HALO + SUB),
+        ]
+        unpack(6, sources, field_put(f, (me ^ m) * CX + 1))
     factor_ref[...] = magnetic_factor()
 
     totals = totals_ref[...]
@@ -537,15 +578,13 @@
                         at : at + z_count, half * LANES : (half + 1) * LANES
                     ]
 
-    size = packed_rows(6)
     z_first = jnp.where(even, 0, HALO)
-    row_first = pl.multiple_of(jnp.where(even, HALO + CZ, 0), SUB)
-    row_second = pl.multiple_of(jnp.where(even, 0, HALO + CZ), SUB)
     for m, block in enumerate(blocks):
         planes = (me ^ m) * CX
+        base = m * (size + 2) + size
         drive(block, ZT * size, planes, 0, CZ, HALO)
-        drive(first_ref, m * (size + 2) + size, planes, z_first, HALO, row_first)
-        drive(second_ref, m * (size + 2) + size, planes, HALO - z_first, HALO, row_second)
+        drive(first_ref, base, planes, z_first, HALO, row_first)
+        drive(second_ref, base, planes, HALO - z_first, HALO, row_second)
 
     run_steps(f, factor_ref, inverse_ref, lambda t, i, ez: ez + drive_ref[t, i - 1])
     write_back(f, (o0, o1, o2, o3))
@@ -567,22 +606,17 @@
     return jax.ShapeDtypeStruct(shape, F32)
 
 
-def in_vmem(count):
-    return [pl.BlockSpec(memory_space=pltpu.VMEM)] * count
-
-
-def call(kernel, args, outs, scratch=(), scalars=()):
-    specs = in_vmem(len(args))
-    for place in scalars:
-        specs[place] = pl.BlockSpec(memory_space=pltpu.SMEM)
-    single = not isinstance(outs, list)
+def call(kernel, args, outs, scratch=(), places=None, limit=48 * 1024 * 1024):
+    spaces = places or {}
     return pl.pallas_call(
         kernel,
         out_shape=outs,
-        in_specs=specs,
-        out_specs=pl.BlockSpec(memory_space=pltpu.VMEM) if single else in_vmem(len(outs)),
+        in_specs=[
+            pl.BlockSpec(memory_space=spaces.get(k, pltpu.VMEM)) for k in range(len(args))
+        ],
+        out_specs=jax.tree.map(lambda _: pl.BlockSpec(memory_space=pltpu.VMEM), outs),
         scratch_shapes=list(scratch),
-        compiler_params=pltpu.CompilerParams(vmem_limit_bytes=48 * 1024 * 1024),
+        compiler_params=pltpu.CompilerParams(vmem_limit_bytes=limit),
     )(*args)
 
 
@@ -603,13 +637,11 @@
     return lax.ppermute(first, "gz", pairs), lax.ppermute(second, "gz", others)
 
 
-def sum_all(table):
-    for axis in ("xy", "gz"):
-        distance = 1
-        while distance < lax.axis_size(axis):
-            table = table + swap(table, axis, distance)
-            distance *= 2
-    return table
+def sum_over(table, axis):
+    terms = [table] + [swap(table, axis, m) for m in range(1, lax.axis_size(axis))]
+    while len(terms) > 1:
+        terms = [a + b for a, b in zip(terms[::2], terms[1::2])]
+    return terms[0]
 
 
 def local_columns(
@@ -626,36 +658,48 @@
     bins = bin_weight.shape[0]
     record_kernel, source_kernel = time_kernels(STEPS)
     by_row = np.tile(np.repeat(record_kernel.T, CX * CZ, axis=1), (1, 2))
-    lists = [
-        v.reshape(SUB, LANES) for v in (monitor_cells, monitor_bins, source_cells, source_bins)
-    ]
     n_fwd, n_adj = packed_rows(7), packed_rows(6)
+    hbm = pltpu.HBM
+    listed = pltpu.VMEM(monitor_cells.shape, jnp.int32)
     sent = call(
         pack_forward_kernel,
-        (fields, material_ids, material_eps, lists[0], lists[1]),
+        (fields, material_ids, material_eps, monitor_cells, monitor_bins),
         [struct(ZT * n_fwd + 2, SUB, LANES)] * TILES,
-        [pltpu.VMEM((CX, CZ, TILES * LANES), F32)],
-        scalars=(2,),
-    )
-    adjoint_sent = call(
+        [
+            pltpu.VMEM(fields.shape, F32),
+            pltpu.VMEM(material_ids.shape, jnp.int32),
+            pltpu.SMEM(material_eps.shape, F32),
+            listed,
+            listed,
+            pltpu.VMEM(material_ids.shape, F32),
+            pltpu.SemaphoreType.DMA((5,)),
+        ],
+        places={k: hbm for k in range(5)},
+        limit=None,
+    )
+    *adjoint_sent, weight, back_kernel = call(
         pack_adjoint_kernel,
-        (adjoint_fields, lists[2], lists[3]),
-        [struct(ZT * n_adj + 2, SUB, LANES)] * TILES,
+        (adjoint_fields, source_cells, source_bins, bin_weight.reshape(1, bins), source_kernel),
+        [struct(ZT * n_adj + 2, SUB, LANES)] * TILES
+        + [struct(1, bins), struct(STEPS, 2 * NFREQ)],
+        [pltpu.VMEM(fields.shape, F32), listed, listed, pltpu.SemaphoreType.DMA((3,))],
+        places={k: hbm for k in range(3)},
+        limit=None,
     )
     blocks = swap_blocks(sent)
     slabs = call(
-        functools.partial(slab_kernel, n_fwd, 0), blocks, [struct(TILES * n_fwd, SUB, LANES)] * 2
+        functools.partial(slab_kernel, 7, 0), blocks, [struct(TILES * n_fwd, SUB, LANES)] * 2
     )
     slabs, adjoint_sent = lax.optimization_barrier((slabs, adjoint_sent))
     first, second = swap_neighbours(*slabs)
     adjoint_blocks = swap_blocks(adjoint_sent)
     (first, second), adjoint_blocks = lax.optimization_barrier(((first, second), adjoint_blocks))
     adjoint_slabs = call(
-        functools.partial(slab_kernel, n_adj, 2),
+        functools.partial(slab_kernel, 6, 2),
         adjoint_blocks,
         [struct(TILES * (n_adj + 2), SUB, LANES)] * 2,
     )
-    adjoint_first, adjoint_second = swap_neighbours(*adjoint_slabs)
+    adjoint_edges = swap_neighbours(*adjoint_slabs)
     field = pltpu.VMEM((6, PLANES + 2, 2, ROWS + 2 * PAD, LANES), F32)
     factor = pltpu.VMEM((2, ROWS, LANES), F32)
     *forward_sent, inverse, table = call(
@@ -670,7 +714,8 @@
             pltpu.VMEM((2 * STEPS * CX * CZ, TILES * ENTRIES), BF16),
         ],
     )
-    totals = sum_all(table)
+    table, forward_sent = lax.optimization_barrier((sum_over(table, "xy"), forward_sent))
+    totals = sum_over(table, "gz")
     forward_blocks = swap_blocks(forward_sent)
     own_count = bins // (lax.axis_size("xy") * lax.axis_size("gz"))
     device_rank = lax.axis_index(("xy", "gz"))
@@ -679,12 +724,11 @@
         adjoint_kernel,
         (
             *adjoint_blocks,
-            adjoint_first,
-            adjoint_second,
+            *adjoint_edges,
             inverse,
             totals,
-            bin_weight.reshape(1, bins),
-            source_kernel,
+            weight,
+            back_kernel,
         ),
         [struct(6 * CX * ZT, SUB, LANES)] * TILES,
         [field, factor, pltpu.VMEM((STEPS, PLANES, 2, ROWS, LANES), F32)],

time: 105 us -> 91.6 us (0.87)
  waiting for transfers between devices: 36.4 us -> 29.5 us
  local copies, waits for them, and re-layouts: 5.4 us -> 1.36 us
  Pallas kernels: 36.9 us -> 33 us
  starting transfers between devices: 25.2 us -> 26.6 us
    ppermute x16 -> x18, waiting for transfers between devices: 36.4 us -> 29.5 us  [swap(): return lax.ppermute(value, axis, [(i, i ^ distance) for i in range(count)])]
    unnamed x22 -> x16, local copies, waits for them, and re-layouts: 4.74 us -> 0.7 us
    pallas_call x8, Pallas kernels: 36.9 us -> 33 us  [call(): pl.pallas_call(kernel, out_shape=outs, in_specs=[pl.BlockSpec(memory_spac...]
    ppermute x16 -> x18, starting transfers between devices: 18.1 us -> 19.5 us  [swap(): return lax.ppermute(value, axis, [(i, i ^ distance) for i in range(count)])]
  transfers between devices with their start and end apart: 20 -> 22, of which waited for: 9 -> 8; matrix products, arithmetic and copies ran while one was open for 1% -> 1% of each run, Pallas kernels for 33% -> 32%
where the time goes in v3:
time: 91.6 us; the launch traced here: 91.3 us
  Pallas kernels  33 us (36%)
  waiting for transfers between devices  29.5 us (32%)
  starting transfers between devices  26.6 us (29%)
  local copies, waits for them, and re-layouts  1.36 us (1%)
    pallas_call x8, Pallas kernels, call(): pl.pallas_call(kernel, out_shape=outs, in_specs=[pl.BlockSpec(memory_spac...  33 us
    ppermute x18, waiting for transfers between devices, swap(): return lax.ppermute(value, axis, [(i, i ^ distance) for i in range(count)])  29.5 us
    ppermute x18, starting transfers between devices, swap(): return lax.ppermute(value, axis, [(i, i ^ distance) for i in range(count)])  19.5 us
    ppermute x2, starting transfers between devices, swap_neighbours(): lax.ppermute(first, 'gz', pairs)  5.72 us
  transfers between devices with their start and end apart: 22, of which 8 were waited for; matrix products, arithmetic and copies ran while one was open for 1% of the time, Pallas kernels for 32%

profile of v3, /device:TPU:1, one launch (start us, length us, event | category | flops | bytes accessed | tf_op | source)
XLA Modules:
  0.0 91.3 jit_solution(9537658035383693121)
XLA Ops:
  0.6 2.5 %shard_map.130 = (f32[66,8,128]{2,1,0:T(8,128)}, f32[66,8,128]{2,1,0:T(8,128)}, f32[66,8,128]{2,1,0:T(8,128)}, f32[66,8,128]{2,1,0:T(8,128)}) custom-call(f32[6,4,16,512]{3,2,1,0:T(8,128)} %fields_hbm.2, s32[4,16,512]{2,1,0:T(8,128)} %ids_hbm.1, f32[4]{0:T(128)} %eps_hbm.1, s32[1,1,1024]{2,1,0:T(1,128)} %cells_hbm.2, s32[1,1,1024]{2,1,0:T(1,128)} %bins_hbm.2), custom_call_target="tpu_custom_call" | custom-call | tf_op jit(solution)/shard_map/pallas_call | solution.py:611
  3.3 2.7 %collective-permute-start.1 = (f32[66,8,128]{2,1,0:T(8,128)}, f32[66,8,128]{2,1,0:T(8,128)S(1)}, u32[]{:S(2)}, u32[]{:S(2)}) collective-permute-start(f32[66,8,128]{2,1,0:T(8,128)} %get-tuple-element.46), channel_id=1, source_target_pairs={{0,8},{4,12},{8,0},{12,4},{1,9},{5,13},{9,1},{13,5},{2,10},{6,14},... | collective-permute-start | bytes 811016 | tf_op jit(solution)/shard_map/ppermute | solution.py:625
  6.0 3.1 %shard_map.132 = (f32[56,8,128]{2,1,0:T(8,128)}, f32[56,8,128]{2,1,0:T(8,128)}, f32[56,8,128]{2,1,0:T(8,128)}, f32[56,8,128]{2,1,0:T(8,128)}, f32[1,128]{1,0:T(1,128)}, /*index=5*/f32[8,8]{1,0:T(8,128)}) custom-call(f32[6,4,16,512]{3,2,1,0:T(8,128)} %fields_hbm.3, s32[1,1,1024]{2,1,0:T(1,128)} %cells_hbm.3, s32[1,1,1024]{2,1,0:T(1,128)} %bins_hbm.3, ...), custom_call_target="tpu_custom_call" | custom-call | tf_op jit(solution)/shard_map/pallas_call | solution.py:611
  9.1 3.8 %collective-permute-done.1.b2 = f32[66,8,128]{2,1,0:T(8,128)S(1)} collective-permute-done((f32[66,8,128]{2,1,0:T(8,128)}, f32[66,8,128]{2,1,0:T(8,128)S(1)}, u32[]{:S(2)}, u32[]{:S(2)}) %collective-permute-start.1) | collective-permute-done | bytes 270368 | tf_op jit(solution)/shard_map/ppermute | solution.py:625
  12.9 5.8 %collective-permute-done.2.b3 = f32[66,8,128]{2,1,0:T(8,128)S(1)} collective-permute-done((f32[66,8,128]{2,1,0:T(8,128)}, f32[66,8,128]{2,1,0:T(8,128)S(1)}, u32[]{:S(2)}, u32[]{:S(2)}) %collective-permute-start.2) | collective-permute-done | bytes 270368 | tf_op jit(solution)/shard_map/ppermute | solution.py:625
  18.8 1.6 %collective-permute-start.3 = (f32[128,8,128]{2,1,0:T(8,128)S(1)}, f32[128,8,128]{2,1,0:T(8,128)S(1)}, u32[]{:S(2)}, u32[]{:S(2)}) collective-permute-start(f32[128,8,128]{2,1,0:T(8,128)S(1)} %get-tuple-element.54), channel_id=1, source_target_pairs={{0,1},{1,0},{2,3},{3,2},{4,5},{5,4},{6,7},{7,6},{8,9},{9,8},{10,11... | collective-permute-start | bytes 1572872 | tf_op jit(solution)/shard_map/ppermute | solution.py:637
  21.7 1.3 %collective-permute-start.6 = (f32[56,8,128]{2,1,0:T(8,128)S(1)}, f32[56,8,128]{2,1,0:T(8,128)S(1)}, u32[]{:S(2)}, u32[]{:S(2)}) collective-permute-start(f32[56,8,128]{2,1,0:T(8,128)S(1)} %copy-done.6), channel_id=1, source_target_pairs={{0,8},{4,12},{8,0},{12,4},{1,9},{5,13},{9,1},{13,5},{2,10},{6,14},... | collective-permute-start | bytes 688136 | tf_op jit(solution)/shard_map/ppermute | solution.py:625
  23.4 5.4 %collective-permute-done.6.b2 = f32[56,8,128]{2,1,0:T(8,128)S(1)} collective-permute-done((f32[56,8,128]{2,1,0:T(8,128)S(1)}, f32[56,8,128]{2,1,0:T(8,128)S(1)}, u32[]{:S(2)}, u32[]{:S(2)}) %collective-permute-start.6) | collective-permute-done | bytes 229408 | tf_op jit(solution)/shard_map/ppermute | solution.py:625
  28.9 5.1 %collective-permute-done.7.b3 = f32[56,8,128]{2,1,0:T(8,128)S(1)} collective-permute-done((f32[56,8,128]{2,1,0:T(8,128)S(1)}, f32[56,8,128]{2,1,0:T(8,128)S(1)}, u32[]{:S(2)}, u32[]{:S(2)}) %collective-permute-start.7) | collective-permute-done | bytes 229408 | tf_op jit(solution)/shard_map/ppermute | solution.py:625
  34.0 4.2 %collective-permute-start.14 = (f32[116,8,128]{2,1,0:T(8,128)S(1)}, f32[116,8,128]{2,1,0:T(8,128)S(1)}, u32[]{:S(2)}, u32[]{:S(2)}) collective-permute-start(f32[116,8,128]{2,1,0:T(8,128)S(1)} %get-tuple-element.75), channel_id=1, source_target_pairs={{0,1},{1,0},{2,3},{3,2},{4,5},{5,4},{6,7},{7,6},{8,9},{9,8},{10,11... | collective-permute-start | bytes 1425416 | tf_op jit(solution)/shard_map/ppermute | solution.py:637
  38.9 12.4 %shard_map.133 = (f32[48,8,128]{2,1,0:T(8,128)S(1)}, f32[48,8,128]{2,1,0:T(8,128)S(1)}, f32[48,8,128]{2,1,0:T(8,128)S(1)}, f32[48,8,128]{2,1,0:T(8,128)S(1)}, f3...) custom-call(f32[66,8,128]{2,1,0:T(8,128)S(1)} %copy-done, f32[66,8,128]{2,1,0:T(8,128)S(1)} %collective-permute-done.b1, ...), custom_call_target="tpu_custom_call" | custom-call | tf_op jit(solution)/shard_map/pallas_call | solution.py:611
  51.3 1.7 %collective-permute-start.10 = (f32[8,128]{1,0:T(8,128)S(1)}, f32[8,128]{1,0:T(8,128)S(1)}, u32[]{:S(2)}, u32[]{:S(2)}) collective-permute-start(f32[8,128]{1,0:T(8,128)S(1)} %get-tuple-element.62), channel_id=1, source_target_pairs={{0,12},{4,8},{8,4},{12,0},{1,13},{5,9},{9,5},{13,1},{2,14},{6,10},... | collective-permute-start | bytes 12296 | tf_op jit(solution)/shard_map/ppermute | solution.py:625
  53.2 1.3 %collective-permute-done.10 = f32[8,128]{1,0:T(8,128)S(1)} collective-permute-done((f32[8,128]{1,0:T(8,128)S(1)}, f32[8,128]{1,0:T(8,128)S(1)}, u32[]{:S(2)}, u32[]{:S(2)}) %collective-permute-start.10) | collective-permute-done | bytes 4128 | tf_op jit(solution)/shard_map/ppermute | solution.py:625
  55.5 2.2 %collective-permute-start.16 = (f32[8,128]{1,0:T(8,128)S(1)}, f32[8,128]{1,0:T(8,128)S(1)}, u32[]{:S(2)}, u32[]{:S(2)}) collective-permute-start(f32[8,128]{1,0:T(8,128)S(1)} %add_add_fusion.1), channel_id=1, source_target_pairs={{0,1},{1,0},{2,3},{3,2},{4,5},{5,4},{6,7},{7,6},{8,9},{9,8},{10,11... | collective-permute-start | bytes 12296 | tf_op jit(solution)/shard_map/ppermute | solution.py:625
  57.9 1.8 %collective-permute-start.18 = (f32[8,128]{1,0:T(8,128)S(1)}, f32[8,128]{1,0:T(8,128)S(1)}, u32[]{:S(2)}, u32[]{:S(2)}) collective-permute-start(f32[8,128]{1,0:T(8,128)S(1)} %add_add_fusion.1), channel_id=1, source_target_pairs={{0,3},{1,2},{2,1},{3,0},{4,7},{5,6},{6,5},{7,4},{8,11},{9,10},{10,... | collective-permute-start | bytes 12296 | tf_op jit(solution)/shard_map/ppermute | solution.py:625
  59.8 2.2 %collective-permute-start.11 = (f32[48,8,128]{2,1,0:T(8,128)S(1)}, f32[48,8,128]{2,1,0:T(8,128)S(1)}, u32[]{:S(2)}, u32[]{:S(2)}) collective-permute-start(f32[48,8,128]{2,1,0:T(8,128)S(1)} %get-tuple-element.68), channel_id=1, source_target_pairs={{0,4},{4,0},{8,12},{12,8},{1,5},{5,1},{9,13},{13,9},{2,6},{6,2},{1... | collective-permute-start | bytes 589832 | tf_op jit(solution)/shard_map/ppermute | solution.py:625
  62.3 3.5 %collective-permute-start.13 = (f32[48,8,128]{2,1,0:T(8,128)S(1)}, f32[48,8,128]{2,1,0:T(8,128)S(1)}, u32[]{:S(2)}, u32[]{:S(2)}) collective-permute-start(f32[48,8,128]{2,1,0:T(8,128)S(1)} %get-tuple-element.70), channel_id=1, source_target_pairs={{0,12},{4,8},{8,4},{12,0},{1,13},{5,9},{9,5},{13,1},{2,14},{6,10},... | collective-permute-start | bytes 589832 | tf_op jit(solution)/shard_map/ppermute | solution.py:625
  66.4 12.9 %shard_map.136 = (f32[48,8,128]{2,1,0:T(8,128)S(1)}, f32[48,8,128]{2,1,0:T(8,128)S(1)}, f32[48,8,128]{2,1,0:T(8,128)S(1)}, f32[48,8,128]{2,1,0:T(8,128)S(1)}) custom-call(f32[56,8,128]{2,1,0:T(8,128)S(1)} %copy-done.1, f32[56,8,128]{2,1,0:T(8,128)S(1)} %collective-permute-done.5.b1, f32[56,8,128]{2,1,0:T(8,128)S(1)} %collective-permute-done.6.b2, ...), custom_call_target="tpu_custom_call" | custom-call | tf_op jit(solution)/shard_map/pallas_call | solution.py:611
  79.4 1.0 %collective-permute-start.20 = (f32[48,8,128]{2,1,0:T(8,128)S(1)}, f32[48,8,128]{2,1,0:T(8,128)S(1)}, u32[]{:S(2)}, u32[]{:S(2)}) collective-permute-start(f32[48,8,128]{2,1,0:T(8,128)S(1)} %get-tuple-element.83), channel_id=1, source_target_pairs={{0,8},{4,12},{8,0},{12,4},{1,9},{5,13},{9,1},{13,5},{2,10},{6,14},... | collective-permute-start | bytes 589832 | tf_op jit(solution)/shard_map/ppermute | solution.py:625
  80.4 1.1 %collective-permute-start.21 = (f32[48,8,128]{2,1,0:T(8,128)S(1)}, f32[48,8,128]{2,1,0:T(8,128)S(1)}, u32[]{:S(2)}, u32[]{:S(2)}) collective-permute-start(f32[48,8,128]{2,1,0:T(8,128)S(1)} %get-tuple-element.84), channel_id=1, source_target_pairs={{0,12},{4,8},{8,4},{12,0},{1,13},{5,9},{9,5},{13,1},{2,14},{6,10},... | collective-permute-start | bytes 589832 | tf_op jit(solution)/shard_map/ppermute | solution.py:625
  82.2 1.0 %shard_map.134 = f32[6,4,16,512]{3,2,1,0:T(8,128)} custom-call(f32[48,8,128]{2,1,0:T(8,128)S(1)} %get-tuple-element.67.b0, f32[48,8,128]{2,1,0:T(8,128)S(1)} %collective-permute-done.11.b1, f32[48,8,128]{2,1,0:T(8,128)S(1)} %collective-permute-done.12.b2, f32[48,8,128]{2,1,0:T(8,128)S(1)} %collective-permute-done.13.b3), custom_call_target="tpu_custom_call" | custom-call | tf_op jit(solution)/shard_map/pallas_call | solution.py:611
  83.2 2.3 %collective-permute-done.20.b2 = f32[48,8,128]{2,1,0:T(8,128)S(1)} collective-permute-done((f32[48,8,128]{2,1,0:T(8,128)S(1)}, f32[48,8,128]{2,1,0:T(8,128)S(1)}, u32[]{:S(2)}, u32[]{:S(2)}) %collective-permute-start.20) | collective-permute-done | bytes 196640 | tf_op jit(solution)/shard_map/ppermute | solution.py:625
  85.5 4.8 %collective-permute-done.21.b3 = f32[48,8,128]{2,1,0:T(8,128)S(1)} collective-permute-done((f32[48,8,128]{2,1,0:T(8,128)S(1)}, f32[48,8,128]{2,1,0:T(8,128)S(1)}, u32[]{:S(2)}, u32[]{:S(2)}) %collective-permute-start.21) | collective-permute-done | bytes 196640 | tf_op jit(solution)/shard_map/ppermute | solution.py:625
  90.3 1.0 %shard_map.137 = f32[6,4,16,512]{3,2,1,0:T(8,128)} custom-call(f32[48,8,128]{2,1,0:T(8,128)S(1)} %get-tuple-element.81.b0, f32[48,8,128]{2,1,0:T(8,128)S(1)} %collective-permute-done.19.b1, f32[48,8,128]{2,1,0:T(8,128)S(1)} %collective-permute-done.20.b2, f32[48,8,128]{2,1,0:T(8,128)S(1)} %collective-permute-done.21.b3), custom_call_target="tpu_custom_call" | custom-call | tf_op jit(solution)/shard_map/pallas_call | solution.py:611
  (47 shorter events, 5.9 us)
Async XLA Ops:
  3.1 6.0 %collective-permute-start = (f32[66,8,128]{2,1,0:T(8,128)}, f32[66,8,128]{2,1,0:T(8,128)S(1)}, u32[]{:S(2)}, u32[]{:S(2)}) collective-permute-start(f32[66,8,128]{2,1,0:T(8,128)} %get-tuple-element.45), channel_id=1, source_target_pairs={{0,4},{4,0},{8,12},{12,8},{1,5},{5,1},{9,13},{13,9},{2,6},{6,2},{1... | collective-permute-start | bytes 811016 | tf_op jit(solution)/shard_map/ppermute | solution.py:625
  3.3 9.7 %collective-permute-start.1 = (f32[66,8,128]{2,1,0:T(8,128)}, f32[66,8,128]{2,1,0:T(8,128)S(1)}, u32[]{:S(2)}, u32[]{:S(2)}) collective-permute-start(f32[66,8,128]{2,1,0:T(8,128)} %get-tuple-element.46), channel_id=1, source_target_pairs={{0,8},{4,12},{8,0},{12,4},{1,9},{5,13},{9,1},{13,5},{2,10},{6,14},... | collective-permute-start | bytes 811016 | tf_op jit(solution)/shard_map/ppermute | solution.py:625
  6.0 12.8 %collective-permute-start.2 = (f32[66,8,128]{2,1,0:T(8,128)}, f32[66,8,128]{2,1,0:T(8,128)S(1)}, u32[]{:S(2)}, u32[]{:S(2)}) collective-permute-start(f32[66,8,128]{2,1,0:T(8,128)} %get-tuple-element.47), channel_id=1, source_target_pairs={{0,12},{4,8},{8,4},{12,0},{1,13},{5,9},{9,5},{13,1},{2,14},{6,10},... | collective-permute-start | bytes 811016 | tf_op jit(solution)/shard_map/ppermute | solution.py:625
  18.7 15.2 %copy-start.1 = (f32[56,8,128]{2,1,0:T(8,128)S(1)}, f32[56,8,128]{2,1,0:T(8,128)}, u32[]{:S(2)}) copy-start(f32[56,8,128]{2,1,0:T(8,128)} %get-tuple-element.71.b0) | copy-start | bytes 688132
  18.8 20.1 %copy-start.2 = (f32[8,1024]{1,0:T(8,128)S(1)}, f32[8,1024]{1,0:T(8,128)}, u32[]{:S(2)}) copy-start(f32[8,1024]{1,0:T(8,128)} %constant.20.clone.kernel_ref) | copy-start | bytes 98308
  18.8 15.1 %collective-permute-start.3 = (f32[128,8,128]{2,1,0:T(8,128)S(1)}, f32[128,8,128]{2,1,0:T(8,128)S(1)}, u32[]{:S(2)}, u32[]{:S(2)}) collective-permute-start(f32[128,8,128]{2,1,0:T(8,128)S(1)} %get-tuple-element.54), channel_id=1, source_target_pairs={{0,1},{1,0},{2,3},{3,2},{4,5},{5,4},{6,7},{7,6},{8,9},{9,8},{10,11... | collective-permute-start | bytes 1572872 | tf_op jit(solution)/shard_map/ppermute | solution.py:637
  20.4 13.5 %collective-permute-start.4 = (f32[128,8,128]{2,1,0:T(8,128)S(1)}, f32[128,8,128]{2,1,0:T(8,128)S(1)}, u32[]{:S(2)}, u32[]{:S(2)}) collective-permute-start(f32[128,8,128]{2,1,0:T(8,128)S(1)} %get-tuple-element.55), channel_id=1, source_target_pairs={{1,2},{2,1},{5,6},{6,5},{9,10},{10,9},{13,14},{14,13},{17,18},{18,... | collective-permute-start | bytes 1572872 | tf_op jit(solution)/shard_map/ppermute | solution.py:637
  21.1 2.3 %collective-permute-start.5 = (f32[56,8,128]{2,1,0:T(8,128)S(1)}, f32[56,8,128]{2,1,0:T(8,128)S(1)}, u32[]{:S(2)}, u32[]{:S(2)}) collective-permute-start(f32[56,8,128]{2,1,0:T(8,128)S(1)} %copy-done.7), channel_id=1, source_target_pairs={{0,4},{4,0},{8,12},{12,8},{1,5},{5,1},{9,13},{13,9},{2,6},{6,2},{1... | collective-permute-start | bytes 688136 | tf_op jit(solution)/shard_map/ppermute | solution.py:625
  21.7 7.2 %collective-permute-start.6 = (f32[56,8,128]{2,1,0:T(8,128)S(1)}, f32[56,8,128]{2,1,0:T(8,128)S(1)}, u32[]{:S(2)}, u32[]{:S(2)}) collective-permute-start(f32[56,8,128]{2,1,0:T(8,128)S(1)} %copy-done.6), channel_id=1, source_target_pairs={{0,8},{4,12},{8,0},{12,4},{1,9},{5,13},{9,1},{13,5},{2,10},{6,14},... | collective-permute-start | bytes 688136 | tf_op jit(solution)/shard_map/ppermute | solution.py:625
  23.0 11.0 %collective-permute-start.7 = (f32[56,8,128]{2,1,0:T(8,128)S(1)}, f32[56,8,128]{2,1,0:T(8,128)S(1)}, u32[]{:S(2)}, u32[]{:S(2)}) collective-permute-start(f32[56,8,128]{2,1,0:T(8,128)S(1)} %copy-done.5), channel_id=1, source_target_pairs={{0,12},{4,8},{8,4},{12,0},{1,13},{5,9},{9,5},{13,1},{2,14},{6,10},... | collective-permute-start | bytes 688136 | tf_op jit(solution)/shard_map/ppermute | solution.py:625
  34.0 31.7 %collective-permute-start.14 = (f32[116,8,128]{2,1,0:T(8,128)S(1)}, f32[116,8,128]{2,1,0:T(8,128)S(1)}, u32[]{:S(2)}, u32[]{:S(2)}) collective-permute-start(f32[116,8,128]{2,1,0:T(8,128)S(1)} %get-tuple-element.75), channel_id=1, source_target_pairs={{0,1},{1,0},{2,3},{3,2},{4,5},{5,4},{6,7},{7,6},{8,9},{9,8},{10,11... | collective-permute-start | bytes 1425416 | tf_op jit(solution)/shard_map/ppermute | solution.py:637
  38.2 27.5 %collective-permute-start.15 = (f32[116,8,128]{2,1,0:T(8,128)S(1)}, f32[116,8,128]{2,1,0:T(8,128)S(1)}, u32[]{:S(2)}, u32[]{:S(2)}) collective-permute-start(f32[116,8,128]{2,1,0:T(8,128)S(1)} %get-tuple-element.76), channel_id=1, source_target_pairs={{1,2},{2,1},{5,6},{6,5},{9,10},{10,9},{13,14},{14,13},{17,18},{18,... | collective-permute-start | bytes 1425416 | tf_op jit(solution)/shard_map/ppermute | solution.py:637
  51.3 3.2 %collective-permute-start.10 = (f32[8,128]{1,0:T(8,128)S(1)}, f32[8,128]{1,0:T(8,128)S(1)}, u32[]{:S(2)}, u32[]{:S(2)}) collective-permute-start(f32[8,128]{1,0:T(8,128)S(1)} %get-tuple-element.62), channel_id=1, source_target_pairs={{0,12},{4,8},{8,4},{12,0},{1,13},{5,9},{9,5},{13,1},{2,14},{6,10},... | collective-permute-start | bytes 12296 | tf_op jit(solution)/shard_map/ppermute | solution.py:625
  53.0 1.5 %collective-permute-start.8 = (f32[8,128]{1,0:T(8,128)S(1)}, f32[8,128]{1,0:T(8,128)S(1)}, u32[]{:S(2)}, u32[]{:S(2)}) collective-permute-start(f32[8,128]{1,0:T(8,128)S(1)} %get-tuple-element.62), channel_id=1, source_target_pairs={{0,4},{4,0},{8,12},{12,8},{1,5},{5,1},{9,13},{13,9},{2,6},{6,2},{1... | collective-permute-start | bytes 12296 | tf_op jit(solution)/shard_map/ppermute | solution.py:625
  53.0 2.5 %collective-permute-start.9 = (f32[8,128]{1,0:T(8,128)S(1)}, f32[8,128]{1,0:T(8,128)S(1)}, u32[]{:S(2)}, u32[]{:S(2)}) collective-permute-start(f32[8,128]{1,0:T(8,128)S(1)} %get-tuple-element.62), channel_id=1, source_target_pairs={{0,8},{4,12},{8,0},{12,4},{1,9},{5,13},{9,1},{13,5},{2,10},{6,14},... | collective-permute-start | bytes 12296 | tf_op jit(solution)/shard_map/ppermute | solution.py:625
  55.5 4.3 %collective-permute-start.16 = (f32[8,128]{1,0:T(8,128)S(1)}, f32[8,128]{1,0:T(8,128)S(1)}, u32[]{:S(2)}, u32[]{:S(2)}) collective-permute-start(f32[8,128]{1,0:T(8,128)S(1)} %add_add_fusion.1), channel_id=1, source_target_pairs={{0,1},{1,0},{2,3},{3,2},{4,5},{5,4},{6,7},{7,6},{8,9},{9,8},{10,11... | collective-permute-start | bytes 12296 | tf_op jit(solution)/shard_map/ppermute | solution.py:625
  57.6 4.4 %collective-permute-start.17 = (f32[8,128]{1,0:T(8,128)S(1)}, f32[8,128]{1,0:T(8,128)S(1)}, u32[]{:S(2)}, u32[]{:S(2)}) collective-permute-start(f32[8,128]{1,0:T(8,128)S(1)} %add_add_fusion.1), channel_id=1, source_target_pairs={{0,2},{1,3},{2,0},{3,1},{4,6},{5,7},{6,4},{7,5},{8,10},{9,11},{10,... | collective-permute-start | bytes 12296 | tf_op jit(solution)/shard_map/ppermute | solution.py:625
  57.9 4.3 %collective-permute-start.18 = (f32[8,128]{1,0:T(8,128)S(1)}, f32[8,128]{1,0:T(8,128)S(1)}, u32[]{:S(2)}, u32[]{:S(2)}) collective-permute-start(f32[8,128]{1,0:T(8,128)S(1)} %add_add_fusion.1), channel_id=1, source_target_pairs={{0,3},{1,2},{2,1},{3,0},{4,7},{5,6},{6,5},{7,4},{8,11},{9,10},{10,... | collective-permute-start | bytes 12296 | tf_op jit(solution)/shard_map/ppermute | solution.py:625
  59.8 20.6 %collective-permute-start.11 = (f32[48,8,128]{2,1,0:T(8,128)S(1)}, f32[48,8,128]{2,1,0:T(8,128)S(1)}, u32[]{:S(2)}, u32[]{:S(2)}) collective-permute-start(f32[48,8,128]{2,1,0:T(8,128)S(1)} %get-tuple-element.68), channel_id=1, source_target_pairs={{0,4},{4,0},{8,12},{12,8},{1,5},{5,1},{9,13},{13,9},{2,6},{6,2},{1... | collective-permute-start | bytes 589832 | tf_op jit(solution)/shard_map/ppermute | solution.py:625
  62.0 20.2 %collective-permute-start.12 = (f32[48,8,128]{2,1,0:T(8,128)S(1)}, f32[48,8,128]{2,1,0:T(8,128)S(1)}, u32[]{:S(2)}, u32[]{:S(2)}) collective-permute-start(f32[48,8,128]{2,1,0:T(8,128)S(1)} %get-tuple-element.69), channel_id=1, source_target_pairs={{0,8},{4,12},{8,0},{12,4},{1,9},{5,13},{9,1},{13,5},{2,10},{6,14},... | collective-permute-start | bytes 589832 | tf_op jit(solution)/shard_map/ppermute | solution.py:625
  62.3 19.9 %collective-permute-start.13 = (f32[48,8,128]{2,1,0:T(8,128)S(1)}, f32[48,8,128]{2,1,0:T(8,128)S(1)}, u32[]{:S(2)}, u32[]{:S(2)}) collective-permute-start(f32[48,8,128]{2,1,0:T(8,128)S(1)} %get-tuple-element.70), channel_id=1, source_target_pairs={{0,12},{4,8},{8,4},{12,0},{1,13},{5,9},{9,5},{13,1},{2,14},{6,10},... | collective-permute-start | bytes 589832 | tf_op jit(solution)/shard_map/ppermute | solution.py:625
  79.3 3.9 %collective-permute-start.19 = (f32[48,8,128]{2,1,0:T(8,128)S(1)}, f32[48,8,128]{2,1,0:T(8,128)S(1)}, u32[]{:S(2)}, u32[]{:S(2)}) collective-permute-start(f32[48,8,128]{2,1,0:T(8,128)S(1)} %get-tuple-element.82), channel_id=1, source_target_pairs={{0,4},{4,0},{8,12},{12,8},{1,5},{5,1},{9,13},{13,9},{2,6},{6,2},{1... | collective-permute-start | bytes 589832 | tf_op jit(solution)/shard_map/ppermute | solution.py:625
  79.4 6.1 %collective-permute-start.20 = (f32[48,8,128]{2,1,0:T(8,128)S(1)}, f32[48,8,128]{2,1,0:T(8,128)S(1)}, u32[]{:S(2)}, u32[]{:S(2)}) collective-permute-start(f32[48,8,128]{2,1,0:T(8,128)S(1)} %get-tuple-element.83), channel_id=1, source_target_pairs={{0,8},{4,12},{8,0},{12,4},{1,9},{5,13},{9,1},{13,5},{2,10},{6,14},... | collective-permute-start | bytes 589832 | tf_op jit(solution)/shard_map/ppermute | solution.py:625
  80.4 9.9 %collective-permute-start.21 = (f32[48,8,128]{2,1,0:T(8,128)S(1)}, f32[48,8,128]{2,1,0:T(8,128)S(1)}, u32[]{:S(2)}, u32[]{:S(2)}) collective-permute-start(f32[48,8,128]{2,1,0:T(8,128)S(1)} %get-tuple-element.84), channel_id=1, source_target_pairs={{0,12},{4,8},{8,4},{12,0},{1,13},{5,9},{9,5},{13,1},{2,14},{6,10},... | collective-permute-start | bytes 589832 | tf_op jit(solution)/shard_map/ppermute | solution.py:625
  (6 other events, 23.7 us)

commit v4 on v3

--- a/solution.py
+++ b/solution.py
@@ -446,7 +446,7 @@
 
 
 def forward_kernel(
-    b0, b1, b2, b3, first_ref, second_ref, kernel_ref,
+    b0, b1, b2, b3, first_ref, second_ref, kernel_ref, token_ref,
     o0, o1, o2, o3, inverse_ref, table_ref,
     f, factor_ref, record_ref, picked_ref,
 ):
@@ -690,21 +690,20 @@
     slabs = call(
         functools.partial(slab_kernel, 7, 0), blocks, [struct(TILES * n_fwd, SUB, LANES)] * 2
     )
-    slabs, adjoint_sent = lax.optimization_barrier((slabs, adjoint_sent))
     first, second = swap_neighbours(*slabs)
     adjoint_blocks = swap_blocks(adjoint_sent)
-    (first, second), adjoint_blocks = lax.optimization_barrier(((first, second), adjoint_blocks))
     adjoint_slabs = call(
         functools.partial(slab_kernel, 6, 2),
         adjoint_blocks,
         [struct(TILES * (n_adj + 2), SUB, LANES)] * 2,
     )
     adjoint_edges = swap_neighbours(*adjoint_slabs)
+    token = swap(adjoint_slabs[0], "xy", 1)
     field = pltpu.VMEM((6, PLANES + 2, 2, ROWS + 2 * PAD, LANES), F32)
     factor = pltpu.VMEM((2, ROWS, LANES), F32)
     *forward_sent, inverse, table = call(
         forward_kernel,
-        (*blocks, first, second, by_row),
+        (*blocks, first, second, by_row, token),
         [struct(6 * CX * ZT, SUB, LANES)] * TILES
         + [struct(PLANES + 2, 2, ROWS, LANES), struct(2 * NFREQ, bins)],
         [
@@ -713,6 +712,7 @@
             pltpu.VMEM((TILES, 2, STEPS, CX, CZ, LANES), BF16),
             pltpu.VMEM((2 * STEPS * CX * CZ, TILES * ENTRIES), BF16),
         ],
+        places={7: hbm},
     )
     table, forward_sent = lax.optimization_barrier((sum_over(table, "xy"), forward_sent))
     totals = sum_over(table, "gz")

time: 91.6 us -> 88.7 us (0.968)
  waiting for transfers between devices: 29.5 us -> 26.5 us
    ppermute x18 -> x19, waiting for transfers between devices: 29.5 us -> 24.8 us  [swap(): return lax.ppermute(value, axis, [(i, i ^ distance) for i in range(count)])]
    ppermute x18 -> x19, starting transfers between devices: 19.5 us -> 22.2 us  [swap(): return lax.ppermute(value, axis, [(i, i ^ distance) for i in range(count)])]
    ppermute x2, starting transfers between devices: 5.72 us -> 3.28 us  [swap_neighbours(): lax.ppermute(first, 'gz', pairs)]
    ppermute x2, waiting for transfers between devices: 0.01 us -> 1.65 us  [swap_neighbours(): lax.ppermute(first, 'gz', pairs)]
  transfers between devices with their start and end apart: 22 -> 23, of which waited for: 8 -> 9; matrix products, arithmetic and copies ran while one was open for 1% -> 1% of each run, Pallas kernels for 32% -> 33%
where the time goes in v4:
time: 88.7 us; the launch traced here: 88.4 us
  Pallas kernels  33 us (37%)
  starting transfers between devices  26.9 us (30%)
  waiting for transfers between devices  26.5 us (30%)
  local copies, waits for them, and re-layouts  1.34 us (2%)
    pallas_call x8, Pallas kernels, call(): pl.pallas_call(kernel, out_shape=outs, in_specs=[pl.BlockSpec(memory_spac...  33 us
    ppermute x19, waiting for transfers between devices, swap(): return lax.ppermute(value, axis, [(i, i ^ distance) for i in range(count)])  24.8 us
    ppermute x19, starting transfers between devices, swap(): return lax.ppermute(value, axis, [(i, i ^ distance) for i in range(count)])  22.2 us
    ppermute x2, starting transfers between devices, swap_neighbours(): lax.ppermute(first, 'gz', pairs)  3.28 us
  transfers between devices with their start and end apart: 23, of which 9 were waited for; matrix products, arithmetic and copies ran while one was open for 1% of the time, Pallas kernels for 33%

profile of v4, /device:TPU:1, one launch (start us, length us, event | category | flops | bytes accessed | tf_op | source)
XLA Modules:
  0.0 88.4 jit_solution(10675341160668400613)
XLA Ops:
  0.6 2.5 %shard_map.130 = (f32[66,8,128]{2,1,0:T(8,128)}, f32[66,8,128]{2,1,0:T(8,128)}, f32[66,8,128]{2,1,0:T(8,128)}, f32[66,8,128]{2,1,0:T(8,128)}) custom-call(f32[6,4,16,512]{3,2,1,0:T(8,128)} %fields_hbm.2, s32[4,16,512]{2,1,0:T(8,128)} %ids_hbm.1, f32[4]{0:T(128)} %eps_hbm.1, s32[1,1,1024]{2,1,0:T(1,128)} %cells_hbm.2, s32[1,1,1024]{2,1,0:T(1,128)} %bins_hbm.2), custom_call_target="tpu_custom_call" | custom-call | tf_op jit(solution)/shard_map/pallas_call | solution.py:611
  3.2 2.7 %collective-permute-start.1 = (f32[66,8,128]{2,1,0:T(8,128)}, f32[66,8,128]{2,1,0:T(8,128)S(1)}, u32[]{:S(2)}, u32[]{:S(2)}) collective-permute-start(f32[66,8,128]{2,1,0:T(8,128)} %get-tuple-element.34), channel_id=1, source_target_pairs={{0,8},{4,12},{8,0},{12,4},{1,9},{5,13},{9,1},{13,5},{2,10},{6,14},... | collective-permute-start | bytes 811016 | tf_op jit(solution)/shard_map/ppermute | solution.py:625
  6.0 3.1 %shard_map.132 = (f32[56,8,128]{2,1,0:T(8,128)}, f32[56,8,128]{2,1,0:T(8,128)}, f32[56,8,128]{2,1,0:T(8,128)}, f32[56,8,128]{2,1,0:T(8,128)}, f32[1,128]{1,0:T(1,128)}, /*index=5*/f32[8,8]{1,0:T(8,128)}) custom-call(f32[6,4,16,512]{3,2,1,0:T(8,128)} %fields_hbm.3, s32[1,1,1024]{2,1,0:T(1,128)} %cells_hbm.3, s32[1,1,1024]{2,1,0:T(1,128)} %bins_hbm.3, ...), custom_call_target="tpu_custom_call" | custom-call | tf_op jit(solution)/shard_map/pallas_call | solution.py:611
  9.5 1.4 %collective-permute-start.6 = (f32[56,8,128]{2,1,0:T(8,128)}, f32[56,8,128]{2,1,0:T(8,128)S(1)}, u32[]{:S(2)}, u32[]{:S(2)}) collective-permute-start(f32[56,8,128]{2,1,0:T(8,128)} %get-tuple-element.40), channel_id=1, source_target_pairs={{0,8},{4,12},{8,0},{12,4},{1,9},{5,13},{9,1},{13,5},{2,10},{6,14},... | collective-permute-start | bytes 688136 | tf_op jit(solution)/shard_map/ppermute | solution.py:625
  11.3 1.6 %collective-permute-done.1.b2 = f32[66,8,128]{2,1,0:T(8,128)S(1)} collective-permute-done((f32[66,8,128]{2,1,0:T(8,128)}, f32[66,8,128]{2,1,0:T(8,128)S(1)}, u32[]{:S(2)}, u32[]{:S(2)}) %collective-permute-start.1) | collective-permute-done | bytes 270368 | tf_op jit(solution)/shard_map/ppermute | solution.py:625
  12.9 6.0 %collective-permute-done.2.b3 = f32[66,8,128]{2,1,0:T(8,128)S(1)} collective-permute-done((f32[66,8,128]{2,1,0:T(8,128)}, f32[66,8,128]{2,1,0:T(8,128)S(1)}, u32[]{:S(2)}, u32[]{:S(2)}) %collective-permute-start.2) | collective-permute-done | bytes 270368 | tf_op jit(solution)/shard_map/ppermute | solution.py:625
  19.0 1.8 %collective-permute-start.3 = (f32[128,8,128]{2,1,0:T(8,128)S(1)}, f32[128,8,128]{2,1,0:T(8,128)S(1)}, u32[]{:S(2)}, u32[]{:S(2)}) collective-permute-start(f32[128,8,128]{2,1,0:T(8,128)S(1)} %get-tuple-element.36), channel_id=1, source_target_pairs={{0,1},{1,0},{2,3},{3,2},{4,5},{5,4},{6,7},{7,6},{8,9},{9,8},{10,11... | collective-permute-start | bytes 1572872 | tf_op jit(solution)/shard_map/ppermute | solution.py:637
  21.5 2.1 %collective-permute-done.6.b2 = f32[56,8,128]{2,1,0:T(8,128)S(1)} collective-permute-done((f32[56,8,128]{2,1,0:T(8,128)}, f32[56,8,128]{2,1,0:T(8,128)S(1)}, u32[]{:S(2)}, u32[]{:S(2)}) %collective-permute-start.6) | collective-permute-done | bytes 229408 | tf_op jit(solution)/shard_map/ppermute | solution.py:625
  23.6 5.2 %collective-permute-done.7.b3 = f32[56,8,128]{2,1,0:T(8,128)S(1)} collective-permute-done((f32[56,8,128]{2,1,0:T(8,128)}, f32[56,8,128]{2,1,0:T(8,128)S(1)}, u32[]{:S(2)}, u32[]{:S(2)}) %collective-permute-start.7) | collective-permute-done | bytes 229408 | tf_op jit(solution)/shard_map/ppermute | solution.py:625
  29.1 1.5 %collective-permute-start.15 = (f32[116,8,128]{2,1,0:T(8,128)S(1)}, f32[116,8,128]{2,1,0:T(8,128)S(1)}, u32[]{:S(2)}, u32[]{:S(2)}) collective-permute-start(f32[116,8,128]{2,1,0:T(8,128)S(1)} %get-tuple-element.42), channel_id=1, source_target_pairs={{0,1},{1,0},{2,3},{3,2},{4,5},{5,4},{6,7},{7,6},{8,9},{9,8},{10,11... | collective-permute-start | bytes 1425416 | tf_op jit(solution)/shard_map/ppermute | solution.py:637
  31.3 1.7 %collective-permute-done.3.first_ref = f32[128,8,128]{2,1,0:T(8,128)S(1)} collective-permute-done((f32[128,8,128]{2,1,0:T(8,128)S(1)}, f32[128,8,128]{2,1,0:T(8,128)S(1)}, u32[]{:S(2)}, u32[]{:S(2)}) %collective-permute-start.3) | collective-permute-done | bytes 524320 | tf_op jit(solution)/shard_map/ppermute | solution.py:637
  32.9 12.4 %shard_map.134 = (f32[48,8,128]{2,1,0:T(8,128)S(1)}, f32[48,8,128]{2,1,0:T(8,128)S(1)}, f32[48,8,128]{2,1,0:T(8,128)S(1)}, f32[48,8,128]{2,1,0:T(8,128)S(1)}, f3...) custom-call(f32[66,8,128]{2,1,0:T(8,128)S(1)} %copy-done, f32[66,8,128]{2,1,0:T(8,128)S(1)} %collective-permute-done.b1, ...), custom_call_target="tpu_custom_call" | custom-call | tf_op jit(solution)/shard_map/pallas_call | solution.py:611
  45.3 1.6 %collective-permute-start.10 = (f32[8,128]{1,0:T(8,128)S(1)}, f32[8,128]{1,0:T(8,128)S(1)}, u32[]{:S(2)}, u32[]{:S(2)}) collective-permute-start(f32[8,128]{1,0:T(8,128)S(1)} %get-tuple-element.43), channel_id=1, source_target_pairs={{0,8},{4,12},{8,0},{12,4},{1,9},{5,13},{9,1},{13,5},{2,10},{6,14},... | collective-permute-start | bytes 12296 | tf_op jit(solution)/shard_map/ppermute | solution.py:625
  46.9 1.2 %collective-permute-start.11 = (f32[8,128]{1,0:T(8,128)S(1)}, f32[8,128]{1,0:T(8,128)S(1)}, u32[]{:S(2)}, u32[]{:S(2)}) collective-permute-start(f32[8,128]{1,0:T(8,128)S(1)} %get-tuple-element.43), channel_id=1, source_target_pairs={{0,12},{4,8},{8,4},{12,0},{1,13},{5,9},{9,5},{13,1},{2,14},{6,10},... | collective-permute-start | bytes 12296 | tf_op jit(solution)/shard_map/ppermute | solution.py:625
  48.2 1.8 %collective-permute-done.11 = f32[8,128]{1,0:T(8,128)S(1)} collective-permute-done((f32[8,128]{1,0:T(8,128)S(1)}, f32[8,128]{1,0:T(8,128)S(1)}, u32[]{:S(2)}, u32[]{:S(2)}) %collective-permute-start.11) | collective-permute-done | bytes 4128 | tf_op jit(solution)/shard_map/ppermute | solution.py:625
  50.0 4.4 %collective-permute-start.17 = (f32[8,128]{1,0:T(8,128)S(1)}, f32[8,128]{1,0:T(8,128)S(1)}, u32[]{:S(2)}, u32[]{:S(2)}) collective-permute-start(f32[8,128]{1,0:T(8,128)S(1)} %add_add_fusion.1), channel_id=1, source_target_pairs={{0,1},{1,0},{2,3},{3,2},{4,5},{5,4},{6,7},{7,6},{8,9},{9,8},{10,11... | collective-permute-start | bytes 12296 | tf_op jit(solution)/shard_map/ppermute | solution.py:625
  54.3 1.3 %collective-permute-start.18 = (f32[8,128]{1,0:T(8,128)S(1)}, f32[8,128]{1,0:T(8,128)S(1)}, u32[]{:S(2)}, u32[]{:S(2)}) collective-permute-start(f32[8,128]{1,0:T(8,128)S(1)} %add_add_fusion.1), channel_id=1, source_target_pairs={{0,2},{1,3},{2,0},{3,1},{4,6},{5,7},{6,4},{7,5},{8,10},{9,11},{10,... | collective-permute-start | bytes 12296 | tf_op jit(solution)/shard_map/ppermute | solution.py:625
  55.7 1.1 %collective-permute-start.19 = (f32[8,128]{1,0:T(8,128)S(1)}, f32[8,128]{1,0:T(8,128)S(1)}, u32[]{:S(2)}, u32[]{:S(2)}) collective-permute-start(f32[8,128]{1,0:T(8,128)S(1)} %add_add_fusion.1), channel_id=1, source_target_pairs={{0,3},{1,2},{2,1},{3,0},{4,7},{5,6},{6,5},{7,4},{8,11},{9,10},{10,... | collective-permute-start | bytes 12296 | tf_op jit(solution)/shard_map/ppermute | solution.py:625
  56.8 1.8 %collective-permute-start.12 = (f32[48,8,128]{2,1,0:T(8,128)S(1)}, f32[48,8,128]{2,1,0:T(8,128)S(1)}, u32[]{:S(2)}, u32[]{:S(2)}) collective-permute-start(f32[48,8,128]{2,1,0:T(8,128)S(1)} %get-tuple-element.49), channel_id=1, source_target_pairs={{0,4},{4,0},{8,12},{12,8},{1,5},{5,1},{9,13},{13,9},{2,6},{6,2},{1... | collective-permute-start | bytes 589832 | tf_op jit(solution)/shard_map/ppermute | solution.py:625
  59.9 2.9 %collective-permute-start.14 = (f32[48,8,128]{2,1,0:T(8,128)S(1)}, f32[48,8,128]{2,1,0:T(8,128)S(1)}, u32[]{:S(2)}, u32[]{:S(2)}) collective-permute-start(f32[48,8,128]{2,1,0:T(8,128)S(1)} %get-tuple-element.51), channel_id=1, source_target_pairs={{0,12},{4,8},{8,4},{12,0},{1,13},{5,9},{9,5},{13,1},{2,14},{6,10},... | collective-permute-start | bytes 589832 | tf_op jit(solution)/shard_map/ppermute | solution.py:625
  63.5 12.9 %shard_map.136 = (f32[48,8,128]{2,1,0:T(8,128)S(1)}, f32[48,8,128]{2,1,0:T(8,128)S(1)}, f32[48,8,128]{2,1,0:T(8,128)S(1)}, f32[48,8,128]{2,1,0:T(8,128)S(1)}) custom-call(f32[56,8,128]{2,1,0:T(8,128)S(1)} %copy-done.1, f32[56,8,128]{2,1,0:T(8,128)S(1)} %collective-permute-done.5.b1, f32[56,8,128]{2,1,0:T(8,128)S(1)} %collective-permute-done.6.b2, ...), custom_call_target="tpu_custom_call" | custom-call | tf_op jit(solution)/shard_map/pallas_call | solution.py:611
  76.5 1.2 %collective-permute-start.21 = (f32[48,8,128]{2,1,0:T(8,128)S(1)}, f32[48,8,128]{2,1,0:T(8,128)S(1)}, u32[]{:S(2)}, u32[]{:S(2)}) collective-permute-start(f32[48,8,128]{2,1,0:T(8,128)S(1)} %get-tuple-element.59), channel_id=1, source_target_pairs={{0,8},{4,12},{8,0},{12,4},{1,9},{5,13},{9,1},{13,5},{2,10},{6,14},... | collective-permute-start | bytes 589832 | tf_op jit(solution)/shard_map/ppermute | solution.py:625
  80.3 2.3 %collective-permute-done.21.b2 = f32[48,8,128]{2,1,0:T(8,128)S(1)} collective-permute-done((f32[48,8,128]{2,1,0:T(8,128)S(1)}, f32[48,8,128]{2,1,0:T(8,128)S(1)}, u32[]{:S(2)}, u32[]{:S(2)}) %collective-permute-start.21) | collective-permute-done | bytes 196640 | tf_op jit(solution)/shard_map/ppermute | solution.py:625
  82.6 4.8 %collective-permute-done.22.b3 = f32[48,8,128]{2,1,0:T(8,128)S(1)} collective-permute-done((f32[48,8,128]{2,1,0:T(8,128)S(1)}, f32[48,8,128]{2,1,0:T(8,128)S(1)}, u32[]{:S(2)}, u32[]{:S(2)}) %collective-permute-start.22) | collective-permute-done | bytes 196640 | tf_op jit(solution)/shard_map/ppermute | solution.py:625
  (43 shorter events, 8.3 us)
Async XLA Ops:
  3.1 7.8 %collective-permute-start = (f32[66,8,128]{2,1,0:T(8,128)}, f32[66,8,128]{2,1,0:T(8,128)S(1)}, u32[]{:S(2)}, u32[]{:S(2)}) collective-permute-start(f32[66,8,128]{2,1,0:T(8,128)} %get-tuple-element.33), channel_id=1, source_target_pairs={{0,4},{4,0},{8,12},{12,8},{1,5},{5,1},{9,13},{13,9},{2,6},{6,2},{1... | collective-permute-start | bytes 811016 | tf_op jit(solution)/shard_map/ppermute | solution.py:625
  3.2 9.7 %collective-permute-start.1 = (f32[66,8,128]{2,1,0:T(8,128)}, f32[66,8,128]{2,1,0:T(8,128)S(1)}, u32[]{:S(2)}, u32[]{:S(2)}) collective-permute-start(f32[66,8,128]{2,1,0:T(8,128)} %get-tuple-element.34), channel_id=1, source_target_pairs={{0,8},{4,12},{8,0},{12,4},{1,9},{5,13},{9,1},{13,5},{2,10},{6,14},... | collective-permute-start | bytes 811016 | tf_op jit(solution)/shard_map/ppermute | solution.py:625
  5.9 13.0 %collective-permute-start.2 = (f32[66,8,128]{2,1,0:T(8,128)}, f32[66,8,128]{2,1,0:T(8,128)S(1)}, u32[]{:S(2)}, u32[]{:S(2)}) collective-permute-start(f32[66,8,128]{2,1,0:T(8,128)} %get-tuple-element.35), channel_id=1, source_target_pairs={{0,12},{4,8},{8,4},{12,0},{1,13},{5,9},{9,5},{13,1},{2,14},{6,10},... | collective-permute-start | bytes 811016 | tf_op jit(solution)/shard_map/ppermute | solution.py:625
  6.0 13.0 %copy-start = (f32[66,8,128]{2,1,0:T(8,128)S(1)}, f32[66,8,128]{2,1,0:T(8,128)}, u32[]{:S(2)}) copy-start(f32[66,8,128]{2,1,0:T(8,128)} %get-tuple-element.32.b0) | copy-start | bytes 811012
  9.1 12.4 %collective-permute-start.5 = (f32[56,8,128]{2,1,0:T(8,128)}, f32[56,8,128]{2,1,0:T(8,128)S(1)}, u32[]{:S(2)}, u32[]{:S(2)}) collective-permute-start(f32[56,8,128]{2,1,0:T(8,128)} %get-tuple-element.39), channel_id=1, source_target_pairs={{0,4},{4,0},{8,12},{12,8},{1,5},{5,1},{9,13},{13,9},{2,6},{6,2},{1... | collective-permute-start | bytes 688136 | tf_op jit(solution)/shard_map/ppermute | solution.py:625
  9.5 14.1 %collective-permute-start.6 = (f32[56,8,128]{2,1,0:T(8,128)}, f32[56,8,128]{2,1,0:T(8,128)S(1)}, u32[]{:S(2)}, u32[]{:S(2)}) collective-permute-start(f32[56,8,128]{2,1,0:T(8,128)} %get-tuple-element.40), channel_id=1, source_target_pairs={{0,8},{4,12},{8,0},{12,4},{1,9},{5,13},{9,1},{13,5},{2,10},{6,14},... | collective-permute-start | bytes 688136 | tf_op jit(solution)/shard_map/ppermute | solution.py:625
  11.0 17.8 %collective-permute-start.7 = (f32[56,8,128]{2,1,0:T(8,128)}, f32[56,8,128]{2,1,0:T(8,128)S(1)}, u32[]{:S(2)}, u32[]{:S(2)}) collective-permute-start(f32[56,8,128]{2,1,0:T(8,128)} %get-tuple-element.41), channel_id=1, source_target_pairs={{0,12},{4,8},{8,4},{12,0},{1,13},{5,9},{9,5},{13,1},{2,14},{6,10},... | collective-permute-start | bytes 688136 | tf_op jit(solution)/shard_map/ppermute | solution.py:625
  19.0 13.9 %collective-permute-start.3 = (f32[128,8,128]{2,1,0:T(8,128)S(1)}, f32[128,8,128]{2,1,0:T(8,128)S(1)}, u32[]{:S(2)}, u32[]{:S(2)}) collective-permute-start(f32[128,8,128]{2,1,0:T(8,128)S(1)} %get-tuple-element.36), channel_id=1, source_target_pairs={{0,1},{1,0},{2,3},{3,2},{4,5},{5,4},{6,7},{7,6},{8,9},{9,8},{10,11... | collective-permute-start | bytes 1572872 | tf_op jit(solution)/shard_map/ppermute | solution.py:637
  20.8 12.1 %collective-permute-start.4 = (f32[128,8,128]{2,1,0:T(8,128)S(1)}, f32[128,8,128]{2,1,0:T(8,128)S(1)}, u32[]{:S(2)}, u32[]{:S(2)}) collective-permute-start(f32[128,8,128]{2,1,0:T(8,128)S(1)} %get-tuple-element.37), channel_id=1, source_target_pairs={{1,2},{2,1},{5,6},{6,5},{9,10},{10,9},{13,14},{14,13},{17,18},{18,... | collective-permute-start | bytes 1572872 | tf_op jit(solution)/shard_map/ppermute | solution.py:637
  28.9 2.4 %collective-permute-start.8 = (f32[116,8,128]{2,1,0:T(8,128)S(1)}, f32[116,8,128]{2,1,0:T(8,128)S(1)}, u32[]{:S(2)}, u32[]{:S(2)}) collective-permute-start(f32[116,8,128]{2,1,0:T(8,128)S(1)} %get-tuple-element.42), channel_id=1, source_target_pairs={{0,4},{4,0},{8,12},{12,8},{1,5},{5,1},{9,13},{13,9},{2,6},{6,2},{1... | collective-permute-start | bytes 1425416 | tf_op jit(solution)/shard_map/ppermute | solution.py:625
  29.1 33.8 %collective-permute-start.15 = (f32[116,8,128]{2,1,0:T(8,128)S(1)}, f32[116,8,128]{2,1,0:T(8,128)S(1)}, u32[]{:S(2)}, u32[]{:S(2)}) collective-permute-start(f32[116,8,128]{2,1,0:T(8,128)S(1)} %get-tuple-element.42), channel_id=1, source_target_pairs={{0,1},{1,0},{2,3},{3,2},{4,5},{5,4},{6,7},{7,6},{8,9},{9,8},{10,11... | collective-permute-start | bytes 1425416 | tf_op jit(solution)/shard_map/ppermute | solution.py:637
  30.6 32.3 %collective-permute-start.16 = (f32[116,8,128]{2,1,0:T(8,128)S(1)}, f32[116,8,128]{2,1,0:T(8,128)S(1)}, u32[]{:S(2)}, u32[]{:S(2)}) collective-permute-start(f32[116,8,128]{2,1,0:T(8,128)S(1)} %get-tuple-element.52), channel_id=1, source_target_pairs={{1,2},{2,1},{5,6},{6,5},{9,10},{10,9},{13,14},{14,13},{17,18},{18,... | collective-permute-start | bytes 1425416 | tf_op jit(solution)/shard_map/ppermute | solution.py:637
  45.3 2.8 %collective-permute-start.10 = (f32[8,128]{1,0:T(8,128)S(1)}, f32[8,128]{1,0:T(8,128)S(1)}, u32[]{:S(2)}, u32[]{:S(2)}) collective-permute-start(f32[8,128]{1,0:T(8,128)S(1)} %get-tuple-element.43), channel_id=1, source_target_pairs={{0,8},{4,12},{8,0},{12,4},{1,9},{5,13},{9,1},{13,5},{2,10},{6,14},... | collective-permute-start | bytes 12296 | tf_op jit(solution)/shard_map/ppermute | solution.py:625
  46.9 3.0 %collective-permute-start.11 = (f32[8,128]{1,0:T(8,128)S(1)}, f32[8,128]{1,0:T(8,128)S(1)}, u32[]{:S(2)}, u32[]{:S(2)}) collective-permute-start(f32[8,128]{1,0:T(8,128)S(1)} %get-tuple-element.43), channel_id=1, source_target_pairs={{0,12},{4,8},{8,4},{12,0},{1,13},{5,9},{9,5},{13,1},{2,14},{6,10},... | collective-permute-start | bytes 12296 | tf_op jit(solution)/shard_map/ppermute | solution.py:625
  48.2 1.8 %collective-permute-start.9 = (f32[8,128]{1,0:T(8,128)S(1)}, f32[8,128]{1,0:T(8,128)S(1)}, u32[]{:S(2)}, u32[]{:S(2)}) collective-permute-start(f32[8,128]{1,0:T(8,128)S(1)} %get-tuple-element.43), channel_id=1, source_target_pairs={{0,4},{4,0},{8,12},{12,8},{1,5},{5,1},{9,13},{13,9},{2,6},{6,2},{1... | collective-permute-start | bytes 12296 | tf_op jit(solution)/shard_map/ppermute | solution.py:625
  50.0 6.8 %collective-permute-start.17 = (f32[8,128]{1,0:T(8,128)S(1)}, f32[8,128]{1,0:T(8,128)S(1)}, u32[]{:S(2)}, u32[]{:S(2)}) collective-permute-start(f32[8,128]{1,0:T(8,128)S(1)} %add_add_fusion.1), channel_id=1, source_target_pairs={{0,1},{1,0},{2,3},{3,2},{4,5},{5,4},{6,7},{7,6},{8,9},{9,8},{10,11... | collective-permute-start | bytes 12296 | tf_op jit(solution)/shard_map/ppermute | solution.py:625
  54.3 4.3 %collective-permute-start.18 = (f32[8,128]{1,0:T(8,128)S(1)}, f32[8,128]{1,0:T(8,128)S(1)}, u32[]{:S(2)}, u32[]{:S(2)}) collective-permute-start(f32[8,128]{1,0:T(8,128)S(1)} %add_add_fusion.1), channel_id=1, source_target_pairs={{0,2},{1,3},{2,0},{3,1},{4,6},{5,7},{6,4},{7,5},{8,10},{9,11},{10,... | collective-permute-start | bytes 12296 | tf_op jit(solution)/shard_map/ppermute | solution.py:625
  55.7 4.3 %collective-permute-start.19 = (f32[8,128]{1,0:T(8,128)S(1)}, f32[8,128]{1,0:T(8,128)S(1)}, u32[]{:S(2)}, u32[]{:S(2)}) collective-permute-start(f32[8,128]{1,0:T(8,128)S(1)} %add_add_fusion.1), channel_id=1, source_target_pairs={{0,3},{1,2},{2,1},{3,0},{4,7},{5,6},{6,5},{7,4},{8,11},{9,10},{10,... | collective-permute-start | bytes 12296 | tf_op jit(solution)/shard_map/ppermute | solution.py:625
  56.8 20.9 %collective-permute-start.12 = (f32[48,8,128]{2,1,0:T(8,128)S(1)}, f32[48,8,128]{2,1,0:T(8,128)S(1)}, u32[]{:S(2)}, u32[]{:S(2)}) collective-permute-start(f32[48,8,128]{2,1,0:T(8,128)S(1)} %get-tuple-element.49), channel_id=1, source_target_pairs={{0,4},{4,0},{8,12},{12,8},{1,5},{5,1},{9,13},{13,9},{2,6},{6,2},{1... | collective-permute-start | bytes 589832 | tf_op jit(solution)/shard_map/ppermute | solution.py:625
  58.6 20.7 %collective-permute-start.13 = (f32[48,8,128]{2,1,0:T(8,128)S(1)}, f32[48,8,128]{2,1,0:T(8,128)S(1)}, u32[]{:S(2)}, u32[]{:S(2)}) collective-permute-start(f32[48,8,128]{2,1,0:T(8,128)S(1)} %get-tuple-element.50), channel_id=1, source_target_pairs={{0,8},{4,12},{8,0},{12,4},{1,9},{5,13},{9,1},{13,5},{2,10},{6,14},... | collective-permute-start | bytes 589832 | tf_op jit(solution)/shard_map/ppermute | solution.py:625
  59.9 19.4 %collective-permute-start.14 = (f32[48,8,128]{2,1,0:T(8,128)S(1)}, f32[48,8,128]{2,1,0:T(8,128)S(1)}, u32[]{:S(2)}, u32[]{:S(2)}) collective-permute-start(f32[48,8,128]{2,1,0:T(8,128)S(1)} %get-tuple-element.51), channel_id=1, source_target_pairs={{0,12},{4,8},{8,4},{12,0},{1,13},{5,9},{9,5},{13,1},{2,14},{6,10},... | collective-permute-start | bytes 589832 | tf_op jit(solution)/shard_map/ppermute | solution.py:625
  76.4 3.9 %collective-permute-start.20 = (f32[48,8,128]{2,1,0:T(8,128)S(1)}, f32[48,8,128]{2,1,0:T(8,128)S(1)}, u32[]{:S(2)}, u32[]{:S(2)}) collective-permute-start(f32[48,8,128]{2,1,0:T(8,128)S(1)} %get-tuple-element.58), channel_id=1, source_target_pairs={{0,4},{4,0},{8,12},{12,8},{1,5},{5,1},{9,13},{13,9},{2,6},{6,2},{1... | collective-permute-start | bytes 589832 | tf_op jit(solution)/shard_map/ppermute | solution.py:625
  76.5 6.1 %collective-permute-start.21 = (f32[48,8,128]{2,1,0:T(8,128)S(1)}, f32[48,8,128]{2,1,0:T(8,128)S(1)}, u32[]{:S(2)}, u32[]{:S(2)}) collective-permute-start(f32[48,8,128]{2,1,0:T(8,128)S(1)} %get-tuple-element.59), channel_id=1, source_target_pairs={{0,8},{4,12},{8,0},{12,4},{1,9},{5,13},{9,1},{13,5},{2,10},{6,14},... | collective-permute-start | bytes 589832 | tf_op jit(solution)/shard_map/ppermute | solution.py:625
  77.7 9.7 %collective-permute-start.22 = (f32[48,8,128]{2,1,0:T(8,128)S(1)}, f32[48,8,128]{2,1,0:T(8,128)S(1)}, u32[]{:S(2)}, u32[]{:S(2)}) collective-permute-start(f32[48,8,128]{2,1,0:T(8,128)S(1)} %get-tuple-element.60), channel_id=1, source_target_pairs={{0,12},{4,8},{8,4},{12,0},{1,13},{5,9},{9,5},{13,1},{2,14},{6,10},... | collective-permute-start | bytes 589832 | tf_op jit(solution)/shard_map/ppermute | solution.py:625
  (4 other events, 15.3 us)

commit v5 on v4

--- a/solution.py
+++ b/solution.py
@@ -162,7 +162,7 @@
 HALO = 8
 ROWS = CZ + 2 * HALO
 PAD = 8
-GROUP = 2
+GROUP = 4
 WIDE = 2 * LANES
 PLANES = TILES * CX
 ENTRIES = 1024

time: 88.7 us -> 88.4 us (level)
  no operation moved by 1% of the time
where the time goes in v5:
time: 88.4 us; the launch traced here: 88.1 us
  Pallas kernels  32.7 us (37%)
  starting transfers between devices  26.9 us (30%)
  waiting for transfers between devices  26.5 us (30%)
  local copies, waits for them, and re-layouts  1.34 us (2%)
    pallas_call x8, Pallas kernels, call(): pl.pallas_call(kernel, out_shape=outs, in_specs=[pl.BlockSpec(memory_spac...  32.7 us
    ppermute x19, waiting for transfers between devices, swap(): return lax.ppermute(value, axis, [(i, i ^ distance) for i in range(count)])  24.8 us
    ppermute x19, starting transfers between devices, swap(): return lax.ppermute(value, axis, [(i, i ^ distance) for i in range(count)])  22.2 us
    ppermute x2, starting transfers between devices, swap_neighbours(): lax.ppermute(first, 'gz', pairs)  3.28 us
  transfers between devices with their start and end apart: 23, of which 9 were waited for; matrix products, arithmetic and copies ran while one was open for 1% of the time, Pallas kernels for 33%

profile of v5, /device:TPU:1, one launch (start us, length us, event | category | flops | bytes accessed | tf_op | source)
XLA Modules:
  0.0 88.1 jit_solution(9175230866814805521)
XLA Ops:
  0.6 2.5 %shard_map.130 = (f32[66,8,128]{2,1,0:T(8,128)}, f32[66,8,128]{2,1,0:T(8,128)}, f32[66,8,128]{2,1,0:T(8,128)}, f32[66,8,128]{2,1,0:T(8,128)}) custom-call(f32[6,4,16,512]{3,2,1,0:T(8,128)} %fields_hbm.2, s32[4,16,512]{2,1,0:T(8,128)} %ids_hbm.1, f32[4]{0:T(128)} %eps_hbm.1, s32[1,1,1024]{2,1,0:T(1,128)} %cells_hbm.2, s32[1,1,1024]{2,1,0:T(1,128)} %bins_hbm.2), custom_call_target="tpu_custom_call" | custom-call | tf_op jit(solution)/shard_map/pallas_call | solution.py:611
  3.2 2.7 %collective-permute-start.1 = (f32[66,8,128]{2,1,0:T(8,128)}, f32[66,8,128]{2,1,0:T(8,128)S(1)}, u32[]{:S(2)}, u32[]{:S(2)}) collective-permute-start(f32[66,8,128]{2,1,0:T(8,128)} %get-tuple-element.34), channel_id=1, source_target_pairs={{0,8},{4,12},{8,0},{12,4},{1,9},{5,13},{9,1},{13,5},{2,10},{6,14},... | collective-permute-start | bytes 811016 | tf_op jit(solution)/shard_map/ppermute | solution.py:625
  6.0 3.1 %shard_map.132 = (f32[56,8,128]{2,1,0:T(8,128)}, f32[56,8,128]{2,1,0:T(8,128)}, f32[56,8,128]{2,1,0:T(8,128)}, f32[56,8,128]{2,1,0:T(8,128)}, f32[1,128]{1,0:T(1,128)}, /*index=5*/f32[8,8]{1,0:T(8,128)}) custom-call(f32[6,4,16,512]{3,2,1,0:T(8,128)} %fields_hbm.3, s32[1,1,1024]{2,1,0:T(1,128)} %cells_hbm.3, s32[1,1,1024]{2,1,0:T(1,128)} %bins_hbm.3, ...), custom_call_target="tpu_custom_call" | custom-call | tf_op jit(solution)/shard_map/pallas_call | solution.py:611
  9.5 1.4 %collective-permute-start.6 = (f32[56,8,128]{2,1,0:T(8,128)}, f32[56,8,128]{2,1,0:T(8,128)S(1)}, u32[]{:S(2)}, u32[]{:S(2)}) collective-permute-start(f32[56,8,128]{2,1,0:T(8,128)} %get-tuple-element.40), channel_id=1, source_target_pairs={{0,8},{4,12},{8,0},{12,4},{1,9},{5,13},{9,1},{13,5},{2,10},{6,14},... | collective-permute-start | bytes 688136 | tf_op jit(solution)/shard_map/ppermute | solution.py:625
  11.3 1.6 %collective-permute-done.1.b2 = f32[66,8,128]{2,1,0:T(8,128)S(1)} collective-permute-done((f32[66,8,128]{2,1,0:T(8,128)}, f32[66,8,128]{2,1,0:T(8,128)S(1)}, u32[]{:S(2)}, u32[]{:S(2)}) %collective-permute-start.1) | collective-permute-done | bytes 270368 | tf_op jit(solution)/shard_map/ppermute | solution.py:625
  12.9 6.0 %collective-permute-done.2.b3 = f32[66,8,128]{2,1,0:T(8,128)S(1)} collective-permute-done((f32[66,8,128]{2,1,0:T(8,128)}, f32[66,8,128]{2,1,0:T(8,128)S(1)}, u32[]{:S(2)}, u32[]{:S(2)}) %collective-permute-start.2) | collective-permute-done | bytes 270368 | tf_op jit(solution)/shard_map/ppermute | solution.py:625
  19.0 1.8 %collective-permute-start.3 = (f32[128,8,128]{2,1,0:T(8,128)S(1)}, f32[128,8,128]{2,1,0:T(8,128)S(1)}, u32[]{:S(2)}, u32[]{:S(2)}) collective-permute-start(f32[128,8,128]{2,1,0:T(8,128)S(1)} %get-tuple-element.36), channel_id=1, source_target_pairs={{0,1},{1,0},{2,3},{3,2},{4,5},{5,4},{6,7},{7,6},{8,9},{9,8},{10,11... | collective-permute-start | bytes 1572872 | tf_op jit(solution)/shard_map/ppermute | solution.py:637
  21.5 2.1 %collective-permute-done.6.b2 = f32[56,8,128]{2,1,0:T(8,128)S(1)} collective-permute-done((f32[56,8,128]{2,1,0:T(8,128)}, f32[56,8,128]{2,1,0:T(8,128)S(1)}, u32[]{:S(2)}, u32[]{:S(2)}) %collective-permute-start.6) | collective-permute-done | bytes 229408 | tf_op jit(solution)/shard_map/ppermute | solution.py:625
  23.6 5.2 %collective-permute-done.7.b3 = f32[56,8,128]{2,1,0:T(8,128)S(1)} collective-permute-done((f32[56,8,128]{2,1,0:T(8,128)}, f32[56,8,128]{2,1,0:T(8,128)S(1)}, u32[]{:S(2)}, u32[]{:S(2)}) %collective-permute-start.7) | collective-permute-done | bytes 229408 | tf_op jit(solution)/shard_map/ppermute | solution.py:625
  29.1 1.5 %collective-permute-start.15 = (f32[116,8,128]{2,1,0:T(8,128)S(1)}, f32[116,8,128]{2,1,0:T(8,128)S(1)}, u32[]{:S(2)}, u32[]{:S(2)}) collective-permute-start(f32[116,8,128]{2,1,0:T(8,128)S(1)} %get-tuple-element.42), channel_id=1, source_target_pairs={{0,1},{1,0},{2,3},{3,2},{4,5},{5,4},{6,7},{7,6},{8,9},{9,8},{10,11... | collective-permute-start | bytes 1425416 | tf_op jit(solution)/shard_map/ppermute | solution.py:637
  31.3 1.7 %collective-permute-done.3.first_ref = f32[128,8,128]{2,1,0:T(8,128)S(1)} collective-permute-done((f32[128,8,128]{2,1,0:T(8,128)S(1)}, f32[128,8,128]{2,1,0:T(8,128)S(1)}, u32[]{:S(2)}, u32[]{:S(2)}) %collective-permute-start.3) | collective-permute-done | bytes 524320 | tf_op jit(solution)/shard_map/ppermute | solution.py:637
  32.9 12.3 %shard_map.134 = (f32[48,8,128]{2,1,0:T(8,128)S(1)}, f32[48,8,128]{2,1,0:T(8,128)S(1)}, f32[48,8,128]{2,1,0:T(8,128)S(1)}, f32[48,8,128]{2,1,0:T(8,128)S(1)}, f3...) custom-call(f32[66,8,128]{2,1,0:T(8,128)S(1)} %copy-done, f32[66,8,128]{2,1,0:T(8,128)S(1)} %collective-permute-done.b1, ...), custom_call_target="tpu_custom_call" | custom-call | tf_op jit(solution)/shard_map/pallas_call | solution.py:611
  45.2 1.6 %collective-permute-start.10 = (f32[8,128]{1,0:T(8,128)S(1)}, f32[8,128]{1,0:T(8,128)S(1)}, u32[]{:S(2)}, u32[]{:S(2)}) collective-permute-start(f32[8,128]{1,0:T(8,128)S(1)} %get-tuple-element.43), channel_id=1, source_target_pairs={{0,8},{4,12},{8,0},{12,4},{1,9},{5,13},{9,1},{13,5},{2,10},{6,14},... | collective-permute-start | bytes 12296 | tf_op jit(solution)/shard_map/ppermute | solution.py:625
  46.8 1.2 %collective-permute-start.11 = (f32[8,128]{1,0:T(8,128)S(1)}, f32[8,128]{1,0:T(8,128)S(1)}, u32[]{:S(2)}, u32[]{:S(2)}) collective-permute-start(f32[8,128]{1,0:T(8,128)S(1)} %get-tuple-element.43), channel_id=1, source_target_pairs={{0,12},{4,8},{8,4},{12,0},{1,13},{5,9},{9,5},{13,1},{2,14},{6,10},... | collective-permute-start | bytes 12296 | tf_op jit(solution)/shard_map/ppermute | solution.py:625
  48.0 1.8 %collective-permute-done.11 = f32[8,128]{1,0:T(8,128)S(1)} collective-permute-done((f32[8,128]{1,0:T(8,128)S(1)}, f32[8,128]{1,0:T(8,128)S(1)}, u32[]{:S(2)}, u32[]{:S(2)}) %collective-permute-start.11) | collective-permute-done | bytes 4128 | tf_op jit(solution)/shard_map/ppermute | solution.py:625
  49.8 4.4 %collective-permute-start.17 = (f32[8,128]{1,0:T(8,128)S(1)}, f32[8,128]{1,0:T(8,128)S(1)}, u32[]{:S(2)}, u32[]{:S(2)}) collective-permute-start(f32[8,128]{1,0:T(8,128)S(1)} %add_add_fusion.1), channel_id=1, source_target_pairs={{0,1},{1,0},{2,3},{3,2},{4,5},{5,4},{6,7},{7,6},{8,9},{9,8},{10,11... | collective-permute-start | bytes 12296 | tf_op jit(solution)/shard_map/ppermute | solution.py:625
  54.2 1.3 %collective-permute-start.18 = (f32[8,128]{1,0:T(8,128)S(1)}, f32[8,128]{1,0:T(8,128)S(1)}, u32[]{:S(2)}, u32[]{:S(2)}) collective-permute-start(f32[8,128]{1,0:T(8,128)S(1)} %add_add_fusion.1), channel_id=1, source_target_pairs={{0,2},{1,3},{2,0},{3,1},{4,6},{5,7},{6,4},{7,5},{8,10},{9,11},{10,... | collective-permute-start | bytes 12296 | tf_op jit(solution)/shard_map/ppermute | solution.py:625
  55.5 1.1 %collective-permute-start.19 = (f32[8,128]{1,0:T(8,128)S(1)}, f32[8,128]{1,0:T(8,128)S(1)}, u32[]{:S(2)}, u32[]{:S(2)}) collective-permute-start(f32[8,128]{1,0:T(8,128)S(1)} %add_add_fusion.1), channel_id=1, source_target_pairs={{0,3},{1,2},{2,1},{3,0},{4,7},{5,6},{6,5},{7,4},{8,11},{9,10},{10,... | collective-permute-start | bytes 12296 | tf_op jit(solution)/shard_map/ppermute | solution.py:625
  56.6 1.8 %collective-permute-start.12 = (f32[48,8,128]{2,1,0:T(8,128)S(1)}, f32[48,8,128]{2,1,0:T(8,128)S(1)}, u32[]{:S(2)}, u32[]{:S(2)}) collective-permute-start(f32[48,8,128]{2,1,0:T(8,128)S(1)} %get-tuple-element.49), channel_id=1, source_target_pairs={{0,4},{4,0},{8,12},{12,8},{1,5},{5,1},{9,13},{13,9},{2,6},{6,2},{1... | collective-permute-start | bytes 589832 | tf_op jit(solution)/shard_map/ppermute | solution.py:625
  59.8 2.9 %collective-permute-start.14 = (f32[48,8,128]{2,1,0:T(8,128)S(1)}, f32[48,8,128]{2,1,0:T(8,128)S(1)}, u32[]{:S(2)}, u32[]{:S(2)}) collective-permute-start(f32[48,8,128]{2,1,0:T(8,128)S(1)} %get-tuple-element.51), channel_id=1, source_target_pairs={{0,12},{4,8},{8,4},{12,0},{1,13},{5,9},{9,5},{13,1},{2,14},{6,10},... | collective-permute-start | bytes 589832 | tf_op jit(solution)/shard_map/ppermute | solution.py:625
  63.4 12.7 %shard_map.136 = (f32[48,8,128]{2,1,0:T(8,128)S(1)}, f32[48,8,128]{2,1,0:T(8,128)S(1)}, f32[48,8,128]{2,1,0:T(8,128)S(1)}, f32[48,8,128]{2,1,0:T(8,128)S(1)}) custom-call(f32[56,8,128]{2,1,0:T(8,128)S(1)} %copy-done.1, f32[56,8,128]{2,1,0:T(8,128)S(1)} %collective-permute-done.5.b1, f32[56,8,128]{2,1,0:T(8,128)S(1)} %collective-permute-done.6.b2, ...), custom_call_target="tpu_custom_call" | custom-call | tf_op jit(solution)/shard_map/pallas_call | solution.py:611
  76.2 1.2 %collective-permute-start.21 = (f32[48,8,128]{2,1,0:T(8,128)S(1)}, f32[48,8,128]{2,1,0:T(8,128)S(1)}, u32[]{:S(2)}, u32[]{:S(2)}) collective-permute-start(f32[48,8,128]{2,1,0:T(8,128)S(1)} %get-tuple-element.59), channel_id=1, source_target_pairs={{0,8},{4,12},{8,0},{12,4},{1,9},{5,13},{9,1},{13,5},{2,10},{6,14},... | collective-permute-start | bytes 589832 | tf_op jit(solution)/shard_map/ppermute | solution.py:625
  80.0 2.3 %collective-permute-done.21.b2 = f32[48,8,128]{2,1,0:T(8,128)S(1)} collective-permute-done((f32[48,8,128]{2,1,0:T(8,128)S(1)}, f32[48,8,128]{2,1,0:T(8,128)S(1)}, u32[]{:S(2)}, u32[]{:S(2)}) %collective-permute-start.21) | collective-permute-done | bytes 196640 | tf_op jit(solution)/shard_map/ppermute | solution.py:625
  82.3 4.8 %collective-permute-done.22.b3 = f32[48,8,128]{2,1,0:T(8,128)S(1)} collective-permute-done((f32[48,8,128]{2,1,0:T(8,128)S(1)}, f32[48,8,128]{2,1,0:T(8,128)S(1)}, u32[]{:S(2)}, u32[]{:S(2)}) %collective-permute-start.22) | collective-permute-done | bytes 196640 | tf_op jit(solution)/shard_map/ppermute | solution.py:625
  (43 shorter events, 8.3 us)
Async XLA Ops:
  3.1 7.8 %collective-permute-start = (f32[66,8,128]{2,1,0:T(8,128)}, f32[66,8,128]{2,1,0:T(8,128)S(1)}, u32[]{:S(2)}, u32[]{:S(2)}) collective-permute-start(f32[66,8,128]{2,1,0:T(8,128)} %get-tuple-element.33), channel_id=1, source_target_pairs={{0,4},{4,0},{8,12},{12,8},{1,5},{5,1},{9,13},{13,9},{2,6},{6,2},{1... | collective-permute-start | bytes 811016 | tf_op jit(solution)/shard_map/ppermute | solution.py:625
  3.2 9.7 %collective-permute-start.1 = (f32[66,8,128]{2,1,0:T(8,128)}, f32[66,8,128]{2,1,0:T(8,128)S(1)}, u32[]{:S(2)}, u32[]{:S(2)}) collective-permute-start(f32[66,8,128]{2,1,0:T(8,128)} %get-tuple-element.34), channel_id=1, source_target_pairs={{0,8},{4,12},{8,0},{12,4},{1,9},{5,13},{9,1},{13,5},{2,10},{6,14},... | collective-permute-start | bytes 811016 | tf_op jit(solution)/shard_map/ppermute | solution.py:625
  5.9 13.0 %collective-permute-start.2 = (f32[66,8,128]{2,1,0:T(8,128)}, f32[66,8,128]{2,1,0:T(8,128)S(1)}, u32[]{:S(2)}, u32[]{:S(2)}) collective-permute-start(f32[66,8,128]{2,1,0:T(8,128)} %get-tuple-element.35), channel_id=1, source_target_pairs={{0,12},{4,8},{8,4},{12,0},{1,13},{5,9},{9,5},{13,1},{2,14},{6,10},... | collective-permute-start | bytes 811016 | tf_op jit(solution)/shard_map/ppermute | solution.py:625
  6.0 13.0 %copy-start = (f32[66,8,128]{2,1,0:T(8,128)S(1)}, f32[66,8,128]{2,1,0:T(8,128)}, u32[]{:S(2)}) copy-start(f32[66,8,128]{2,1,0:T(8,128)} %get-tuple-element.32.b0) | copy-start | bytes 811012
  9.1 12.4 %collective-permute-start.5 = (f32[56,8,128]{2,1,0:T(8,128)}, f32[56,8,128]{2,1,0:T(8,128)S(1)}, u32[]{:S(2)}, u32[]{:S(2)}) collective-permute-start(f32[56,8,128]{2,1,0:T(8,128)} %get-tuple-element.39), channel_id=1, source_target_pairs={{0,4},{4,0},{8,12},{12,8},{1,5},{5,1},{9,13},{13,9},{2,6},{6,2},{1... | collective-permute-start | bytes 688136 | tf_op jit(solution)/shard_map/ppermute | solution.py:625
  9.5 14.1 %collective-permute-start.6 = (f32[56,8,128]{2,1,0:T(8,128)}, f32[56,8,128]{2,1,0:T(8,128)S(1)}, u32[]{:S(2)}, u32[]{:S(2)}) collective-permute-start(f32[56,8,128]{2,1,0:T(8,128)} %get-tuple-element.40), channel_id=1, source_target_pairs={{0,8},{4,12},{8,0},{12,4},{1,9},{5,13},{9,1},{13,5},{2,10},{6,14},... | collective-permute-start | bytes 688136 | tf_op jit(solution)/shard_map/ppermute | solution.py:625
  11.0 17.8 %collective-permute-start.7 = (f32[56,8,128]{2,1,0:T(8,128)}, f32[56,8,128]{2,1,0:T(8,128)S(1)}, u32[]{:S(2)}, u32[]{:S(2)}) collective-permute-start(f32[56,8,128]{2,1,0:T(8,128)} %get-tuple-element.41), channel_id=1, source_target_pairs={{0,12},{4,8},{8,4},{12,0},{1,13},{5,9},{9,5},{13,1},{2,14},{6,10},... | collective-permute-start | bytes 688136 | tf_op jit(solution)/shard_map/ppermute | solution.py:625
  19.0 13.9 %collective-permute-start.3 = (f32[128,8,128]{2,1,0:T(8,128)S(1)}, f32[128,8,128]{2,1,0:T(8,128)S(1)}, u32[]{:S(2)}, u32[]{:S(2)}) collective-permute-start(f32[128,8,128]{2,1,0:T(8,128)S(1)} %get-tuple-element.36), channel_id=1, source_target_pairs={{0,1},{1,0},{2,3},{3,2},{4,5},{5,4},{6,7},{7,6},{8,9},{9,8},{10,11... | collective-permute-start | bytes 1572872 | tf_op jit(solution)/shard_map/ppermute | solution.py:637
  20.8 12.1 %collective-permute-start.4 = (f32[128,8,128]{2,1,0:T(8,128)S(1)}, f32[128,8,128]{2,1,0:T(8,128)S(1)}, u32[]{:S(2)}, u32[]{:S(2)}) collective-permute-start(f32[128,8,128]{2,1,0:T(8,128)S(1)} %get-tuple-element.37), channel_id=1, source_target_pairs={{1,2},{2,1},{5,6},{6,5},{9,10},{10,9},{13,14},{14,13},{17,18},{18,... | collective-permute-start | bytes 1572872 | tf_op jit(solution)/shard_map/ppermute | solution.py:637
  28.9 2.4 %collective-permute-start.8 = (f32[116,8,128]{2,1,0:T(8,128)S(1)}, f32[116,8,128]{2,1,0:T(8,128)S(1)}, u32[]{:S(2)}, u32[]{:S(2)}) collective-permute-start(f32[116,8,128]{2,1,0:T(8,128)S(1)} %get-tuple-element.42), channel_id=1, source_target_pairs={{0,4},{4,0},{8,12},{12,8},{1,5},{5,1},{9,13},{13,9},{2,6},{6,2},{1... | collective-permute-start | bytes 1425416 | tf_op jit(solution)/shard_map/ppermute | solution.py:625
  29.1 33.7 %collective-permute-start.15 = (f32[116,8,128]{2,1,0:T(8,128)S(1)}, f32[116,8,128]{2,1,0:T(8,128)S(1)}, u32[]{:S(2)}, u32[]{:S(2)}) collective-permute-start(f32[116,8,128]{2,1,0:T(8,128)S(1)} %get-tuple-element.42), channel_id=1, source_target_pairs={{0,1},{1,0},{2,3},{3,2},{4,5},{5,4},{6,7},{7,6},{8,9},{9,8},{10,11... | collective-permute-start | bytes 1425416 | tf_op jit(solution)/shard_map/ppermute | solution.py:637
  30.6 32.2 %collective-permute-start.16 = (f32[116,8,128]{2,1,0:T(8,128)S(1)}, f32[116,8,128]{2,1,0:T(8,128)S(1)}, u32[]{:S(2)}, u32[]{:S(2)}) collective-permute-start(f32[116,8,128]{2,1,0:T(8,128)S(1)} %get-tuple-element.52), channel_id=1, source_target_pairs={{1,2},{2,1},{5,6},{6,5},{9,10},{10,9},{13,14},{14,13},{17,18},{18,... | collective-permute-start | bytes 1425416 | tf_op jit(solution)/shard_map/ppermute | solution.py:637
  45.2 2.8 %collective-permute-start.10 = (f32[8,128]{1,0:T(8,128)S(1)}, f32[8,128]{1,0:T(8,128)S(1)}, u32[]{:S(2)}, u32[]{:S(2)}) collective-permute-start(f32[8,128]{1,0:T(8,128)S(1)} %get-tuple-element.43), channel_id=1, source_target_pairs={{0,8},{4,12},{8,0},{12,4},{1,9},{5,13},{9,1},{13,5},{2,10},{6,14},... | collective-permute-start | bytes 12296 | tf_op jit(solution)/shard_map/ppermute | solution.py:625
  46.8 3.0 %collective-permute-start.11 = (f32[8,128]{1,0:T(8,128)S(1)}, f32[8,128]{1,0:T(8,128)S(1)}, u32[]{:S(2)}, u32[]{:S(2)}) collective-permute-start(f32[8,128]{1,0:T(8,128)S(1)} %get-tuple-element.43), channel_id=1, source_target_pairs={{0,12},{4,8},{8,4},{12,0},{1,13},{5,9},{9,5},{13,1},{2,14},{6,10},... | collective-permute-start | bytes 12296 | tf_op jit(solution)/shard_map/ppermute | solution.py:625
  48.0 1.8 %collective-permute-start.9 = (f32[8,128]{1,0:T(8,128)S(1)}, f32[8,128]{1,0:T(8,128)S(1)}, u32[]{:S(2)}, u32[]{:S(2)}) collective-permute-start(f32[8,128]{1,0:T(8,128)S(1)} %get-tuple-element.43), channel_id=1, source_target_pairs={{0,4},{4,0},{8,12},{12,8},{1,5},{5,1},{9,13},{13,9},{2,6},{6,2},{1... | collective-permute-start | bytes 12296 | tf_op jit(solution)/shard_map/ppermute | solution.py:625
  49.8 6.8 %collective-permute-start.17 = (f32[8,128]{1,0:T(8,128)S(1)}, f32[8,128]{1,0:T(8,128)S(1)}, u32[]{:S(2)}, u32[]{:S(2)}) collective-permute-start(f32[8,128]{1,0:T(8,128)S(1)} %add_add_fusion.1), channel_id=1, source_target_pairs={{0,1},{1,0},{2,3},{3,2},{4,5},{5,4},{6,7},{7,6},{8,9},{9,8},{10,11... | collective-permute-start | bytes 12296 | tf_op jit(solution)/shard_map/ppermute | solution.py:625
  54.2 4.3 %collective-permute-start.18 = (f32[8,128]{1,0:T(8,128)S(1)}, f32[8,128]{1,0:T(8,128)S(1)}, u32[]{:S(2)}, u32[]{:S(2)}) collective-permute-start(f32[8,128]{1,0:T(8,128)S(1)} %add_add_fusion.1), channel_id=1, source_target_pairs={{0,2},{1,3},{2,0},{3,1},{4,6},{5,7},{6,4},{7,5},{8,10},{9,11},{10,... | collective-permute-start | bytes 12296 | tf_op jit(solution)/shard_map/ppermute | solution.py:625
  55.5 4.3 %collective-permute-start.19 = (f32[8,128]{1,0:T(8,128)S(1)}, f32[8,128]{1,0:T(8,128)S(1)}, u32[]{:S(2)}, u32[]{:S(2)}) collective-permute-start(f32[8,128]{1,0:T(8,128)S(1)} %add_add_fusion.1), channel_id=1, source_target_pairs={{0,3},{1,2},{2,1},{3,0},{4,7},{5,6},{6,5},{7,4},{8,11},{9,10},{10,... | collective-permute-start | bytes 12296 | tf_op jit(solution)/shard_map/ppermute | solution.py:625
  56.6 20.8 %collective-permute-start.12 = (f32[48,8,128]{2,1,0:T(8,128)S(1)}, f32[48,8,128]{2,1,0:T(8,128)S(1)}, u32[]{:S(2)}, u32[]{:S(2)}) collective-permute-start(f32[48,8,128]{2,1,0:T(8,128)S(1)} %get-tuple-element.49), channel_id=1, source_target_pairs={{0,4},{4,0},{8,12},{12,8},{1,5},{5,1},{9,13},{13,9},{2,6},{6,2},{1... | collective-permute-start | bytes 589832 | tf_op jit(solution)/shard_map/ppermute | solution.py:625
  58.5 20.5 %collective-permute-start.13 = (f32[48,8,128]{2,1,0:T(8,128)S(1)}, f32[48,8,128]{2,1,0:T(8,128)S(1)}, u32[]{:S(2)}, u32[]{:S(2)}) collective-permute-start(f32[48,8,128]{2,1,0:T(8,128)S(1)} %get-tuple-element.50), channel_id=1, source_target_pairs={{0,8},{4,12},{8,0},{12,4},{1,9},{5,13},{9,1},{13,5},{2,10},{6,14},... | collective-permute-start | bytes 589832 | tf_op jit(solution)/shard_map/ppermute | solution.py:625
  59.8 19.2 %collective-permute-start.14 = (f32[48,8,128]{2,1,0:T(8,128)S(1)}, f32[48,8,128]{2,1,0:T(8,128)S(1)}, u32[]{:S(2)}, u32[]{:S(2)}) collective-permute-start(f32[48,8,128]{2,1,0:T(8,128)S(1)} %get-tuple-element.51), channel_id=1, source_target_pairs={{0,12},{4,8},{8,4},{12,0},{1,13},{5,9},{9,5},{13,1},{2,14},{6,10},... | collective-permute-start | bytes 589832 | tf_op jit(solution)/shard_map/ppermute | solution.py:625
  76.2 3.9 %collective-permute-start.20 = (f32[48,8,128]{2,1,0:T(8,128)S(1)}, f32[48,8,128]{2,1,0:T(8,128)S(1)}, u32[]{:S(2)}, u32[]{:S(2)}) collective-permute-start(f32[48,8,128]{2,1,0:T(8,128)S(1)} %get-tuple-element.58), channel_id=1, source_target_pairs={{0,4},{4,0},{8,12},{12,8},{1,5},{5,1},{9,13},{13,9},{2,6},{6,2},{1... | collective-permute-start | bytes 589832 | tf_op jit(solution)/shard_map/ppermute | solution.py:625
  76.2 6.1 %collective-permute-start.21 = (f32[48,8,128]{2,1,0:T(8,128)S(1)}, f32[48,8,128]{2,1,0:T(8,128)S(1)}, u32[]{:S(2)}, u32[]{:S(2)}) collective-permute-start(f32[48,8,128]{2,1,0:T(8,128)S(1)} %get-tuple-element.59), channel_id=1, source_target_pairs={{0,8},{4,12},{8,0},{12,4},{1,9},{5,13},{9,1},{13,5},{2,10},{6,14},... | collective-permute-start | bytes 589832 | tf_op jit(solution)/shard_map/ppermute | solution.py:625
  77.4 9.7 %collective-permute-start.22 = (f32[48,8,128]{2,1,0:T(8,128)S(1)}, f32[48,8,128]{2,1,0:T(8,128)S(1)}, u32[]{:S(2)}, u32[]{:S(2)}) collective-permute-start(f32[48,8,128]{2,1,0:T(8,128)S(1)} %get-tuple-element.60), channel_id=1, source_target_pairs={{0,12},{4,8},{8,4},{12,0},{1,13},{5,9},{9,5},{13,1},{2,14},{6,10},... | collective-permute-start | bytes 589832 | tf_op jit(solution)/shard_map/ppermute | solution.py:625
  (4 other events, 15.3 us)
